TPU v7x, 512 devices: a whole 4x8x8 slice. The times are simulated.
512 devices in a mesh: gz: 16 (over y, x_hi), gy: 32 (over z, x_lo, core).
Axes of the slice: x: 4 (x_hi: 2, x_lo: 2; x = x_hi * 2 + x_lo), y: 8, z: 8, core: 2. Of those that a mesh axis runs over, the one named last changes fastest.
Arguments:
- field_b: float32 [3, 2, 2048, 2048], P(None, None, 'gy', 'gz'), may hold values from -6 to 6
- density: float32 [2, 2048, 2048], P(None, 'gy', 'gz'), may hold values from 0.5 to 2
- level_y: int32 [2048], P('gy'), may hold values from 0 to 7
- level_z: int32 [2048], P('gz'), may hold values from 0 to 7
- bins: int32 [1024, 2048], P(('gz', 'gy')), may hold values from 0 to 1023
Outputs:
- emf: bfloat16 [3, 2, 2048, 2048], P(None, None, 'gy', 'gz')
- mode_power: float32 [1024, 2048], P(('gz', 'gy'))
- spectrum: float32 [1024], replicated
All inputs are finite; a program needn't handle non-finite values.
Results may differ from a plain program's by a relative error of at most 0.0035.
Values may be sent and summed in bfloat16 or wider, within the bound.
No kernel may reach another device: no remote copies, remote signals or barrier semaphores. Data moves between devices by JAX's collectives and lax.ppermute only.
A program may use at most 64 MiB of HBM per device.

v0:
```python
import math

import jax
import jax.numpy as jnp
from jax import lax
from jax.sharding import PartitionSpec as P

NY = 2048
NZ = 2048
NB = 1024
KZ = 1024


def extended(cells, sides, width):
    for axis, dim in sides:
        count = lax.axis_size(axis)
        head = lax.slice_in_dim(cells, 0, width, axis=dim)
        tail = lax.slice_in_dim(cells, cells.shape[dim] - width, cells.shape[dim], axis=dim)
        cells = jnp.concatenate(
            [
                lax.ppermute(tail, axis, [(i, (i + 1) % count) for i in range(count)]),
                cells,
                lax.ppermute(head, axis, [((i + 1) % count, i) for i in range(count)]),
            ],
            axis=dim,
        )
    return cells


def metric(level):
    return 1.0 / (1.0 + 0.25 * level.astype(jnp.float32))


def twiddle(positions, modes, length):
    phase = positions[:, None] * modes[None, :] % length
    angle = phase.astype(jnp.float32) * (2.0 * math.pi / length)
    factor = 1.0 / math.sqrt(length)
    return (
        (jnp.cos(angle) * factor).astype(jnp.bfloat16),
        (jnp.sin(angle) * factor).astype(jnp.bfloat16),
    )


def on_device(field_b, density, level_y, level_z, bins):
    planes = field_b.shape[1]
    y_local = field_b.shape[2]
    metric_y = metric(level_y)[None, None, :, None]
    metric_z = metric(level_z)[None, None, None, :]
    padded = extended(field_b, (("gz", 3), ("gy", 2)), 1)
    grad_y = 0.5 * (padded[:, :, 2:, 1:-1] - padded[:, :, :-2, 1:-1]) * metric_y
    grad_z = 0.5 * (padded[:, :, 1:-1, 2:] - padded[:, :, 1:-1, :-2]) * metric_z
    x_padded = jnp.pad(field_b, ((0, 0), (1, 1), (0, 0), (0, 0)))
    grad_x = 0.5 * (x_padded[:, 2:] - x_padded[:, :-2])
    cur_x = grad_y[2] - grad_z[1]
    cur_y = grad_z[0] - grad_x[2]
    cur_z = grad_x[1] - grad_y[0]
    e_x = (cur_y * field_b[2] - cur_z * field_b[1]) / density
    e_y = (cur_z * field_b[0] - cur_x * field_b[2]) / density
    e_z = (cur_x * field_b[1] - cur_y * field_b[0]) / density
    emf = jnp.stack([e_x, e_y, e_z]).astype(jnp.bfloat16)
    kz_dev = KZ // lax.axis_size("gz")
    z_pos = jnp.arange(NZ, dtype=jnp.int32)
    k_start = lax.axis_index("gz") * kz_dev
    z_cos, z_sin = twiddle(z_pos, k_start + jnp.arange(kz_dev, dtype=jnp.int32), NZ)
    table_z = jnp.concatenate([z_cos, -z_sin], axis=1)
    summed = jnp.einsum(
        "cxyz,zk->kcxy",
        lax.all_gather(emf, "gz", axis=3, tiled=True),
        table_z,
        preferred_element_type=jnp.float32,
    )
    z_modes = summed.reshape(2, kz_dev, 3, planes, y_local).astype(jnp.bfloat16)
    spread = lax.all_to_all(z_modes, "gy", split_axis=1, concat_axis=4, tiled=True)
    k_few = spread.shape[1]
    count = k_few * 3 * planes
    lhs_rows = spread.reshape(2 * count, NY)
    y_block = min(512, NY)
    y_pos = jnp.arange(NY, dtype=jnp.int32)

    def power_block(block_id):
        y_cos, y_sin = twiddle(y_pos, block_id * y_block + jnp.arange(y_block, dtype=jnp.int32), NY)
        product = jnp.dot(
            lhs_rows, jnp.concatenate([y_cos, y_sin], axis=1), preferred_element_type=jnp.float32
        )
        re_cos = product[:count, :y_block]
        re_sin = product[:count, y_block:]
        im_cos = product[count:, :y_block]
        im_sin = product[count:, y_block:]
        real_part = re_cos + im_sin
        imag_part = im_cos - re_sin
        power = (real_part * real_part + imag_part * imag_part).reshape(k_few, 3 * planes, y_block)
        return jnp.sum(power, axis=1) / (3 * planes)

    blocks = lax.map(power_block, jnp.arange(NY // y_block, dtype=jnp.int32))
    mode_power = blocks.transpose(1, 0, 2).reshape(k_few, NY)
    local_bins = jax.ops.segment_sum(mode_power.reshape(-1), bins.reshape(-1), num_segments=NB) * (
        NB / (KZ * NY)
    )
    spectrum = lax.psum(local_bins, ("gz", "gy"))
    return (emf, mode_power, spectrum)


def solution(mesh):
    placed = (
        P(None, None, "gy", "gz"),
        P(None, "gy", "gz"),
        P("gy"),
        P("gz"),
        P(("gz", "gy"), None),
    )
    return jax.shard_map(
        on_device,
        mesh=mesh,
        in_specs=placed,
        out_specs=(P(None, None, "gy", "gz"), P(("gz", "gy"), None), P()),
        check_vma=False,
    )
```

profile of v0, /device:TPU:1, one launch (start us, length us, event | category | flops | bytes accessed | tf_op | source)
XLA Modules:
  0.0 355.4 jit_solution(7134544797630249698)
XLA Ops:
  7.2 0.0 copy-start
  7.2 0.0 copy-start.1
  7.2 0.0 all-gather.2.cloned.1.call-start
  7.2 1.2 fusion.43
  8.4 8.4 %collective-permute-start = (f32[3,2,64,1]{3,2,1,0:T(8,128)S(1)}, f32[3,2,64,1]{3,2,1,0:T(8,128)S(1)}, u32[]{:S(2)}, u32[]{:S(2)}) collective-permute-start(f32[3,2,64,1]{3,2,1,0:T(8,128)S(1)} %get-tuple-element.98), channel_id=1, source_target_pairs={{32,0},{64,32},{96,64},{128,96},{160,128},{192,160},{224,192},{256... | collective-permute-start | bytes 4616 | tf_op jit(solution)/shard_map/ppermute | solution.py:23
  16.8 1.9 collective-permute-start.1
  18.7 0.7 divide_multiply_fusion
  19.4 1.0 collective-permute-done
  20.4 7.4 %collective-permute-done.1 = f32[3,2,64,1]{3,2,1,0:T(8,128)S(1)} collective-permute-done((f32[3,2,64,1]{3,2,1,0:T(8,128)S(1)}, f32[3,2,64,1]{3,2,1,0:T(8,128)S(1)}, u32[]{:S(2)}, u32[]{:S(2)}) %collective-permute-start.1) | collective-permute-done | bytes 1568 | tf_op jit(solution)/shard_map/ppermute | solution.py:21
  27.8 0.9 pad_maximum_fusion.11
  28.6 3.8 %collective-permute-start.2 = (f32[3,2,1,130]{3,2,1,0:T(1,128)S(1)}, f32[3,2,1,130]{3,2,1,0:T(1,128)S(1)}, u32[]{:S(2)}, u32[]{:S(2)}) collective-permute-start(f32[3,2,1,130]{3,2,1,0:T(1,128)S(1)} %get-tuple-element.95), channel_id=1, source_target_pairs={{1,0},{2,1},{3,2},{4,3},{5,4},{6,5},{7,6},{8,7},{9,8},{10,9},{11,1... | collective-permute-start | bytes 9368 | tf_op jit(solution)/shard_map/ppermute | solution.py:23
  32.4 2.1 collective-permute-start.3
  34.6 0.7 divide_multiply_fusion.1
  35.2 0.0 collective-permute-done.2
  35.2 7.1 %collective-permute-done.3 = f32[3,2,1,130]{3,2,1,0:T(1,128)S(1)} collective-permute-done((f32[3,2,1,130]{3,2,1,0:T(1,128)S(1)}, f32[3,2,1,130]{3,2,1,0:T(1,128)S(1)}, u32[]{:S(2)}, u32[]{:S(2)}) %collective-permute-start.3) | collective-permute-done | bytes 3152 | tf_op jit(solution)/shard_map/ppermute | solution.py:21
  42.3 1.7 fusion.31
  44.0 0.0 copy-done
  44.0 0.0 copy-done.1
  44.0 0.1 fusion.37
  44.1 0.7 pad_maximum_fusion.8
  44.8 0.0 copy-start.2
  44.8 0.0 all-gather.2.cloned.1.call-update
  44.8 2.1 fusion.27
  46.9 2.1 multiply_convert_fusion.3
  49.1 75.1 %all-gather.2.cloned.1.call-done = bf16[3,2,64,2048]{3,2,1,0:T(8,128)(2,1)} async-done(((bf16[3,2,64,128]{3,2,1,0:T(8,128)(2,1)}), bf16[3,2,64,2048]{3,2,1,0:T(8,128)(2,1)}) %all-gather.2.cloned.1.call-update) | async-done | bytes 1572880 | tf_op jit(solution)/shard_map/all_gather | solution.py:68
  124.2 2.0 convolution_convert_fusion
  126.1 0.1 convert_element_type.48
  126.3 0.2 copy.23
  126.4 0.8 reshape.73
  127.2 11.8 %all-to-all-start = ((bf16[32,2,768]{2,1,0:T(2,128)(2,1)}), bf16[32,2,768]{2,1,0:T(2,128)(2,1)S(1)}, u32[]{:S(2)}, u32[]{:S(2)}) async-start(bf16[32,2,768]{2,1,0:T(2,128)(2,1)} %reshape.73), calls=%async_computation | async-start | bytes 196608 | tf_op jit(solution)/shard_map/all_to_all | solution.py:73
  139.0 0.0 copy-done.2
  139.0 8.7 %all-to-all-done = bf16[32,2,768]{2,1,0:T(2,128)(2,1)S(1)} async-done(((bf16[32,2,768]{2,1,0:T(2,128)(2,1)}), bf16[32,2,768]{2,1,0:T(2,128)(2,1)S(1)}, u32[]{:S(2)}, u32[]{:S(2)}) %all-to-all-start) | async-done | bytes 98336 | tf_op jit(solution)/shard_map/all_to_all | solution.py:73
  147.8 0.2 reshape.74
  148.0 0.2 reshape.58
  148.3 76.5 %while.13 = (s32[]{:T(128)}, f32[4,2,512]{2,1,0:T(2,128)S(1)}, s32[4]{0:T(128)S(1)}, bf16[24,2048]{1,0:T(8,128)(2,1)S(1)}, s32[]{:T(128)}, /*index=5*/s32[1]{0:T(128)}, f32[]{:T(128)}) while((s32[]{:T(128)}, f32[4,2,512]{2,1,0:T(2,128)S(1)}, s32[4]{0:T(128)S(1)}, bf16[24,2048]{1,0:T(8,128)(2,1)S(1)}, s32[]{:T(128)}, ...), condition=%wide.region_2.3_spmd.clone, body=%wide.region_0.2_spmd.clone.sunk | while | flops 127963648 | bytes 8798321 | solution.py:94
  148.3 0.6 dynamic_slice.9
  149.5 17.1 %multiply_convert_fusion.5 = (bf16[2048,512]{1,0:T(8,128)(2,1)S(1)}, bf16[2048,512]{1,0:T(8,128)(2,1)S(1)}) fusion(s32[512]{0:T(512)S(1)} %iota_add_fusion.3), kind=kLoop, calls=%fused_computation.16.clone.1 | loop fusion | flops 18874368 | bytes 4196352 | tf_op jit(solution)/shard_map/while/body/eval_jaxpr/convert_element_type | solution.py:39
  166.6 0.6 fusion.52
  167.4 0.6 dynamic_slice.9
  168.6 17.1 %multiply_convert_fusion.5 = (bf16[2048,512]{1,0:T(8,128)(2,1)S(1)}, bf16[2048,512]{1,0:T(8,128)(2,1)S(1)}) fusion(s32[512]{0:T(512)S(1)} %iota_add_fusion.3), kind=kLoop, calls=%fused_computation.16.clone.1 | loop fusion | flops 18874368 | bytes 4196352 | tf_op jit(solution)/shard_map/while/body/eval_jaxpr/convert_element_type | solution.py:39
  185.8 0.6 fusion.52
  186.5 0.6 dynamic_slice.9
  187.8 17.1 %multiply_convert_fusion.5 = (bf16[2048,512]{1,0:T(8,128)(2,1)S(1)}, bf16[2048,512]{1,0:T(8,128)(2,1)S(1)}) fusion(s32[512]{0:T(512)S(1)} %iota_add_fusion.3), kind=kLoop, calls=%fused_computation.16.clone.1 | loop fusion | flops 18874368 | bytes 4196352 | tf_op jit(solution)/shard_map/while/body/eval_jaxpr/convert_element_type | solution.py:39
  204.9 0.6 fusion.52
  205.6 0.6 dynamic_slice.9
  206.9 17.1 %multiply_convert_fusion.5 = (bf16[2048,512]{1,0:T(8,128)(2,1)S(1)}, bf16[2048,512]{1,0:T(8,128)(2,1)S(1)}) fusion(s32[512]{0:T(512)S(1)} %iota_add_fusion.3), kind=kLoop, calls=%fused_computation.16.clone.1 | loop fusion | flops 18874368 | bytes 4196352 | tf_op jit(solution)/shard_map/while/body/eval_jaxpr/convert_element_type | solution.py:39
  224.0 0.6 fusion.52
  224.8 0.0 copy-start.3
  224.8 28.8 %scatter_custom_fusion = f32[1024]{0:T(1024)S(1)} fusion(s32[4096]{0:T(1024)S(1)} %bitcast.67, f32[4096]{0:T(1024)S(1)} %bitcast.70, f32[]{:T(128)} %constant.93.clone.1), kind=kCustom, calls=%fused_computation.77 | custom fusion | flops 4096 | bytes 4100 | tf_op jit(solution)/shard_map/scatter-add | solution.py:96
  253.6 95.0 %psum.7 = f32[1024]{0:T(1024)} all-reduce(f32[1024]{0:T(1024)S(1)} %broadcast_multiply_fusion), channel_id=1, replica_groups=mesh['gz'=16,'gy'=32] {'gz','gy'}, use_global_device_ids=true, to_apply=%region_4.5 | all-reduce | flops 1024 | bytes 8192 | tf_op jit(solution)/shard_map/psum | solution.py:99
  348.6 0.0 copy-done.3
  (29 shorter events, 0.4 us)
Async XLA Ops:
  7.2 36.9 %copy-start = (f32[3,2,64,128]{3,2,1,0:T(8,128)S(1)}, f32[3,2,64,128]{3,2,1,0:T(8,128)}, u32[]{:S(2)}) copy-start(f32[3,2,64,128]{3,2,1,0:T(8,128)} %param.7) | copy-start | bytes 589828
  7.2 36.9 %copy-start.1 = (f32[2,64,128]{2,1,0:T(8,128)S(1)}, f32[2,64,128]{2,1,0:T(8,128)}, u32[]{:S(2)}) copy-start(f32[2,64,128]{2,1,0:T(8,128)} %param.8) | copy-start | bytes 196612
  7.2 117.0 %all-gather.2.cloned.1.call-start = ((), (), s32[]{:S(2)}) async-start(), calls=%async_computation.1 | async-start | bytes 1671168 | tf_op jit(solution)/shard_map/all_gather | solution.py:68
  8.4 11.9 %collective-permute-start = (f32[3,2,64,1]{3,2,1,0:T(8,128)S(1)}, f32[3,2,64,1]{3,2,1,0:T(8,128)S(1)}, u32[]{:S(2)}, u32[]{:S(2)}) collective-permute-start(f32[3,2,64,1]{3,2,1,0:T(8,128)S(1)} %get-tuple-element.98), channel_id=1, source_target_pairs={{32,0},{64,32},{96,64},{128,96},{160,128},{192,160},{224,192},{256... | collective-permute-start | bytes 4616 | tf_op jit(solution)/shard_map/ppermute | solution.py:23
  16.8 11.0 %collective-permute-start.1 = (f32[3,2,64,1]{3,2,1,0:T(8,128)S(1)}, f32[3,2,64,1]{3,2,1,0:T(8,128)S(1)}, u32[]{:S(2)}, u32[]{:S(2)}) collective-permute-start(f32[3,2,64,1]{3,2,1,0:T(8,128)S(1)} %get-tuple-element.99), channel_id=1, source_target_pairs={{0,32},{32,64},{64,96},{96,128},{128,160},{160,192},{192,224},{224... | collective-permute-start | bytes 4616 | tf_op jit(solution)/shard_map/ppermute | solution.py:21
  28.6 6.6 %collective-permute-start.2 = (f32[3,2,1,130]{3,2,1,0:T(1,128)S(1)}, f32[3,2,1,130]{3,2,1,0:T(1,128)S(1)}, u32[]{:S(2)}, u32[]{:S(2)}) collective-permute-start(f32[3,2,1,130]{3,2,1,0:T(1,128)S(1)} %get-tuple-element.95), channel_id=1, source_target_pairs={{1,0},{2,1},{3,2},{4,3},{5,4},{6,5},{7,6},{8,7},{9,8},{10,9},{11,1... | collective-permute-start | bytes 9368 | tf_op jit(solution)/shard_map/ppermute | solution.py:23
  32.4 9.9 %collective-permute-start.3 = (f32[3,2,1,130]{3,2,1,0:T(1,128)S(1)}, f32[3,2,1,130]{3,2,1,0:T(1,128)S(1)}, u32[]{:S(2)}, u32[]{:S(2)}) collective-permute-start(f32[3,2,1,130]{3,2,1,0:T(1,128)S(1)} %get-tuple-element.96), channel_id=1, source_target_pairs={{0,1},{1,2},{2,3},{3,4},{4,5},{5,6},{6,7},{7,8},{8,9},{9,10},{10,1... | collective-permute-start | bytes 9368 | tf_op jit(solution)/shard_map/ppermute | solution.py:21
  44.8 94.3 %copy-start.2 = (s32[2,2048]{1,0:T(2,128)S(1)}, s32[2,2048]{1,0:T(2,128)}, u32[]{:S(2)}) copy-start(s32[2,2048]{1,0:T(2,128)} %param.11) | copy-start | bytes 49156
  127.2 20.5 %all-to-all-start = ((bf16[32,2,768]{2,1,0:T(2,128)(2,1)}), bf16[32,2,768]{2,1,0:T(2,128)(2,1)S(1)}, u32[]{:S(2)}, u32[]{:S(2)}) async-start(bf16[32,2,768]{2,1,0:T(2,128)(2,1)} %reshape.73), calls=%async_computation | async-start | bytes 196608 | tf_op jit(solution)/shard_map/all_to_all | solution.py:73
  224.8 123.8 %copy-start.3 = (f32[4,2,512]{2,1,0:T(2,128)}, f32[4,2,512]{2,1,0:T(2,128)S(1)}, u32[]{:S(2)}) copy-start(f32[4,2,512]{2,1,0:T(2,128)S(1)} %get-tuple-element.69) | copy-start | bytes 49156
Sparse Core Ops, SparseCore 0:
  44.9 79.1 all-gather.1
where the time goes:
time: 356 us; the launch traced here: 355 us
  other arithmetic  106 us (30%)
  waiting for transfers between devices  99.3 us (28%)
  blocking collectives  95 us (27%)
  starting transfers between devices  28 us (8%)
  between operations  14.3 us (4%)
  local copies, waits for them, and re-layouts  5.11 us (1%)
  matrix products  4.56 us (1%)
    psum x1, blocking collectives, on_device(): spectrum = lax.psum(local_bins, ('gz', 'gy'))  95 us
    all_gather x1, waiting for transfers between devices, on_device(): lax.all_gather(emf, 'gz', axis=3, tiled=True)  75.1 us
    convert_element_type x5, other arithmetic, twiddle(): (jnp.cos(angle) * factor).astype(jnp.bfloat16)  70.6 us
    scatter-add x1, other arithmetic, on_device(): jax.ops.segment_sum(mode_power.reshape(-1), bins.reshape(-1), num_segment...  28.8 us
    ppermute x2, waiting for transfers between devices, extended(): lax.ppermute(tail, axis, [(i, (i + 1) % count) for i in range(count)])  14.5 us
    ppermute x2, starting transfers between devices, extended(): lax.ppermute(head, axis, [((i + 1) % count, i) for i in range(count)])  12.2 us
    all_to_all x1, starting transfers between devices, on_device(): lax.all_to_all(z_modes, 'gy', split_axis=1, concat_axis=4, tiled=True)  11.8 us
    all_to_all x1, waiting for transfers between devices, on_device(): lax.all_to_all(z_modes, 'gy', split_axis=1, concat_axis=4, tiled=True)  8.73 us
  transfers between devices with their start and end apart: 6, of which 5 were waited for; matrix products, arithmetic and copies ran while one was open for 2% of the time, Pallas kernels for 0%

commit v1 on v0

v1 whole, which is shorter than its diff:
```python
import math

import jax
import jax.numpy as jnp
import numpy as np
from jax import lax
from jax.experimental import pallas as pl
from jax.experimental.pallas import tpu as pltpu
from jax.sharding import PartitionSpec as P

NY = 2048
NZ = 2048
NB = 1024
KZ = 1024
BF = jnp.bfloat16
F32 = jnp.float32


def angle(a, b, length):
    return 2.0 * math.pi * ((a[:, None] * b[None, :]) % length) / length


def pieces(table):
    high = table.astype(jnp.bfloat16)
    low = (table - high.astype(np.float64)).astype(jnp.bfloat16)
    return high, low


def z_tables():
    inner = angle(np.arange(64), np.arange(128), 128)
    high, low = pieces(np.concatenate([np.cos(inner), np.sin(inner)], axis=1))
    turn = angle(np.arange(16), np.arange(128), 2048)
    return np.concatenate([high, low], axis=0), np.stack([np.cos(turn), np.sin(turn)]).astype(np.float32)


def y_tables():
    rows = (8 * np.arange(32)[None, :] + np.arange(8)[:, None]).reshape(-1)
    inner = angle(rows, np.arange(256), 256)
    high, low = pieces(np.concatenate([np.cos(inner), np.sin(inner)], axis=1))
    turn = angle(np.arange(8), np.arange(256), 2048)
    order = np.zeros((128, 128), np.float32)
    for c in range(2):
        for e in range(2):
            for comp in range(4):
                for y0 in range(8):
                    order[c * 64 + y0 * 8 + e * 4 + comp, c * 64 + e * 32 + comp * 8 + y0] = 1.0
    return high, low, np.stack([np.cos(turn), np.sin(turn)]).astype(np.float32), order.astype(jnp.bfloat16)


def emf_kernel(fb, den, my_ref, mz_ref, ylo_ref, yhi_ref, zlo_ref, zhi_ref, emf_ref, msg_ref):
    rows, lanes = fb.shape[2], fb.shape[3]
    row = lax.broadcasted_iota(jnp.int32, (rows, lanes), 0)
    lane = lax.broadcasted_iota(jnp.int32, (rows, lanes), 1)
    my = my_ref[...]
    mz = mz_ref[...]
    zlo = jnp.transpose(zlo_ref[...])
    zhi = jnp.transpose(zhi_ref[...])

    def d_y(f, at):
        up = jnp.where(row == rows - 1, yhi_ref[at : at + 1, :], pltpu.roll(f, rows - 1, 0))
        down = jnp.where(row == 0, ylo_ref[at : at + 1, :], pltpu.roll(f, 1, 0))
        return (up - down) * my

    def d_z(f, at):
        up = jnp.where(lane == lanes - 1, zhi[:, at : at + 1], pltpu.roll(f, lanes - 1, 1))
        down = jnp.where(lane == 0, zlo[:, at : at + 1], pltpu.roll(f, 1, 1))
        return (up - down) * mz

    for p in range(2):
        b_x, b_y, b_z = fb[0, p], fb[1, p], fb[2, p]
        half = 0.5 if p == 0 else -0.5
        cur_x = d_y(b_z, 2 + p) - d_z(b_y, 2 + p)
        cur_y = d_z(b_x, p) - half * fb[2, 1 - p]
        cur_z = half * fb[1, 1 - p] - d_y(b_x, p)
        dens = den[p]
        parts = (
            (cur_y * b_z - cur_z * b_y) / dens,
            (cur_z * b_x - cur_x * b_z) / dens,
            (cur_x * b_y - cur_y * b_x) / dens,
        )
        for comp in range(3):
            value = parts[comp].astype(BF)
            emf_ref[comp, p] = value
            for block in range(8):
                msg_ref[2 * block + p, comp] = parts[comp][8 * block : 8 * block + 8].astype(BF)


def fourier16(x):
    plus = [x[i] + x[i + 8] for i in range(8)]
    minus = [x[i] - x[i + 8] for i in range(8)]
    out = {}
    a = [plus[i] + plus[i + 4] for i in range(4)]
    b = [plus[i] - plus[i + 4] for i in range(4)]
    r = math.sqrt(0.5)
    out[0] = ((a[0] + a[2]) + (a[1] + a[3]), None)
    out[8] = ((a[0] + a[2]) - (a[1] + a[3]), None)
    out[4] = (a[0] - a[2], a[3] - a[1])
    s1, s3 = (b[1] - b[3]) * r, (b[1] + b[3]) * r
    out[2] = (b[0] + s1, -(b[2] + s3))
    out[6] = (b[0] - s1, b[2] - s3)
    even = [minus[i] - minus[8 - i] for i in (1, 2, 3)]
    odd = [minus[i] + minus[8 - i] for i in (1, 2, 3)]
    for k in (1, 3, 5, 7):
        real = minus[0]
        imag = minus[4] * (-math.sin(math.pi * k / 2))
        for i in (1, 2, 3):
            real = real + even[i - 1] * math.cos(math.pi * i * k / 8)
            imag = imag - odd[i - 1] * math.sin(math.pi * i * k / 8)
        out[k] = (real, imag)
    return out


def z_kernel(x_ref, table_ref, turn_ref, out_ref, high_ref, low_ref):
    x = [x_ref[i].astype(F32) for i in range(16)]
    y = fourier16(x)
    zero = jnp.zeros((8, 128), BF)
    for k in range(16):
        cos = turn_ref[0, k : k + 1, :]
        sin = turn_ref[1, k : k + 1, :]
        real, imag = y[k] if k <= 8 else y[16 - k]
        if imag is None:
            t_re, t_im = real * cos, -(real * sin)
        else:
            if k > 8:
                imag = -imag
            t_re, t_im = real * cos + imag * sin, imag * cos - real * sin
        d0, e = k // 2, k % 2
        for value, spots in ((t_re, ((0, 0, 1), (1, 1, -1))), (t_im, ((0, 1, 1), (1, 0, 1)))):
            high = value.astype(BF)
            low = (value - high.astype(F32)).astype(BF)
            for c, side, sign in spots:
                at = d0 * 128 + c * 64 + e * 32
                for ref, piece in ((high_ref, high), (low_ref, low)):
                    ref[at : at + 24, side * 128 : side * 128 + 128] = piece if sign > 0 else -piece
                    ref[at + 24 : at + 32, side * 128 : side * 128 + 128] = zero
    contract = (((1,), (1,)), ((), ()))
    both = lax.dot_general(table_ref[...], high_ref[...], contract, preferred_element_type=F32)
    rest = lax.dot_general(table_ref[0:64, :], low_ref[...], contract, preferred_element_type=F32)
    out = both[0:64] + (both[64:128] + rest)
    for d0 in range(8):
        out_ref[pl.ds(d0, 64, stride=8), :] = out[:, d0 * 128 : d0 * 128 + 128]


def fourier8(re, im):
    def add(a, b):
        return (a[0] + b[0], a[1] + b[1])

    def sub(a, b):
        return (a[0] - b[0], a[1] - b[1])

    def turn(a):
        return (a[1], -a[0])

    def four(x):
        s, d = add(x[0], x[2]), sub(x[0], x[2])
        t, u = add(x[1], x[3]), turn(sub(x[1], x[3]))
        return [add(s, t), add(d, u), sub(s, t), sub(d, u)]

    x = list(zip(re, im))
    r = math.sqrt(0.5)
    even = four([add(x[i], x[i + 4]) for i in range(4)])
    low = [sub(x[i], x[i + 4]) for i in range(4)]
    low[1] = ((low[1][0] + low[1][1]) * r, (low[1][1] - low[1][0]) * r)
    low[2] = turn(low[2])
    low[3] = ((low[3][1] - low[3][0]) * r, -(low[3][0] + low[3][1]) * r)
    odd = four(low)
    return [even[k // 2] if k % 2 == 0 else odd[k // 2] for k in range(8)]


def y_kernel(x_ref, high_ref, low_ref, turn_ref, order_ref, bins_ref, power_ref, sums_ref):
    total = [None] * 8
    for p in range(2):
        held = jnp.concatenate([x_ref[64 * b + 32 * p : 64 * b + 32 * p + 32, :] for b in range(8)], axis=0)
        lhs = lax.dot_general(
            order_ref[...], held.astype(BF), (((1,), (1,)), ((), ())), preferred_element_type=F32
        ).astype(BF)
        product = jnp.dot(lhs, high_ref[...], preferred_element_type=F32) + jnp.dot(
            lhs, low_ref[...], preferred_element_type=F32
        )
        real = product[0:64, 0:256] + product[64:128, 256:512]
        imag = product[64:128, 0:256] - product[0:64, 256:512]
        re, im = [], []
        for y0 in range(8):
            a, b = real[8 * y0 : 8 * y0 + 8], imag[8 * y0 : 8 * y0 + 8]
            if y0 > 0:
                cos, sin = turn_ref[0, y0 : y0 + 1, :], turn_ref[1, y0 : y0 + 1, :]
                a, b = a * cos + b * sin, b * cos - a * sin
            re.append(a)
            im.append(b)
        for q1, (a, b) in enumerate(fourier8(re, im)):
            power = a * a + b * b
            total[q1] = power if p == 0 else total[q1] + power
    scale = 1.0 / (6.0 * 2048.0 * 2048.0)
    for q1 in range(8):
        for e in range(2):
            power_ref[e : e + 1, 256 * q1 : 256 * q1 + 256] = (
                jnp.sum(total[q1][4 * e : 4 * e + 4], axis=0, keepdims=True) * scale
            )
    sums = jnp.zeros((8, 128), F32)
    for e in range(2):
        value = power_ref[e : e + 1, :]
        bins = bins_ref[e : e + 1, :]
        coarse = lax.broadcasted_iota(jnp.int32, (8, 2048), 0) == (bins >> 7)
        fine = (lax.broadcasted_iota(jnp.int32, (128, 2048), 0) == (bins & 127)).astype(F32).astype(BF)
        spread = jnp.where(coarse, value, 0.0)
        first = spread.astype(BF)
        spread = spread - first.astype(F32)
        second = spread.astype(BF)
        third = (spread - second.astype(F32)).astype(BF)
        for piece in (third, second, first):
            sums += lax.dot_general(piece, fine, (((1,), (1,)), ((), ())), preferred_element_type=F32)
    sums_ref[...] = sums * (NB / (KZ * NY))


def metric(level):
    return 1.0 / (1.0 + 0.25 * level.astype(F32))


def everywhere(block, axis):
    count = lax.axis_size(axis)
    copies = jnp.broadcast_to(block[None], (count,) + block.shape)
    return jnp.sum(lax.all_to_all(copies, axis, 0, 0, tiled=True), axis=0)


def on_device(field_b, density, level_y, level_z, bins):
    y_local, z_local = field_b.shape[2], field_b.shape[3]

    def shift(cells, axis, step):
        count = lax.axis_size(axis)
        return lax.ppermute(cells, axis, [(i, (i + step) % count) for i in range(count)])

    zlo = shift(field_b[0:2, :, :, z_local - 1].reshape(4, y_local), "gz", 1)
    zhi = shift(field_b[0:2, :, :, 0].reshape(4, y_local), "gz", -1)
    ylo = shift(field_b[0::2, :, y_local - 1, :].reshape(4, z_local), "gy", 1)
    yhi = shift(field_b[0::2, :, 0, :].reshape(4, z_local), "gy", -1)
    my = jnp.broadcast_to(0.5 * metric(level_y)[:, None], (y_local, z_local))
    mz = (0.5 * metric(level_z))[None, :]
    emf, message = pl.pallas_call(
        emf_kernel,
        out_shape=(
            jax.ShapeDtypeStruct(field_b.shape, BF),
            jax.ShapeDtypeStruct((16, 3, 8, z_local), BF),
        ),
    )(field_b, density, my, mz, ylo, yhi, zlo, zhi)
    lines = lax.all_to_all(message, "gz", 0, 0, tiled=True).reshape(16, 24, z_local)
    z_table, z_turn = z_tables()
    z_modes = pl.pallas_call(
        z_kernel,
        out_shape=jax.ShapeDtypeStruct((512, 128), F32),
        scratch_shapes=[pltpu.VMEM((1024, 256), BF), pltpu.VMEM((1024, 256), BF)],
    )(lines, z_table, z_turn)
    spread = lax.all_to_all(z_modes.reshape(512, 1, 128), ("gz", "gy"), 0, 0, tiled=True).reshape(512, 128)
    y_high, y_low, y_turn, order = y_tables()
    mode_power, sums = pl.pallas_call(
        y_kernel,
        out_shape=(jax.ShapeDtypeStruct((2, NY), F32), jax.ShapeDtypeStruct((8, 128), F32)),
    )(spread, y_high, y_low, y_turn, order, bins)
    spectrum = everywhere(everywhere(sums, "gz"), "gy").reshape(NB)
    return (emf, mode_power, spectrum)


def solution(mesh):
    placed = (
        P(None, None, "gy", "gz"),
        P(None, "gy", "gz"),
        P("gy"),
        P("gz"),
        P(("gz", "gy"), None),
    )
    return jax.shard_map(
        on_device,
        mesh=mesh,
        in_specs=placed,
        out_specs=(P(None, None, "gy", "gz"), P(("gz", "gy"), None), P()),
        check_vma=False,
    )
```

time: 356 us -> 111 us (0.31)
  other arithmetic: 106 us -> 1.2 us
  waiting for transfers between devices: 99.3 us -> 0.18 us
  blocking collectives: 95 us -> 77.4 us
  between operations: 14.3 us -> 0.75 us
  starting transfers between devices: 28 us -> 20.2 us
  Pallas kernels: 0 us -> 7.71 us
  matrix products: 4.56 us -> 0 us
    psum x1 -> x0, blocking collectives: 95 us -> none  [on_device(): spectrum = lax.psum(local_bins, ('gz', 'gy'))]
    all_to_all x0 -> x4, blocking collectives: none -> 77.4 us  [the longest x1 35.5 us: on_device(): lax.all_to_all(z_modes.reshape(512, 1, 128), ('gz', 'gy'), 0, 0, tiled=True)]
    all_gather x1 -> x0, waiting for transfers between devices: 75.1 us -> none  [on_device(): lax.all_gather(emf, 'gz', axis=3, tiled=True)]
    convert_element_type x5 -> x0, other arithmetic: 70.6 us -> none  [twiddle(): (jnp.cos(angle) * factor).astype(jnp.bfloat16)]
    scatter-add x1 -> x0, other arithmetic: 28.8 us -> none  [on_device(): jax.ops.segment_sum(mode_power.reshape(-1), bins.reshape(-1), num_segment...]
    ppermute x4, waiting for transfers between devices: 15.5 us -> 0.18 us  [shift(): lax.ppermute(cells, axis, [(i, (i + step) % count) for i in range(count)])]
    all_to_all x1 -> x0, starting transfers between devices: 11.8 us -> none  [on_device(): lax.all_to_all(z_modes, 'gy', split_axis=1, concat_axis=4, tiled=True)]
    all_to_all x1 -> x0, waiting for transfers between devices: 8.73 us -> none  [on_device(): lax.all_to_all(z_modes, 'gy', split_axis=1, concat_axis=4, tiled=True)]
  transfers between devices with their start and end apart: 6 -> 4, of which waited for: 5 -> 1; matrix products, arithmetic and copies ran while one was open for 2% -> 1% of each run, Pallas kernels for 0% -> 0%
where the time goes in v1:
time: 111 us
  blocking collectives  77.4 us (70%)
  starting transfers between devices  20.2 us (18%)
  Pallas kernels  7.71 us (7%)
  local copies, waits for them, and re-layouts  3.35 us (3%)
  other arithmetic  1.2 us (1%)
    all_to_all x1, blocking collectives, on_device(): lax.all_to_all(z_modes.reshape(512, 1, 128), ('gz', 'gy'), 0, 0, tiled=True)  35.5 us
    all_to_all x2, blocking collectives, everywhere(): return jnp.sum(lax.all_to_all(copies, axis, 0, 0, tiled=True), axis=0)  27.3 us
    ppermute x4, starting transfers between devices, shift(): lax.ppermute(cells, axis, [(i, (i + step) % count) for i in range(count)])  20.2 us
    all_to_all x1, blocking collectives, on_device(): lax.all_to_all(message, 'gz', 0, 0, tiled=True).reshape(16, 24, z_local)  14.7 us
    pallas_call x1, Pallas kernels, on_device(): pl.pallas_call(y_kernel, out_shape=(jax.ShapeDtypeStruct((2, NY), F32), j...  3.54 us
  transfers between devices with their start and end apart: 4, of which 1 were waited for; matrix products, arithmetic and copies ran while one was open for 1% of the time, Pallas kernels for 0%

profile of v1, /device:TPU:1, one launch (start us, length us, event | category | flops | bytes accessed | tf_op | source)
XLA Modules:
  0.0 110.7 jit_solution(18313829108365030426)
XLA Ops:
  0.6 1.2 %slice_reduce_fusion = (f32[2,2,64]{2,1,0:T(2,128)S(1)}, f32[2,2,64]{2,1,0:T(2,128)S(1)}) fusion(f32[3,2,64,128]{3,2,1,0:T(8,128)} %fb.1), kind=kLoop, calls=%fused_computation | loop fusion | bytes 4096 | tf_op jit(solution)/shard_map/slice | solution.py:233
  1.8 5.5 %collective-permute-start.2 = (f32[4,64]{1,0:T(4,128)S(1)}, f32[4,64]{1,0:T(4,128)S(1)}, u32[]{:S(2)}, u32[]{:S(2)}) collective-permute-start(f32[4,64]{1,0:T(4,128)S(1)} %bitcast.17), channel_id=1, source_target_pairs={{0,32},{32,64},{64,96},{96,128},{128,160},{160,192},{192,224},{224... | collective-permute-start | bytes 3080 | tf_op jit(solution)/shard_map/ppermute | solution.py:230
  7.3 4.8 %collective-permute-start.3 = (f32[4,64]{1,0:T(4,128)S(1)}, f32[4,64]{1,0:T(4,128)S(1)}, u32[]{:S(2)}, u32[]{:S(2)}) collective-permute-start(f32[4,64]{1,0:T(4,128)S(1)} %bitcast.16), channel_id=1, source_target_pairs={{0,480},{32,0},{64,32},{96,64},{128,96},{160,128},{192,160},{224,1... | collective-permute-start | bytes 3080 | tf_op jit(solution)/shard_map/ppermute | solution.py:230
  12.1 0.8 fusion
  12.9 3.6 %collective-permute-start = (f32[4,128]{1,0:T(4,128)S(1)}, f32[4,128]{1,0:T(4,128)S(1)}, u32[]{:S(2)}, u32[]{:S(2)}) collective-permute-start(f32[4,128]{1,0:T(4,128)S(1)} %bitcast.19), channel_id=1, source_target_pairs={{0,1},{1,2},{2,3},{3,4},{4,5},{5,6},{6,7},{7,8},{8,9},{9,10},{10,1... | collective-permute-start | bytes 6152 | tf_op jit(solution)/shard_map/ppermute | solution.py:230
  16.5 0.0 copy-start.4
  16.6 0.0 copy-start.5
  16.6 6.2 %collective-permute-start.1 = (f32[4,128]{1,0:T(4,128)S(1)}, f32[4,128]{1,0:T(4,128)S(1)}, u32[]{:S(2)}, u32[]{:S(2)}) collective-permute-start(f32[4,128]{1,0:T(4,128)S(1)} %bitcast.18), channel_id=1, source_target_pairs={{0,31},{1,0},{2,1},{3,2},{4,3},{5,4},{6,5},{7,6},{8,7},{9,8},{10,9... | collective-permute-start | bytes 6152 | tf_op jit(solution)/shard_map/ppermute | solution.py:230
  22.8 0.0 copy-done.4
  22.8 0.0 copy-done.5
  22.8 0.5 multiply_bitcast_fusion.mz_ref
  23.4 0.0 collective-permute-done.2.zlo_ref
  23.4 0.0 copy-start
  23.4 0.0 collective-permute-done.3.zhi_ref
  23.4 0.0 copy-start.1
  23.4 0.0 collective-permute-done.ylo_ref
  23.4 0.0 copy-start.2
  23.4 0.2 collective-permute-done.1.yhi_ref
  23.6 0.0 copy-start.3
  23.6 0.7 broadcast_in_dim.8.my_ref
  24.3 0.0 copy-done
  24.3 0.0 copy-done.1
  24.3 0.0 copy-done.2
  24.3 0.0 copy-done.3
  24.3 2.0 %shard_map.130 = (bf16[3,2,64,128]{3,2,1,0:T(8,128)(2,1)}, bf16[16,3,8,128]{3,2,1,0:T(8,128)(2,1)}) custom-call(f32[3,2,64,128]{3,2,1,0:T(8,128)} %fb.1, f32[2,64,128]{2,1,0:T(8,128)} %den.1, f32[64,128]{1,0:T(8,128)} %broadcast_in_dim.8.my_ref, f32[1,128]{1,0:T(1,128)} %multiply_bitcast_fusion.mz_ref, f32[4,128]{1,0:T(4,128)} %copy-done.2, ...), custom_call_target="tpu_custom_call" | custom-call | tf_op jit(solution)/shard_map/pallas_call | solution.py:238
  26.2 14.7 %all_to_all.20 = bf16[16,3,8,128]{3,2,1,0:T(8,128)(2,1)} all-to-all(bf16[16,3,8,128]{3,2,1,0:T(8,128)(2,1)} %get-tuple-element.8), channel_id=1, replica_groups=mesh['gz'=16,'gy'=32] {'gz'}, dimensions={0} | all-to-all | bytes 196608 | tf_op jit(solution)/shard_map/all_to_all | solution.py:245
  40.9 2.2 %shard_map.131 = f32[512,128]{1,0:T(8,128)} custom-call(bf16[16,24,128]{2,1,0:T(8,128)(2,1)} %bitcast.14, bf16[128,256]{1,0:T(8,128)(2,1)} %constant.7.clone.table_ref, f32[2,16,128]{2,1,0:T(8,128)} %constant.8.clone.turn_ref), custom_call_target="tpu_custom_call" | custom-call | tf_op jit(solution)/shard_map/pallas_call | solution.py:247
  43.1 35.5 %all_to_all.21 = f32[512,1,128]{2,1,0:T(1,128)} all-to-all(f32[512,1,128]{2,1,0:T(1,128)} %bitcast.12), channel_id=1, replica_groups=mesh['gz'=16,'gy'=32] {'gz','gy'}, dimensions={0} | all-to-all | bytes 524288 | tf_op jit(solution)/shard_map/all_to_all | solution.py:252
  78.6 3.5 %shard_map.132 = (f32[2,2048]{1,0:T(2,128)}, f32[8,128]{1,0:T(8,128)}) custom-call(f32[512,128]{1,0:T(8,128)} %bitcast.13, bf16[256,512]{1,0:T(8,128)(2,1)} %constant.9.clone.high_ref, bf16[256,512]{1,0:T(8,128)(2,1)} %constant.26.clone.low_ref, f32[2,8,256]{2,1,0:T(8,128)} %constant.27.clone.turn_ref, bf16[128,128]{1,0:T(8,128)(2,1)} %constant.28.clone.order_ref, ...), custom_call_target="tpu_custom_call" | custom-call | tf_op jit(solution)/shard_map/pallas_call | solution.py:254
  82.1 0.7 broadcast_in_dim.10
  82.8 12.0 %all_to_all.22 = f32[16,8,128]{2,1,0:T(8,128)S(1)} all-to-all(f32[16,8,128]{2,1,0:T(8,128)S(1)} %broadcast_in_dim.10), channel_id=1, replica_groups=mesh['gz'=16,'gy'=32] {'gz'}, dimensions={0} | all-to-all | bytes 131072 | tf_op jit(solution)/shard_map/all_to_all | solution.py:222
  94.8 15.3 %all_to_all.23 = f32[32,8,128]{2,1,0:T(8,128)S(1)} all-to-all(f32[32,8,128]{2,1,0:T(8,128)S(1)} %broadcast_in_dim.11), channel_id=1, replica_groups=mesh['gz'=16,'gy'=32] {'gy'}, dimensions={0} | all-to-all | bytes 262144 | tf_op jit(solution)/shard_map/all_to_all | solution.py:222
  110.1 0.6 reduce_sum.19
  (3 shorter events, 0.0 us)
Async XLA Ops:
  1.8 21.5 %collective-permute-start.2 = (f32[4,64]{1,0:T(4,128)S(1)}, f32[4,64]{1,0:T(4,128)S(1)}, u32[]{:S(2)}, u32[]{:S(2)}) collective-permute-start(f32[4,64]{1,0:T(4,128)S(1)} %bitcast.17), channel_id=1, source_target_pairs={{0,32},{32,64},{64,96},{96,128},{128,160},{160,192},{192,224},{224... | collective-permute-start | bytes 3080 | tf_op jit(solution)/shard_map/ppermute | solution.py:230
  7.3 16.1 %collective-permute-start.3 = (f32[4,64]{1,0:T(4,128)S(1)}, f32[4,64]{1,0:T(4,128)S(1)}, u32[]{:S(2)}, u32[]{:S(2)}) collective-permute-start(f32[4,64]{1,0:T(4,128)S(1)} %bitcast.16), channel_id=1, source_target_pairs={{0,480},{32,0},{64,32},{96,64},{128,96},{160,128},{192,160},{224,1... | collective-permute-start | bytes 3080 | tf_op jit(solution)/shard_map/ppermute | solution.py:230
  12.9 10.5 %collective-permute-start = (f32[4,128]{1,0:T(4,128)S(1)}, f32[4,128]{1,0:T(4,128)S(1)}, u32[]{:S(2)}, u32[]{:S(2)}) collective-permute-start(f32[4,128]{1,0:T(4,128)S(1)} %bitcast.19), channel_id=1, source_target_pairs={{0,1},{1,2},{2,3},{3,4},{4,5},{5,6},{6,7},{7,8},{8,9},{9,10},{10,1... | collective-permute-start | bytes 6152 | tf_op jit(solution)/shard_map/ppermute | solution.py:230
  16.5 6.2 %copy-start.4 = (s32[64]{0:T(128)S(1)}, s32[64]{0:T(128)}, u32[]{:S(2)}) copy-start(s32[64]{0:T(128)} %param.13) | copy-start | bytes 772
  16.6 6.2 %copy-start.5 = (s32[128]{0:T(128)S(1)}, s32[128]{0:T(128)}, u32[]{:S(2)}) copy-start(s32[128]{0:T(128)} %param.14) | copy-start | bytes 1540
  16.6 7.0 %collective-permute-start.1 = (f32[4,128]{1,0:T(4,128)S(1)}, f32[4,128]{1,0:T(4,128)S(1)}, u32[]{:S(2)}, u32[]{:S(2)}) collective-permute-start(f32[4,128]{1,0:T(4,128)S(1)} %bitcast.18), channel_id=1, source_target_pairs={{0,31},{1,0},{2,1},{3,2},{4,3},{5,4},{6,5},{7,6},{8,7},{9,8},{10,9... | collective-permute-start | bytes 6152 | tf_op jit(solution)/shard_map/ppermute | solution.py:230
  23.4 0.9 copy-start
  23.4 0.9 copy-start.1
  23.4 0.9 copy-start.2
  23.6 0.7 copy-start.3

commit v2 on v0

v2 whole, which is shorter than its diff:
```python
import math

import jax
import jax.numpy as jnp
import numpy as np
from jax import lax
from jax.experimental import pallas as pl
from jax.experimental.pallas import tpu as pltpu
from jax.sharding import Mesh, PartitionSpec as P

NY = 2048
NZ = 2048
NB = 1024
KZ = 1024
BF = jnp.bfloat16
F32 = jnp.float32
GZ = ("yh", "yl", "xh")
GY = ("z", "xl", "c")
ACROSS = (((1,), (1,)), ((), ()))


def angle(a, b, length):
    return 2.0 * math.pi * ((a[:, None] * b[None, :]) % length) / length


def z_table():
    part, kappa, yh, jh = np.meshgrid(*(np.arange(n) for n in (4, 16, 4, 4)), indexing="ij")
    modes = (16 * (16 * yh + 4 * part + jh) + kappa).reshape(4, 1, 256, 1)
    turn = (modes * np.arange(128) % NZ + 128 * np.arange(8).reshape(1, 8, 1, 1)) % NZ
    return (np.cos(2.0 * math.pi * turn / NZ) / math.sqrt(NZ)).astype(jnp.bfloat16)


def y_tables():
    inner = angle((4 * np.arange(32)[None, :] + np.arange(4)[:, None]).reshape(-1), np.arange(128), 128)
    table = np.zeros((128, 2, 2, 2, 2, 128))
    for e in range(2):
        table[:, 0, e, e, 0] = np.cos(inner)
        table[:, 0, e, e, 1] = -np.sin(inner)
        table[:, 1, e, e, 0] = np.sin(inner)
        table[:, 1, e, e, 1] = np.cos(inner)
    turn = angle(np.arange(16), np.arange(128), NY)
    order = np.zeros((128, 128), np.float32)
    for cp in range(6):
        for y0 in range(16):
            order[y0 * 8 + cp, cp * 16 + y0] = 1.0
    return (
        table.reshape(512, 512).astype(jnp.bfloat16),
        np.stack([np.cos(turn), np.sin(turn)]).astype(np.float32),
        order.astype(jnp.bfloat16),
    )


def metric(level):
    return 1.0 / (1.0 + 0.25 * level.astype(F32))


def emf_kernel(
    fb_far, den_far, ly_far, lz_far, ylo_ref, yhi_ref, zlo_ref, zhi_ref, emf_ref, msg_ref, fb, den, ly_ref, lz_ref, sems
):
    far_near = ((ly_far, ly_ref), (lz_far, lz_ref), (fb_far, fb), (den_far, den))
    copies = [pltpu.make_async_copy(far, near, sems.at[n]) for n, (far, near) in enumerate(far_near)]
    for copy in copies:
        copy.start()
    copies[0].wait()
    copies[1].wait()
    rows, lanes = fb.shape[2], fb.shape[3]
    row = lax.broadcasted_iota(jnp.int32, (rows, lanes), 0)
    lane = lax.broadcasted_iota(jnp.int32, (rows, lanes), 1)
    half_y = jnp.broadcast_to(0.5 * metric(ly_ref[...]), (8, rows))
    upright = jnp.transpose(jnp.concatenate([zlo_ref[...], zhi_ref[...], half_y], axis=0))
    my = jnp.broadcast_to(upright[:, 8:9], (rows, lanes))
    mz = 0.5 * metric(lz_ref[...])

    def d_y(f, at):
        up = jnp.where(row == rows - 1, yhi_ref[at : at + 1, :], pltpu.roll(f, rows - 1, 0))
        down = jnp.where(row == 0, ylo_ref[at : at + 1, :], pltpu.roll(f, 1, 0))
        return (up - down) * my

    def d_z(f, at):
        up = jnp.where(lane == lanes - 1, upright[:, 4 + at : 5 + at], pltpu.roll(f, lanes - 1, 1))
        down = jnp.where(lane == 0, upright[:, at : at + 1], pltpu.roll(f, 1, 1))
        return (up - down) * mz

    copies[2].wait()
    copies[3].wait()
    for p in range(2):
        b_x, b_y, b_z = fb[0, p], fb[1, p], fb[2, p]
        half = 0.5 if p == 0 else -0.5
        cur_x = d_y(b_z, 2 + p) - d_z(b_y, 2 + p)
        cur_y = d_z(b_x, p) - half * fb[2, 1 - p]
        cur_z = half * fb[1, 1 - p] - d_y(b_x, p)
        dens = den[p]
        parts = (
            (cur_y * b_z - cur_z * b_y) / dens,
            (cur_z * b_x - cur_x * b_z) / dens,
            (cur_x * b_y - cur_y * b_x) / dens,
        )
        for comp in range(3):
            value = parts[comp].astype(BF)
            emf_ref[comp, p] = value
            at = 16 * (2 * comp + p)
            for block in range(4):
                for copy in range(4):
                    msg_ref[4 * block + copy, at : at + 16, :] = value[16 * block : 16 * block + 16]


def z_kernel(x_ref, table_ref, out_ref, mix_ref):
    zero = jnp.zeros((32, 512), BF)
    total = None
    for n in range(4):
        lines = jnp.concatenate([x_ref[4 * n + i] for i in range(4)], axis=1)
        lines = jnp.concatenate([lines, zero], axis=0)
        blocks = []
        for c in range(2):
            for kappa in range(16):
                turns = [(kappa * i + 4 * c) % 16 for i in range(4 * n, 4 * n + 4)]
                cells = [table_ref[m % 8, 16 * kappa : 16 * kappa + 16, :] for m in turns]
                blocks.append(jnp.concatenate([-x if m >= 8 else x for m, x in zip(turns, cells)], axis=1))
        product = lax.dot_general(jnp.concatenate(blocks, axis=0), lines, ACROSS, preferred_element_type=F32)
        total = product if n == 0 else total + product
    for c in range(2):
        for kappa in range(16):
            spot = 4 * (kappa // 2) + 2 * c + kappa % 2
            at = 16 * (16 * c + kappa)
            mix_ref[pl.ds(spot, 16, stride=32), :] = total[at : at + 16]
    out_ref[...] = mix_ref[...].astype(BF)


def add(a, b):
    return (a[0] + b[0], a[1] + b[1])


def sub(a, b):
    return (a[0] - b[0], a[1] - b[1])


def turned(a, eighths):
    eighths %= 16
    if eighths == 0:
        return a
    if eighths == 4:
        return (a[1], -a[0])
    if eighths == 2:
        r = math.sqrt(0.5)
        return ((a[0] + a[1]) * r, (a[1] - a[0]) * r)
    if eighths == 6:
        r = math.sqrt(0.5)
        return ((a[1] - a[0]) * r, -(a[0] + a[1]) * r)
    cos, sin = math.cos(math.pi * eighths / 8), math.sin(math.pi * eighths / 8)
    return (a[0] * cos + a[1] * sin, a[1] * cos - a[0] * sin)


def fourier4(x):
    s, d = add(x[0], x[2]), sub(x[0], x[2])
    t, u = add(x[1], x[3]), turned(sub(x[1], x[3]), 4)
    return [add(s, t), add(d, u), sub(s, t), sub(d, u)]


def fourier16(x):
    inner = [fourier4([x[4 * i + n] for i in range(4)]) for n in range(4)]
    out = [None] * 16
    for k in range(4):
        for b, value in enumerate(fourier4([turned(inner[n][k], n * k) for n in range(4)])):
            out[k + 4 * b] = value
    return out


def y_kernel(x_ref, table_ref, turn_ref, order_ref, bins_ref, power_ref, sums_ref):
    lhs = lax.dot_general(order_ref[...], x_ref[...], ACROSS, preferred_element_type=F32).astype(BF)
    product = jnp.dot(lhs, table_ref[...], preferred_element_type=F32)
    scale = 1.0 / (6.0 * NY)
    for e in range(2):
        held = []
        for y0 in range(16):
            a = product[8 * y0 : 8 * y0 + 8, 256 * e : 256 * e + 128]
            b = product[8 * y0 : 8 * y0 + 8, 256 * e + 128 : 256 * e + 256]
            if y0 > 0:
                cos, sin = turn_ref[0, y0 : y0 + 1, :], turn_ref[1, y0 : y0 + 1, :]
                a, b = a * cos + b * sin, b * cos - a * sin
            held.append((a, b))
        for q1, (a, b) in enumerate(fourier16(held)):
            power_ref[e : e + 1, 128 * q1 : 128 * q1 + 128] = (
                jnp.sum(a * a + b * b, axis=0, keepdims=True) * scale
            )
    sums = jnp.zeros((8, 128), F32)
    for e in range(2):
        value = power_ref[e : e + 1, :]
        bins = bins_ref[e : e + 1, :]
        coarse = lax.broadcasted_iota(jnp.int32, (8, NY), 0) == (bins >> 7)
        fine = (lax.broadcasted_iota(jnp.int32, (128, NY), 0) == (bins & 127)).astype(F32).astype(BF)
        spread = jnp.where(coarse, value, 0.0)
        first = spread.astype(BF)
        spread = spread - first.astype(F32)
        second = spread.astype(BF)
        third = (spread - second.astype(F32)).astype(BF)
        for piece in (third, second, first):
            sums += lax.dot_general(piece, fine, ACROSS, preferred_element_type=F32)
    sums = sums * (NB / (KZ * NY))
    for copy in range(sums_ref.shape[0]):
        sums_ref[copy] = sums


def on_device(field_b, density, level_y, level_z, bins):
    y_local, z_local = field_b.shape[2], field_b.shape[3]

    def shift(cells, axis, step):
        count = lax.axis_size(axis)
        return lax.ppermute(cells, axis, [(i, (i + step) % count) for i in range(count)])

    zlo = shift(field_b[0:2, :, :, z_local - 1].reshape(4, y_local), GZ, 1)
    zhi = shift(field_b[0:2, :, :, 0].reshape(4, y_local), GZ, -1)
    ylo = shift(field_b[0::2, :, y_local - 1, :].reshape(4, z_local), GY, 1)
    yhi = shift(field_b[0::2, :, 0, :].reshape(4, z_local), GY, -1)
    small = pltpu.CompilerParams(vmem_limit_bytes=16 * 2**20)
    far = [
        pltpu.with_memory_space_constraint(x, pltpu.HBM)
        for x in (field_b, density, level_y[None, :], level_z[None, :])
    ]
    emf, message = pl.pallas_call(
        emf_kernel,
        out_shape=(
            jax.ShapeDtypeStruct(field_b.shape, BF),
            jax.ShapeDtypeStruct((16, 96, z_local), BF),
        ),
        in_specs=[pl.BlockSpec(memory_space=pltpu.HBM)] * 4 + [pl.BlockSpec(memory_space=pltpu.VMEM)] * 4,
        scratch_shapes=[
            pltpu.VMEM(field_b.shape, F32),
            pltpu.VMEM(density.shape, F32),
            pltpu.VMEM((1, y_local), jnp.int32),
            pltpu.VMEM((1, z_local), jnp.int32),
            pltpu.SemaphoreType.DMA((4,)),
        ],
        compiler_params=small,
    )(*far, ylo, yhi, zlo, zhi)
    part = lax.axis_index("yl") * 2 + lax.axis_index("xh")
    quarter = lax.dynamic_index_in_dim(jnp.asarray(z_table()), part, keepdims=False)
    lines = lax.all_to_all(message, GZ, 0, 0, tiled=True)
    z_modes = pl.pallas_call(
        z_kernel,
        out_shape=jax.ShapeDtypeStruct((512, 128), BF),
        scratch_shapes=[pltpu.VMEM((512, 128), F32)],
        compiler_params=small,
    )(lines, quarter)
    spread = lax.all_to_all(z_modes.reshape(128, 4, 128), ("yh",) + GY, 0, 0, tiled=True).reshape(512, 128)
    first = ("yh", "yl", "c")
    second = ("xh", "z", "xl")
    mode_power, sums = pl.pallas_call(
        y_kernel,
        out_shape=(
            jax.ShapeDtypeStruct((2, NY), F32),
            jax.ShapeDtypeStruct((lax.axis_size(first), 8, 128), F32),
        ),
        compiler_params=small,
    )(spread, *y_tables(), bins)
    sums = jnp.sum(lax.all_to_all(sums, first, 0, 0, tiled=True), axis=0)
    copies = jnp.broadcast_to(sums[None], (lax.axis_size(second), 8, 128))
    spectrum = jnp.sum(lax.all_to_all(copies, second, 0, 0, tiled=True), axis=0).reshape(NB)
    return (emf, mode_power, spectrum)


def solution(mesh):
    fine = Mesh(mesh.devices.reshape(4, 2, 2, 8, 2, 2), GZ + GY)
    placed = (
        P(None, None, GY, GZ),
        P(None, GY, GZ),
        P(GY),
        P(GZ),
        P(GZ + GY, None),
    )
    return jax.shard_map(
        on_device,
        mesh=fine,
        in_specs=placed,
        out_specs=(P(None, None, GY, GZ), P(GZ + GY, None), P()),
        check_vma=False,
    )
```

time: 356 us -> 103 us (0.29)
  other arithmetic: 106 us -> 0.64 us
  waiting for transfers between devices: 99.3 us -> 11.9 us
  blocking collectives: 95 us -> 55.4 us
  between operations: 14.3 us -> 0.76 us
  matrix products: 4.56 us -> 0 us
  Pallas kernels: 0 us -> 4.27 us
    psum x1 -> x0, blocking collectives: 95 us -> none  [on_device(): spectrum = lax.psum(local_bins, ('gz', 'gy'))]
    all_gather x1 -> x0, waiting for transfers between devices: 75.1 us -> none  [on_device(): lax.all_gather(emf, 'gz', axis=3, tiled=True)]
    convert_element_type x5 -> x0, other arithmetic: 70.6 us -> none  [twiddle(): (jnp.cos(angle) * factor).astype(jnp.bfloat16)]
    all_to_all x0 -> x3, blocking collectives: none -> 55.4 us  [the longest x1 30.2 us: on_device(): lax.all_to_all(z_modes.reshape(128, 4, 128), ('yh',) + GY, 0, 0, tiled=True)]
    scatter-add x1 -> x0, other arithmetic: 28.8 us -> none  [on_device(): jax.ops.segment_sum(mode_power.reshape(-1), bins.reshape(-1), num_segment...]
    ppermute x4, waiting for transfers between devices: 15.5 us -> 0.71 us  [shift(): lax.ppermute(cells, axis, [(i, (i + step) % count) for i in range(count)])]
    all_to_all x1, starting transfers between devices: 11.8 us -> 6.71 us  [on_device(): lines = lax.all_to_all(message, GZ, 0, 0, tiled=True)]
    dot_general x5 -> x0, matrix products: 4.56 us -> none  [the longest x4 2.58 us: power_block(): jnp.dot(lhs_rows, jnp.concatenate([y_cos, y_sin], axis=1), preferred_elem...]
  transfers between devices with their start and end apart: 6 -> 5, of which waited for: 5 -> 2; matrix products, arithmetic and copies ran while one was open for 2% -> 2% of each run, Pallas kernels for 0% -> 0%
where the time goes in v2:
time: 103 us; the launch traced here: 102 us
  blocking collectives  55.4 us (54%)
  starting transfers between devices  26.3 us (26%)
  waiting for transfers between devices  11.9 us (12%)
  Pallas kernels  4.27 us (4%)
  local copies, waits for them, and re-layouts  3.1 us (3%)
    all_to_all x1, blocking collectives, on_device(): lax.all_to_all(z_modes.reshape(128, 4, 128), ('yh',) + GY, 0, 0, tiled=True)  30.2 us
    ppermute x4, starting transfers between devices, shift(): lax.ppermute(cells, axis, [(i, (i + step) % count) for i in range(count)])  19.6 us
    all_to_all x1, blocking collectives, on_device(): lax.all_to_all(copies, second, 0, 0, tiled=True)  13.5 us
    all_to_all x1, blocking collectives, on_device(): sums = jnp.sum(lax.all_to_all(sums, first, 0, 0, tiled=True), axis=0)  11.7 us
    all_to_all x1, waiting for transfers between devices, on_device(): lines = lax.all_to_all(message, GZ, 0, 0, tiled=True)  11.2 us
    all_to_all x1, starting transfers between devices, on_device(): lines = lax.all_to_all(message, GZ, 0, 0, tiled=True)  6.71 us
  transfers between devices with their start and end apart: 5, of which 2 were waited for; matrix products, arithmetic and copies ran while one was open for 2% of the time, Pallas kernels for 0%

profile of v2, /device:TPU:1, one launch (start us, length us, event | category | flops | bytes accessed | tf_op | source)
XLA Modules:
  0.0 102.4 jit_solution(1268226909652974108)
XLA Ops:
  0.6 0.0 copy-start.1
  0.6 0.0 copy-start.3
  0.7 0.0 copy-start
  0.7 0.0 copy-start.2
  0.7 0.8 fusion
  1.5 4.5 %collective-permute-start = (f32[4,128]{1,0:T(4,128)S(1)}, f32[4,128]{1,0:T(4,128)S(1)}, u32[]{:S(2)}, u32[]{:S(2)}) collective-permute-start(f32[4,128]{1,0:T(4,128)S(1)} %bitcast.17), channel_id=1, source_target_pairs={{0,1},{1,2},{2,3},{3,4},{4,5},{5,6},{6,7},{7,8},{8,9},{9,10},{10,1... | collective-permute-start | bytes 6152 | tf_op jit(solution)/shard_map/ppermute | solution.py:208
  6.0 6.2 %collective-permute-start.1 = (f32[4,128]{1,0:T(4,128)S(1)}, f32[4,128]{1,0:T(4,128)S(1)}, u32[]{:S(2)}, u32[]{:S(2)}) collective-permute-start(f32[4,128]{1,0:T(4,128)S(1)} %bitcast.16), channel_id=1, source_target_pairs={{0,31},{1,0},{2,1},{3,2},{4,3},{5,4},{6,5},{7,6},{8,7},{9,8},{10,9... | collective-permute-start | bytes 6152 | tf_op jit(solution)/shard_map/ppermute | solution.py:208
  12.2 1.2 %slice_reduce_fusion = (f32[2,2,64]{2,1,0:T(2,128)S(1)}, f32[2,2,64]{2,1,0:T(2,128)S(1)}) fusion(f32[3,2,64,128]{3,2,1,0:T(8,128)} %fb_far.1), kind=kLoop, calls=%fused_computation.1 | loop fusion | bytes 4096 | tf_op jit(solution)/shard_map/slice | solution.py:211
  13.4 1.9 %collective-permute-start.2 = (f32[4,64]{1,0:T(4,128)S(1)}, f32[4,64]{1,0:T(4,128)S(1)}, u32[]{:S(2)}, u32[]{:S(2)}) collective-permute-start(f32[4,64]{1,0:T(4,128)S(1)} %bitcast.15), channel_id=1, source_target_pairs={{0,32},{32,64},{64,96},{96,128},{128,160},{160,192},{192,224},{224... | collective-permute-start | bytes 3080 | tf_op jit(solution)/shard_map/ppermute | solution.py:208
  15.3 7.0 %collective-permute-start.3 = (f32[4,64]{1,0:T(4,128)S(1)}, f32[4,64]{1,0:T(4,128)S(1)}, u32[]{:S(2)}, u32[]{:S(2)}) collective-permute-start(f32[4,64]{1,0:T(4,128)S(1)} %bitcast.14), channel_id=1, source_target_pairs={{0,480},{32,0},{64,32},{96,64},{128,96},{160,128},{192,160},{224,1... | collective-permute-start | bytes 3080 | tf_op jit(solution)/shard_map/ppermute | solution.py:208
  22.3 0.0 collective-permute-done.2.zlo_ref
  22.3 0.7 collective-permute-done.3.zhi_ref
  23.0 0.0 collective-permute-done.ylo_ref
  23.0 0.0 collective-permute-done.1.yhi_ref
  23.0 2.0 %shard_map.112 = (bf16[3,2,64,128]{3,2,1,0:T(8,128)(2,1)}, bf16[16,96,128]{2,1,0:T(8,128)(2,1)}) custom-call(f32[3,2,64,128]{3,2,1,0:T(8,128)} %fb_far.1, f32[2,64,128]{2,1,0:T(8,128)} %den_far.1, s32[1,64]{1,0:T(1,128)} %bitcast.18, s32[1,128]{1,0:T(1,128)} %bitcast.19, f32[4,128]{1,0:T(4,128)S(1)} %collective-permute-done.ylo_ref, ...), custom_call_target="tpu_custom_call" | custom-call | tf_op jit(solution)/shard_map/pallas_call | solution.py:219
  25.0 6.7 %all-to-all-start = ((bf16[16,96,128]{2,1,0:T(8,128)(2,1)}), bf16[16,96,128]{2,1,0:T(8,128)(2,1)S(1)}, u32[]{:S(2)}, u32[]{:S(2)}) async-start(bf16[16,96,128]{2,1,0:T(8,128)(2,1)} %get-tuple-element.8), calls=%async_computation | async-start | bytes 786432 | tf_op jit(solution)/shard_map/all_to_all | solution.py:237
  31.8 1.1 %dynamic-slice_bitcast_fusion.table_ref = bf16[8,256,128]{2,1,0:T(8,128)(2,1)S(1)} fusion(bf16[4,8,256,128]{3,2,1,0:T(8,128)(2,1)} %constant.28.clone, s32[]{:T(128)S(6)} %select_n.4), kind=kLoop, calls=%fused_computation | loop fusion | bytes 1048580 | tf_op jit(solution)/shard_map/jit(dynamic_index_in_dim)/squeeze | solution.py:236
  32.8 11.2 %all-to-all-done.x_ref = bf16[16,96,128]{2,1,0:T(8,128)(2,1)S(1)} async-done(((bf16[16,96,128]{2,1,0:T(8,128)(2,1)}), bf16[16,96,128]{2,1,0:T(8,128)(2,1)S(1)}, u32[]{:S(2)}, u32[]{:S(2)}) %all-to-all-start) | async-done | bytes 393248 | tf_op jit(solution)/shard_map/all_to_all | solution.py:237
  44.0 0.8 shard_map.113
  44.9 30.2 %all_to_all.20 = bf16[128,4,128]{2,1,0:T(4,128)(2,1)S(1)} all-to-all(bf16[128,4,128]{2,1,0:T(4,128)(2,1)S(1)} %bitcast.12), channel_id=1, replica_groups=mesh['yh'=4,'yl'=2,'xh'=2,'z'=8,'xl'=2,'c'=2] {'yh','z','xl','c'}, dimensions={0} | all-to-all | bytes 262144 | tf_op jit(solution)/shard_map/all_to_all | solution.py:244
  75.1 0.0 copy-done.1
  75.1 0.0 copy-done.3
  75.1 0.0 copy-done
  75.1 0.0 copy-done.2
  75.1 1.4 %shard_map.114 = (f32[2,2048]{1,0:T(2,128)}, f32[16,8,128]{2,1,0:T(8,128)S(1)}) custom-call(bf16[512,128]{1,0:T(8,128)(2,1)S(1)} %bitcast.11, bf16[512,512]{1,0:T(8,128)(2,1)S(1)} %copy-done, f32[2,16,128]{2,1,0:T(8,128)S(1)} %copy-done.3, bf16[128,128]{1,0:T(8,128)(2,1)S(1)} %copy-done.1, s32[2,2048]{1,0:T(2,128)S(1)} %copy-done.2), custom_call_target="tpu_custom_call" | custom-call | tf_op jit(solution)/shard_map/pallas_call | solution.py:247
  76.5 11.7 %all_to_all.21 = f32[16,8,128]{2,1,0:T(8,128)S(1)} all-to-all(f32[16,8,128]{2,1,0:T(8,128)S(1)} %get-tuple-element.10), channel_id=1, replica_groups=mesh['yh'=4,'yl'=2,'xh'=2,'z'=8,'xl'=2,'c'=2] {'yh','yl','c'}, dimensions={0} | all-to-all | bytes 131072 | tf_op jit(solution)/shard_map/all_to_all | solution.py:255
  88.2 13.5 %all_to_all.22 = f32[32,8,128]{2,1,0:T(8,128)S(1)} all-to-all(f32[32,8,128]{2,1,0:T(8,128)S(1)} %broadcast_in_dim.14), channel_id=1, replica_groups=mesh['yh'=4,'yl'=2,'xh'=2,'z'=8,'xl'=2,'c'=2] {'xh','z','xl'}, dimensions={0} | all-to-all | bytes 262144 | tf_op jit(solution)/shard_map/all_to_all | solution.py:257
  101.7 0.6 reduce_sum.19
  (2 shorter events, 0.0 us)
Async XLA Ops:
  0.6 74.5 %copy-start.1 = (bf16[128,128]{1,0:T(8,128)(2,1)S(1)}, bf16[128,128]{1,0:T(8,128)(2,1)}, u32[]{:S(2)}) copy-start(bf16[128,128]{1,0:T(8,128)(2,1)} %constant.31.clone.order_ref) | copy-start | bytes 98308
  0.6 74.5 %copy-start.3 = (f32[2,16,128]{2,1,0:T(8,128)S(1)}, f32[2,16,128]{2,1,0:T(8,128)}, u32[]{:S(2)}) copy-start(f32[2,16,128]{2,1,0:T(8,128)} %constant.30.clone.turn_ref) | copy-start | bytes 49156
  0.7 74.5 %copy-start = (bf16[512,512]{1,0:T(8,128)(2,1)S(1)}, bf16[512,512]{1,0:T(8,128)(2,1)}, u32[]{:S(2)}) copy-start(bf16[512,512]{1,0:T(8,128)(2,1)} %constant.29.clone.table_ref) | copy-start | bytes 1572868
  0.7 74.4 %copy-start.2 = (s32[2,2048]{1,0:T(2,128)S(1)}, s32[2,2048]{1,0:T(2,128)}, u32[]{:S(2)}) copy-start(s32[2,2048]{1,0:T(2,128)} %bins_ref.1) | copy-start | bytes 49156
  1.5 21.5 %collective-permute-start = (f32[4,128]{1,0:T(4,128)S(1)}, f32[4,128]{1,0:T(4,128)S(1)}, u32[]{:S(2)}, u32[]{:S(2)}) collective-permute-start(f32[4,128]{1,0:T(4,128)S(1)} %bitcast.17), channel_id=1, source_target_pairs={{0,1},{1,2},{2,3},{3,4},{4,5},{5,6},{6,7},{7,8},{8,9},{9,10},{10,1... | collective-permute-start | bytes 6152 | tf_op jit(solution)/shard_map/ppermute | solution.py:208
  6.0 17.0 %collective-permute-start.1 = (f32[4,128]{1,0:T(4,128)S(1)}, f32[4,128]{1,0:T(4,128)S(1)}, u32[]{:S(2)}, u32[]{:S(2)}) collective-permute-start(f32[4,128]{1,0:T(4,128)S(1)} %bitcast.16), channel_id=1, source_target_pairs={{0,31},{1,0},{2,1},{3,2},{4,3},{5,4},{6,5},{7,6},{8,7},{9,8},{10,9... | collective-permute-start | bytes 6152 | tf_op jit(solution)/shard_map/ppermute | solution.py:208
  13.4 8.9 %collective-permute-start.2 = (f32[4,64]{1,0:T(4,128)S(1)}, f32[4,64]{1,0:T(4,128)S(1)}, u32[]{:S(2)}, u32[]{:S(2)}) collective-permute-start(f32[4,64]{1,0:T(4,128)S(1)} %bitcast.15), channel_id=1, source_target_pairs={{0,32},{32,64},{64,96},{96,128},{128,160},{160,192},{192,224},{224... | collective-permute-start | bytes 3080 | tf_op jit(solution)/shard_map/ppermute | solution.py:208
  15.3 7.7 %collective-permute-start.3 = (f32[4,64]{1,0:T(4,128)S(1)}, f32[4,64]{1,0:T(4,128)S(1)}, u32[]{:S(2)}, u32[]{:S(2)}) collective-permute-start(f32[4,64]{1,0:T(4,128)S(1)} %bitcast.14), channel_id=1, source_target_pairs={{0,480},{32,0},{64,32},{96,64},{128,96},{160,128},{192,160},{224,1... | collective-permute-start | bytes 3080 | tf_op jit(solution)/shard_map/ppermute | solution.py:208
  25.0 19.0 %all-to-all-start = ((bf16[16,96,128]{2,1,0:T(8,128)(2,1)}), bf16[16,96,128]{2,1,0:T(8,128)(2,1)S(1)}, u32[]{:S(2)}, u32[]{:S(2)}) async-start(bf16[16,96,128]{2,1,0:T(8,128)(2,1)} %get-tuple-element.8), calls=%async_computation | async-start | bytes 786432 | tf_op jit(solution)/shard_map/all_to_all | solution.py:237

commit v3 on v2

--- a/solution.py
+++ b/solution.py
@@ -54,62 +54,150 @@
     return 1.0 / (1.0 + 0.25 * level.astype(F32))
 
 
-def emf_kernel(
-    fb_far, den_far, ly_far, lz_far, ylo_ref, yhi_ref, zlo_ref, zhi_ref, emf_ref, msg_ref, fb, den, ly_ref, lz_ref, sems
-):
-    far_near = ((ly_far, ly_ref), (lz_far, lz_ref), (fb_far, fb), (den_far, den))
-    copies = [pltpu.make_async_copy(far, near, sems.at[n]) for n, (far, near) in enumerate(far_near)]
-    for copy in copies:
-        copy.start()
-    copies[0].wait()
-    copies[1].wait()
+def roll(x, by, axis):
+    return pltpu.roll(x, by % x.shape[axis], axis)
+
+
+def hall(p, fb, den, my, mz, ylo_ref, yhi_ref, zlo, zhi):
     rows, lanes = fb.shape[2], fb.shape[3]
     row = lax.broadcasted_iota(jnp.int32, (rows, lanes), 0)
     lane = lax.broadcasted_iota(jnp.int32, (rows, lanes), 1)
-    half_y = jnp.broadcast_to(0.5 * metric(ly_ref[...]), (8, rows))
-    upright = jnp.transpose(jnp.concatenate([zlo_ref[...], zhi_ref[...], half_y], axis=0))
-    my = jnp.broadcast_to(upright[:, 8:9], (rows, lanes))
-    mz = 0.5 * metric(lz_ref[...])
 
     def d_y(f, at):
-        up = jnp.where(row == rows - 1, yhi_ref[at : at + 1, :], pltpu.roll(f, rows - 1, 0))
-        down = jnp.where(row == 0, ylo_ref[at : at + 1, :], pltpu.roll(f, 1, 0))
+        up = jnp.where(row == rows - 1, yhi_ref[at : at + 1, :], roll(f, -1, 0))
+        down = jnp.where(row == 0, ylo_ref[at : at + 1, :], roll(f, 1, 0))
         return (up - down) * my
 
     def d_z(f, at):
-        up = jnp.where(lane == lanes - 1, upright[:, 4 + at : 5 + at], pltpu.roll(f, lanes - 1, 1))
-        down = jnp.where(lane == 0, upright[:, at : at + 1], pltpu.roll(f, 1, 1))
+        up = jnp.where(lane == lanes - 1, zhi[at], roll(f, -1, 1))
+        down = jnp.where(lane == 0, zlo[at], roll(f, 1, 1))
         return (up - down) * mz
 
-    copies[2].wait()
-    copies[3].wait()
+    b_x, b_y, b_z = fb[0, p], fb[1, p], fb[2, p]
+    half = 0.5 if p == 0 else -0.5
+    cur_x = d_y(b_z, 2 + p) - d_z(b_y, 2 + p)
+    cur_y = d_z(b_x, p) - half * fb[2, 1 - p]
+    cur_z = half * fb[1, 1 - p] - d_y(b_x, p)
+    dens = den[p]
+    return (
+        (cur_y * b_z - cur_z * b_y) / dens,
+        (cur_z * b_x - cur_x * b_z) / dens,
+        (cur_x * b_y - cur_y * b_x) / dens,
+    )
+
+
+def fetched(far, near, sems):
+    copies = [pltpu.make_async_copy(a, b, sems.at[n]) for n, (a, b) in enumerate(zip(far, near))]
+    for copy in copies:
+        copy.start()
+    for copy in copies:
+        copy.wait()
+
+
+def metrics(ly_ref, lz_ref, shape):
+    half_y = jnp.broadcast_to(0.5 * metric(ly_ref[...]), (8, shape[0]))
+    return jnp.broadcast_to(jnp.transpose(half_y)[:, 0:1], shape), 0.5 * metric(lz_ref[...])
+
+
+def message_kernel(*refs):
+    far, (ylo_ref, yhi_ref, msg_ref), near, sems = refs[0:4], refs[4:7], refs[7:11], refs[11]
+    fetched(far, near, sems)
+    ly_ref, lz_ref, fb, den = near
+    shape = fb.shape[2:]
+    my, mz = metrics(ly_ref, lz_ref, shape)
+    lane = lax.broadcasted_iota(jnp.int32, shape, 1)
+    edge = (lane == 0) | (lane == 127)
+    slot = (lane + 1) >> 1
+    signed = jnp.where(lane == 0, -mz, mz)
+    none = [0.0] * 4
+    held = jnp.zeros(shape, F32)
+    own = jnp.zeros(shape, F32)
     for p in range(2):
-        b_x, b_y, b_z = fb[0, p], fb[1, p], fb[2, p]
-        half = 0.5 if p == 0 else -0.5
-        cur_x = d_y(b_z, 2 + p) - d_z(b_y, 2 + p)
-        cur_y = d_z(b_x, p) - half * fb[2, 1 - p]
-        cur_z = half * fb[1, 1 - p] - d_y(b_x, p)
-        dens = den[p]
-        parts = (
-            (cur_y * b_z - cur_z * b_y) / dens,
-            (cur_z * b_x - cur_x * b_z) / dens,
-            (cur_x * b_y - cur_y * b_x) / dens,
-        )
+        parts = hall(p, fb, den, my, mz, ylo_ref, yhi_ref, none, none)
+        weight = signed / den[p]
+        fields = [fb[comp, p] for comp in range(3)]
         for comp in range(3):
-            value = parts[comp].astype(BF)
-            emf_ref[comp, p] = value
+            value = jnp.where(edge, 0.0, parts[comp]).astype(BF)
             at = 16 * (2 * comp + p)
             for block in range(4):
                 for copy in range(4):
                     msg_ref[4 * block + copy, at : at + 16, :] = value[16 * block : 16 * block + 16]
+        terms = list(parts) + [f * weight for f in fields] + fields[0:2]
+        for q, term in enumerate(terms):
+            k = 8 * p + q + 1
+            held = jnp.where(slot == k, roll(term, 2 * k, 1), held)
+        for comp in range(2):
+            k = 2 * p + comp + 1
+            own = jnp.where(slot == k, roll(fields[comp], 2 * k, 1), own)
+    high = held.astype(BF).astype(F32)
+    low = (held - high).astype(BF).astype(F32)
+    held = (high + roll(low, 64, 1)).astype(BF)
+    first = own.astype(BF).astype(F32)
+    own = own - first
+    second = own.astype(BF).astype(F32)
+    own = first + roll(second, 8, 1) + roll(own - second, 16, 1)
+    folded = own[0:16]
+    for block in range(1, 4):
+        folded = folded + roll(own[16 * block : 16 * block + 16], 32 * block, 1)
+    folded = folded.astype(BF)
+    for block in range(4):
+        for copy in range(4):
+            msg_ref[4 * block + copy, 96:112, :] = held[16 * block : 16 * block + 16]
+            msg_ref[4 * block + copy, 112:128, :] = folded
+
+
+def emf_kernel(*refs):
+    far, (ylo_ref, yhi_ref, lines_ref, emf_ref), near, sems = refs[0:4], refs[4:8], refs[8:12], refs[12]
+    fetched(far, near, sems)
+    ly_ref, lz_ref, fb, den = near
+    my, mz = metrics(ly_ref, lz_ref, fb.shape[2:])
+    me = lax.axis_index("yh") * 4 + lax.axis_index("yl") * 2 + lax.axis_index("xh")
+
+    def columns(block, side):
+        folded = lines_ref[block, 112:128, :].astype(F32)
+        rows = []
+        for n in range(4):
+            own = roll(folded, -32 * n, 1)
+            rows.append(own + (roll(own, -8, 1) + roll(own, -16, 1)))
+        rows = jnp.concatenate(rows, axis=0)
+        at = [2 * (2 * p + comp + 1) - side for comp in range(2) for p in range(2)]
+        return [rows[:, n : n + 1] for n in at]
+
+    zlo = columns(lax.rem(me + 15, 16), 1)
+    zhi = columns(lax.rem(me + 1, 16), 0)
+    for p in range(2):
+        parts = hall(p, fb, den, my, mz, ylo_ref, yhi_ref, zlo, zhi)
+        for comp in range(3):
+            emf_ref[comp, p] = parts[comp].astype(BF)
+
+
+def finished_edges(x_ref):
+    held = jnp.concatenate([x_ref[i, 96:112, :] for i in range(16)], axis=0).astype(F32)
+    held = held + roll(held, 64, 1)
+    lane = lax.broadcasted_iota(jnp.int32, held.shape, 1)
+    slot = ((lane + 1) >> 1) & 7
+    beside = jnp.where((lane & 1) == 1, roll(roll(held, -16, 0), -1, 1), roll(roll(held, 16, 0), 1, 1))
+    flat = roll(beside, -12, 1) * jnp.where(slot == 1, roll(held, -10, 1), roll(held, -8, 1))
+    upright = roll(beside, -10, 1) * roll(held, -4, 1) + roll(beside, -8, 1) * roll(held, -2, 1)
+    held = held + jnp.where(slot == 3, -upright, flat)
+    edge = (lane == 0) | (lane == 127)
+    out = []
+    for comp in range(3):
+        for p in range(2):
+            k = 8 * p + comp + 1
+            out.append(jnp.where(edge, roll(held, -2 * k, 1), 0.0).astype(BF))
+    return out
 
 
 def z_kernel(x_ref, table_ref, out_ref, mix_ref):
+    edges = finished_edges(x_ref)
     zero = jnp.zeros((32, 512), BF)
     total = None
     for n in range(4):
-        lines = jnp.concatenate([x_ref[4 * n + i] for i in range(4)], axis=1)
-        lines = jnp.concatenate([lines, zero], axis=0)
+        lines = []
+        for i in range(4 * n, 4 * n + 4):
+            lines.append(x_ref[i, 0:96, :] + jnp.concatenate([x[16 * i : 16 * i + 16] for x in edges], axis=0))
+        lines = jnp.concatenate([jnp.concatenate(lines, axis=1), zero], axis=0)
         blocks = []
         for c in range(2):
             for kappa in range(16):
@@ -207,31 +295,27 @@
         count = lax.axis_size(axis)
         return lax.ppermute(cells, axis, [(i, (i + step) % count) for i in range(count)])
 
-    zlo = shift(field_b[0:2, :, :, z_local - 1].reshape(4, y_local), GZ, 1)
-    zhi = shift(field_b[0:2, :, :, 0].reshape(4, y_local), GZ, -1)
     ylo = shift(field_b[0::2, :, y_local - 1, :].reshape(4, z_local), GY, 1)
     yhi = shift(field_b[0::2, :, 0, :].reshape(4, z_local), GY, -1)
     small = pltpu.CompilerParams(vmem_limit_bytes=16 * 2**20)
     far = [
         pltpu.with_memory_space_constraint(x, pltpu.HBM)
-        for x in (field_b, density, level_y[None, :], level_z[None, :])
+        for x in (level_y[None, :], level_z[None, :], field_b, density)
     ]
-    emf, message = pl.pallas_call(
-        emf_kernel,
-        out_shape=(
-            jax.ShapeDtypeStruct(field_b.shape, BF),
-            jax.ShapeDtypeStruct((16, 96, z_local), BF),
-        ),
-        in_specs=[pl.BlockSpec(memory_space=pltpu.HBM)] * 4 + [pl.BlockSpec(memory_space=pltpu.VMEM)] * 4,
-        scratch_shapes=[
-            pltpu.VMEM(field_b.shape, F32),
-            pltpu.VMEM(density.shape, F32),
-            pltpu.VMEM((1, y_local), jnp.int32),
-            pltpu.VMEM((1, z_local), jnp.int32),
-            pltpu.SemaphoreType.DMA((4,)),
-        ],
+    scratch = [
+        pltpu.VMEM((1, y_local), jnp.int32),
+        pltpu.VMEM((1, z_local), jnp.int32),
+        pltpu.VMEM(field_b.shape, F32),
+        pltpu.VMEM(density.shape, F32),
+        pltpu.SemaphoreType.DMA((4,)),
+    ]
+    message = pl.pallas_call(
+        message_kernel,
+        out_shape=jax.ShapeDtypeStruct((16, 128, z_local), BF),
+        in_specs=[pl.BlockSpec(memory_space=pltpu.HBM)] * 4 + [pl.BlockSpec(memory_space=pltpu.VMEM)] * 2,
+        scratch_shapes=scratch,
         compiler_params=small,
-    )(*far, ylo, yhi, zlo, zhi)
+    )(*far, ylo, yhi)
     part = lax.axis_index("yl") * 2 + lax.axis_index("xh")
     quarter = lax.dynamic_index_in_dim(jnp.asarray(z_table()), part, keepdims=False)
     lines = lax.all_to_all(message, GZ, 0, 0, tiled=True)
@@ -241,6 +325,14 @@
         scratch_shapes=[pltpu.VMEM((512, 128), F32)],
         compiler_params=small,
     )(lines, quarter)
+    emf = pl.pallas_call(
+        emf_kernel,
+        out_shape=jax.ShapeDtypeStruct(field_b.shape, BF),
+        in_specs=[pl.BlockSpec(memory_space=pltpu.HBM)] * 4 + [pl.BlockSpec(memory_space=pltpu.VMEM)] * 3,
+        scratch_shapes=scratch,
+        compiler_params=small,
+        cost_estimate=pl.CostEstimate(flops=2_000_000, bytes_accessed=1_000_000, transcendentals=0),
+    )(*far, ylo, yhi, lines)
     spread = lax.all_to_all(z_modes.reshape(128, 4, 128), ("yh",) + GY, 0, 0, tiled=True).reshape(512, 128)
     first = ("yh", "yl", "c")
     second = ("xh", "z", "xl")

time: 103 us -> 98.6 us (0.957)
  blocking collectives: 55.4 us -> 43.6 us
  waiting for transfers between devices: 11.9 us -> 21.6 us
  starting transfers between devices: 26.3 us -> 21.6 us
  Pallas kernels: 4.27 us -> 7.39 us
    all_to_all x1 -> x0, blocking collectives: 13.5 us -> none  [on_device(): lax.all_to_all(copies, second, 0, 0, tiled=True)]
    ppermute x4 -> x2, starting transfers between devices: 19.6 us -> 10.7 us  [shift(): lax.ppermute(cells, axis, [(i, (i + step) % count) for i in range(count)])]
    all_to_all x0 -> x1, waiting for transfers between devices: none -> 8.5 us  [on_device(): lax.all_to_all(copies, second, 0, 0, tiled=True)]
    all_to_all x0 -> x1, starting transfers between devices: none -> 3.86 us  [on_device(): lax.all_to_all(copies, second, 0, 0, tiled=True)]
    pallas_call x1 -> x2, Pallas kernels: 2.03 us -> 4.42 us  [the longest x1 2.4 us: on_device(): pl.pallas_call(message_kernel, out_shape=jax.ShapeDtypeStruct((16, 128, z...]
    all_to_all x1, blocking collectives: 30.2 us -> 32 us  [on_device(): lax.all_to_all(z_modes.reshape(128, 4, 128), ('yh',) + GY, 0, 0, tiled=True)]
    slice x1 -> x0, local copies, waits for them, and re-layouts: 1.18 us -> none  [on_device(): zhi = shift(field_b[0:2, :, :, 0].reshape(4, y_local), GZ, -1)]
    all_to_all x1, waiting for transfers between devices: 11.2 us -> 12.3 us  [on_device(): lines = lax.all_to_all(message, GZ, 0, 0, tiled=True)]
  transfers between devices with their start and end apart: 5 -> 4, of which waited for: 2 -> 3; matrix products, arithmetic and copies ran while one was open for 2% -> 1% of each run, Pallas kernels for 0% -> 2%
where the time goes in v3:
time: 98.6 us; the launch traced here: 98.1 us
  blocking collectives  43.6 us (44%)
  starting transfers between devices  21.6 us (22%)
  waiting for transfers between devices  21.6 us (22%)
  Pallas kernels  7.39 us (7%)
  local copies, waits for them, and re-layouts  2.5 us (3%)
    all_to_all x1, blocking collectives, on_device(): lax.all_to_all(z_modes.reshape(128, 4, 128), ('yh',) + GY, 0, 0, tiled=True)  32 us
    all_to_all x1, waiting for transfers between devices, on_device(): lines = lax.all_to_all(message, GZ, 0, 0, tiled=True)  12.3 us
    all_to_all x1, blocking collectives, on_device(): sums = jnp.sum(lax.all_to_all(sums, first, 0, 0, tiled=True), axis=0)  11.6 us
    ppermute x2, starting transfers between devices, shift(): lax.ppermute(cells, axis, [(i, (i + step) % count) for i in range(count)])  10.7 us
    all_to_all x1, waiting for transfers between devices, on_device(): lax.all_to_all(copies, second, 0, 0, tiled=True)  8.5 us
    all_to_all x1, starting transfers between devices, on_device(): lines = lax.all_to_all(message, GZ, 0, 0, tiled=True)  7.01 us
    all_to_all x1, starting transfers between devices, on_device(): lax.all_to_all(copies, second, 0, 0, tiled=True)  3.86 us
    pallas_call x1, Pallas kernels, on_device(): pl.pallas_call(message_kernel, out_shape=jax.ShapeDtypeStruct((16, 128, z...  2.4 us
  transfers between devices with their start and end apart: 4, of which 3 were waited for; matrix products, arithmetic and copies ran while one was open for 1% of the time, Pallas kernels for 2%

profile of v3, /device:TPU:1, one launch (start us, length us, event | category | flops | bytes accessed | tf_op | source)
XLA Modules:
  0.0 98.1 jit_solution(17405368654575332846)
XLA Ops:
  0.6 0.7 fusion
  1.4 4.5 %collective-permute-start = (f32[4,128]{1,0:T(4,128)S(1)}, f32[4,128]{1,0:T(4,128)S(1)}, u32[]{:S(2)}, u32[]{:S(2)}) collective-permute-start(f32[4,128]{1,0:T(4,128)S(1)} %bitcast.17), channel_id=1, source_target_pairs={{0,1},{1,2},{2,3},{3,4},{4,5},{5,6},{6,7},{7,8},{8,9},{9,10},{10,1... | collective-permute-start | bytes 6152 | tf_op jit(solution)/shard_map/ppermute | solution.py:296
  5.9 6.2 %collective-permute-start.1 = (f32[4,128]{1,0:T(4,128)S(1)}, f32[4,128]{1,0:T(4,128)S(1)}, u32[]{:S(2)}, u32[]{:S(2)}) collective-permute-start(f32[4,128]{1,0:T(4,128)S(1)} %bitcast.16), channel_id=1, source_target_pairs={{0,31},{1,0},{2,1},{3,2},{4,3},{5,4},{6,5},{7,6},{8,7},{9,8},{10,9... | collective-permute-start | bytes 6152 | tf_op jit(solution)/shard_map/ppermute | solution.py:296
  12.1 0.0 collective-permute-done.refs_4_
  12.1 0.8 collective-permute-done.1.refs_5_
  12.9 0.0 copy-start
  12.9 0.0 copy-start.1
  12.9 0.0 copy-start.2
  12.9 0.0 copy-start.3
  12.9 2.4 %shard_map.112 = bf16[16,128,128]{2,1,0:T(8,128)(2,1)} custom-call(s32[1,64]{1,0:T(1,128)} %bitcast.12, s32[1,128]{1,0:T(1,128)} %bitcast.14, f32[3,2,64,128]{3,2,1,0:T(8,128)} %refs_2_.3, f32[2,64,128]{2,1,0:T(8,128)} %refs_3_.3, f32[4,128]{1,0:T(4,128)S(1)} %collective-permute-done.refs_4_, f32[4,128]{1,0:T(4,128)S(1)} %collective-permute-done.1.refs_5_), custom_call_target="tpu_custom_call" | custom-call | tf_op jit(solution)/shard_map/pallas_call | solution.py:312
  15.3 7.0 %all-to-all-start = ((bf16[16,128,128]{2,1,0:T(8,128)(2,1)}), bf16[16,128,128]{2,1,0:T(8,128)(2,1)S(1)}, u32[]{:S(2)}, u32[]{:S(2)}) async-start(bf16[16,128,128]{2,1,0:T(8,128)(2,1)} %shard_map.112), calls=%async_computation | async-start | bytes 1048576 | tf_op jit(solution)/shard_map/all_to_all | solution.py:321
  22.3 1.1 %dynamic-slice_bitcast_fusion.table_ref = bf16[8,256,128]{2,1,0:T(8,128)(2,1)S(1)} fusion(bf16[4,8,256,128]{3,2,1,0:T(8,128)(2,1)} %constant.28.clone, s32[]{:T(128)S(6)} %select_n.4), kind=kLoop, calls=%fused_computation | loop fusion | bytes 1048580 | tf_op jit(solution)/shard_map/jit(dynamic_index_in_dim)/squeeze | solution.py:320
  23.4 12.3 %all-to-all-done.refs_6_.x_ref = bf16[16,128,128]{2,1,0:T(8,128)(2,1)S(1)} async-done(((bf16[16,128,128]{2,1,0:T(8,128)(2,1)}), bf16[16,128,128]{2,1,0:T(8,128)(2,1)S(1)}, u32[]{:S(2)}, u32[]{:S(2)}) %all-to-all-start) | async-done | bytes 524320 | tf_op jit(solution)/shard_map/all_to_all | solution.py:321
  35.7 1.6 %shard_map.114 = bf16[512,128]{1,0:T(8,128)(2,1)S(1)} custom-call(bf16[16,128,128]{2,1,0:T(8,128)(2,1)S(1)} %all-to-all-done.refs_6_.x_ref, bf16[8,256,128]{2,1,0:T(8,128)(2,1)S(1)} %dynamic-slice_bitcast_fusion.table_ref), custom_call_target="tpu_custom_call" | custom-call | tf_op jit(solution)/shard_map/pallas_call | solution.py:322
  37.3 32.0 %all_to_all.20 = bf16[128,4,128]{2,1,0:T(4,128)(2,1)S(1)} all-to-all(bf16[128,4,128]{2,1,0:T(4,128)(2,1)S(1)} %bitcast.9), channel_id=1, replica_groups=mesh['yh'=4,'yl'=2,'xh'=2,'z'=8,'xl'=2,'c'=2] {'yh','z','xl','c'}, dimensions={0} | all-to-all | bytes 262144 | tf_op jit(solution)/shard_map/all_to_all | solution.py:336
  69.3 0.0 copy-done
  69.3 0.0 copy-done.1
  69.3 0.0 copy-done.2
  69.3 0.0 copy-done.3
  69.3 1.4 %shard_map.115 = (f32[2,2048]{1,0:T(2,128)}, f32[16,8,128]{2,1,0:T(8,128)S(1)}) custom-call(bf16[512,128]{1,0:T(8,128)(2,1)S(1)} %bitcast.10, bf16[512,512]{1,0:T(8,128)(2,1)S(1)} %copy-done, f32[2,16,128]{2,1,0:T(8,128)S(1)} %copy-done.3, bf16[128,128]{1,0:T(8,128)(2,1)S(1)} %copy-done.1, s32[2,2048]{1,0:T(2,128)S(1)} %copy-done.2), custom_call_target="tpu_custom_call" | custom-call | tf_op jit(solution)/shard_map/pallas_call | solution.py:339
  70.7 11.6 %all_to_all.21 = f32[16,8,128]{2,1,0:T(8,128)S(1)} all-to-all(f32[16,8,128]{2,1,0:T(8,128)S(1)} %get-tuple-element.6), channel_id=1, replica_groups=mesh['yh'=4,'yl'=2,'xh'=2,'z'=8,'xl'=2,'c'=2] {'yh','yl','c'}, dimensions={0} | all-to-all | bytes 131072 | tf_op jit(solution)/shard_map/all_to_all | solution.py:347
  82.4 0.7 broadcast_in_dim.14
  83.0 3.9 %all-to-all-start.3 = ((f32[32,8,128]{2,1,0:T(8,128)}), f32[32,8,128]{2,1,0:T(8,128)S(1)}, u32[]{:S(2)}, u32[]{:S(2)}) async-start(f32[32,8,128]{2,1,0:T(8,128)} %broadcast_in_dim.14), calls=%async_computation.3 | async-start | bytes 262144 | tf_op jit(solution)/shard_map/all_to_all | solution.py:349
  86.9 2.0 %shard_map.113 = bf16[3,2,64,128]{3,2,1,0:T(8,128)(2,1)} custom-call(s32[1,64]{1,0:T(1,128)} %bitcast.13, s32[1,128]{1,0:T(1,128)} %bitcast.15, f32[3,2,64,128]{3,2,1,0:T(8,128)} %refs_2_.3, f32[2,64,128]{2,1,0:T(8,128)} %refs_3_.3, f32[4,128]{1,0:T(4,128)S(1)} %collective-permute-done.refs_4_, f32[4,128]{1,0:T(4,128)S(1)} %collective-permute-done.1.refs_5_, ...), custom_call_target="tpu_custom_call" | custom-call | flops 2000000 | bytes 1000000 | tf_op jit(solution)/shard_map/pallas_call | solution.py:328
  88.9 8.5 %all-to-all-done.3 = f32[32,8,128]{2,1,0:T(8,128)S(1)} async-done(((f32[32,8,128]{2,1,0:T(8,128)}), f32[32,8,128]{2,1,0:T(8,128)S(1)}, u32[]{:S(2)}, u32[]{:S(2)}) %all-to-all-start.3) | async-done | bytes 131104 | tf_op jit(solution)/shard_map/all_to_all | solution.py:349
  97.4 0.6 reduce_sum.19
  (1 shorter events, 0.0 us)
Async XLA Ops:
  1.4 10.7 %collective-permute-start = (f32[4,128]{1,0:T(4,128)S(1)}, f32[4,128]{1,0:T(4,128)S(1)}, u32[]{:S(2)}, u32[]{:S(2)}) collective-permute-start(f32[4,128]{1,0:T(4,128)S(1)} %bitcast.17), channel_id=1, source_target_pairs={{0,1},{1,2},{2,3},{3,4},{4,5},{5,6},{6,7},{7,8},{8,9},{9,10},{10,1... | collective-permute-start | bytes 6152 | tf_op jit(solution)/shard_map/ppermute | solution.py:296
  5.9 7.0 %collective-permute-start.1 = (f32[4,128]{1,0:T(4,128)S(1)}, f32[4,128]{1,0:T(4,128)S(1)}, u32[]{:S(2)}, u32[]{:S(2)}) collective-permute-start(f32[4,128]{1,0:T(4,128)S(1)} %bitcast.16), channel_id=1, source_target_pairs={{0,31},{1,0},{2,1},{3,2},{4,3},{5,4},{6,5},{7,6},{8,7},{9,8},{10,9... | collective-permute-start | bytes 6152 | tf_op jit(solution)/shard_map/ppermute | solution.py:296
  12.9 56.4 %copy-start = (bf16[512,512]{1,0:T(8,128)(2,1)S(1)}, bf16[512,512]{1,0:T(8,128)(2,1)}, u32[]{:S(2)}) copy-start(bf16[512,512]{1,0:T(8,128)(2,1)} %constant.29.clone.table_ref) | copy-start | bytes 1572868
  12.9 56.4 %copy-start.1 = (bf16[128,128]{1,0:T(8,128)(2,1)S(1)}, bf16[128,128]{1,0:T(8,128)(2,1)}, u32[]{:S(2)}) copy-start(bf16[128,128]{1,0:T(8,128)(2,1)} %constant.31.clone.order_ref) | copy-start | bytes 98308
  12.9 56.4 %copy-start.2 = (s32[2,2048]{1,0:T(2,128)S(1)}, s32[2,2048]{1,0:T(2,128)}, u32[]{:S(2)}) copy-start(s32[2,2048]{1,0:T(2,128)} %bins_ref.1) | copy-start | bytes 49156
  12.9 56.4 %copy-start.3 = (f32[2,16,128]{2,1,0:T(8,128)S(1)}, f32[2,16,128]{2,1,0:T(8,128)}, u32[]{:S(2)}) copy-start(f32[2,16,128]{2,1,0:T(8,128)} %constant.30.clone.turn_ref) | copy-start | bytes 49156
  15.3 20.4 %all-to-all-start = ((bf16[16,128,128]{2,1,0:T(8,128)(2,1)}), bf16[16,128,128]{2,1,0:T(8,128)(2,1)S(1)}, u32[]{:S(2)}, u32[]{:S(2)}) async-start(bf16[16,128,128]{2,1,0:T(8,128)(2,1)} %shard_map.112), calls=%async_computation | async-start | bytes 1048576 | tf_op jit(solution)/shard_map/all_to_all | solution.py:321
  83.0 14.4 %all-to-all-start.3 = ((f32[32,8,128]{2,1,0:T(8,128)}), f32[32,8,128]{2,1,0:T(8,128)S(1)}, u32[]{:S(2)}, u32[]{:S(2)}) async-start(f32[32,8,128]{2,1,0:T(8,128)} %broadcast_in_dim.14), calls=%async_computation.3 | async-start | bytes 262144 | tf_op jit(solution)/shard_map/all_to_all | solution.py:349

commit v4 on v3

--- a/solution.py
+++ b/solution.py
@@ -297,6 +297,9 @@
 
     ylo = shift(field_b[0::2, :, y_local - 1, :].reshape(4, z_local), GY, 1)
     yhi = shift(field_b[0::2, :, 0, :].reshape(4, z_local), GY, -1)
+    part = lax.axis_index("yl") * 2 + lax.axis_index("xh")
+    quarter = lax.dynamic_index_in_dim(jnp.asarray(z_table()), part, keepdims=False)
+    quarter, ylo, yhi = lax.optimization_barrier((quarter, ylo, yhi))
     small = pltpu.CompilerParams(vmem_limit_bytes=16 * 2**20)
     far = [
         pltpu.with_memory_space_constraint(x, pltpu.HBM)
@@ -316,8 +319,6 @@
         scratch_shapes=scratch,
         compiler_params=small,
     )(*far, ylo, yhi)
-    part = lax.axis_index("yl") * 2 + lax.axis_index("xh")
-    quarter = lax.dynamic_index_in_dim(jnp.asarray(z_table()), part, keepdims=False)
     lines = lax.all_to_all(message, GZ, 0, 0, tiled=True)
     z_modes = pl.pallas_call(
         z_kernel,

time: 98.6 us -> 97.4 us (0.988)
  blocking collectives: 43.6 us -> 63.4 us
  waiting for transfers between devices: 21.6 us -> 8.51 us
  starting transfers between devices: 21.6 us -> 14.5 us
    all_to_all x0 -> x1, blocking collectives: none -> 19.8 us  [on_device(): lines = lax.all_to_all(message, GZ, 0, 0, tiled=True)]
    all_to_all x1 -> x0, waiting for transfers between devices: 12.3 us -> none  [on_device(): lines = lax.all_to_all(message, GZ, 0, 0, tiled=True)]
    all_to_all x1 -> x0, starting transfers between devices: 7.01 us -> none  [on_device(): lines = lax.all_to_all(message, GZ, 0, 0, tiled=True)]
  transfers between devices with their start and end apart: 4 -> 3, of which waited for: 3 -> 1; matrix products, arithmetic and copies ran while one was open for 1% -> 1% of each run, Pallas kernels for 2% -> 2%
where the time goes in v4:
time: 97.4 us; the launch traced here: 97 us
  blocking collectives  63.4 us (65%)
  starting transfers between devices  14.5 us (15%)
  waiting for transfers between devices  8.51 us (9%)
  Pallas kernels  6.56 us (7%)
  local copies, waits for them, and re-layouts  2.57 us (3%)
    all_to_all x1, blocking collectives, on_device(): lax.all_to_all(z_modes.reshape(128, 4, 128), ('yh',) + GY, 0, 0, tiled=True)  32 us
    all_to_all x1, blocking collectives, on_device(): lines = lax.all_to_all(message, GZ, 0, 0, tiled=True)  19.8 us
    all_to_all x1, blocking collectives, on_device(): sums = jnp.sum(lax.all_to_all(sums, first, 0, 0, tiled=True), axis=0)  11.6 us
    ppermute x2, starting transfers between devices, shift(): lax.ppermute(cells, axis, [(i, (i + step) % count) for i in range(count)])  10.7 us
    all_to_all x1, waiting for transfers between devices, on_device(): lax.all_to_all(copies, second, 0, 0, tiled=True)  8.5 us
    all_to_all x1, starting transfers between devices, on_device(): lax.all_to_all(copies, second, 0, 0, tiled=True)  3.85 us
    pallas_call x1, Pallas kernels, on_device(): pl.pallas_call(emf_kernel, out_shape=jax.ShapeDtypeStruct(field_b.shape,...  2.02 us
  transfers between devices with their start and end apart: 3, of which 1 were waited for; matrix products, arithmetic and copies ran while one was open for 1% of the time, Pallas kernels for 2%

profile of v4, /device:TPU:1, one launch (start us, length us, event | category | flops | bytes accessed | tf_op | source)
XLA Modules:
  0.0 97.0 jit_solution(6421602556825514517)
XLA Ops:
  0.6 0.7 fusion
  1.4 4.5 %collective-permute-start = (f32[4,128]{1,0:T(4,128)S(1)}, f32[4,128]{1,0:T(4,128)S(1)}, u32[]{:S(2)}, u32[]{:S(2)}) collective-permute-start(f32[4,128]{1,0:T(4,128)S(1)} %bitcast.17), channel_id=1, source_target_pairs={{0,1},{1,2},{2,3},{3,4},{4,5},{5,6},{6,7},{7,8},{8,9},{9,10},{10,1... | collective-permute-start | bytes 6152 | tf_op jit(solution)/shard_map/ppermute | solution.py:296
  5.9 6.2 %collective-permute-start.1 = (f32[4,128]{1,0:T(4,128)S(1)}, f32[4,128]{1,0:T(4,128)S(1)}, u32[]{:S(2)}, u32[]{:S(2)}) collective-permute-start(f32[4,128]{1,0:T(4,128)S(1)} %bitcast.16), channel_id=1, source_target_pairs={{0,31},{1,0},{2,1},{3,2},{4,3},{5,4},{6,5},{7,6},{8,7},{9,8},{10,9... | collective-permute-start | bytes 6152 | tf_op jit(solution)/shard_map/ppermute | solution.py:296
  12.1 0.0 copy-start
  12.1 0.0 copy-start.1
  12.1 0.0 copy-start.2
  12.1 0.0 copy-start.3
  12.1 1.1 %dynamic-slice_bitcast_fusion.table_ref = bf16[8,256,128]{2,1,0:T(8,128)(2,1)S(1)} fusion(bf16[4,8,256,128]{3,2,1,0:T(8,128)(2,1)} %constant.28.clone, s32[]{:T(128)S(6)} %select_n.4), kind=kLoop, calls=%fused_computation | loop fusion | bytes 1048580 | tf_op jit(solution)/shard_map/jit(dynamic_index_in_dim)/squeeze | solution.py:301
  13.3 0.0 collective-permute-done.refs_4_
  13.3 0.0 collective-permute-done.1.refs_5_
  13.3 1.6 %shard_map.112 = bf16[16,128,128]{2,1,0:T(8,128)(2,1)S(1)} custom-call(s32[1,64]{1,0:T(1,128)} %bitcast.12, s32[1,128]{1,0:T(1,128)} %bitcast.14, f32[3,2,64,128]{3,2,1,0:T(8,128)} %refs_2_.3, f32[2,64,128]{2,1,0:T(8,128)} %refs_3_.3, f32[4,128]{1,0:T(4,128)S(1)} %collective-permute-done.refs_4_, f32[4,128]{1,0:T(4,128)S(1)} %collective-permute-done.1.refs_5_), custom_call_target="tpu_custom_call" | custom-call | tf_op jit(solution)/shard_map/pallas_call | solution.py:315
  14.9 19.8 %all_to_all.20.refs_6_.x_ref = bf16[16,128,128]{2,1,0:T(8,128)(2,1)S(1)} all-to-all(bf16[16,128,128]{2,1,0:T(8,128)(2,1)S(1)} %shard_map.112), channel_id=1, replica_groups=mesh['yh'=4,'yl'=2,'xh'=2,'z'=8,'xl'=2,'c'=2] {'yh','yl','xh'}, dimensions={0} | all-to-all | bytes 1048576 | tf_op jit(solution)/shard_map/all_to_all | solution.py:322
  34.6 1.6 %shard_map.114 = bf16[512,128]{1,0:T(8,128)(2,1)S(1)} custom-call(bf16[16,128,128]{2,1,0:T(8,128)(2,1)S(1)} %all_to_all.20.refs_6_.x_ref, bf16[8,256,128]{2,1,0:T(8,128)(2,1)S(1)} %dynamic-slice_bitcast_fusion.table_ref), custom_call_target="tpu_custom_call" | custom-call | tf_op jit(solution)/shard_map/pallas_call | solution.py:323
  36.2 32.0 %all_to_all.21 = bf16[128,4,128]{2,1,0:T(4,128)(2,1)S(1)} all-to-all(bf16[128,4,128]{2,1,0:T(4,128)(2,1)S(1)} %bitcast.9), channel_id=1, replica_groups=mesh['yh'=4,'yl'=2,'xh'=2,'z'=8,'xl'=2,'c'=2] {'yh','z','xl','c'}, dimensions={0} | all-to-all | bytes 262144 | tf_op jit(solution)/shard_map/all_to_all | solution.py:337
  68.2 0.0 copy-done
  68.2 0.0 copy-done.1
  68.2 0.0 copy-done.2
  68.3 0.0 copy-done.3
  68.3 1.4 %shard_map.115 = (f32[2,2048]{1,0:T(2,128)}, f32[16,8,128]{2,1,0:T(8,128)S(1)}) custom-call(bf16[512,128]{1,0:T(8,128)(2,1)S(1)} %bitcast.10, bf16[512,512]{1,0:T(8,128)(2,1)S(1)} %copy-done, f32[2,16,128]{2,1,0:T(8,128)S(1)} %copy-done.3, bf16[128,128]{1,0:T(8,128)(2,1)S(1)} %copy-done.1, s32[2,2048]{1,0:T(2,128)S(1)} %copy-done.2), custom_call_target="tpu_custom_call" | custom-call | tf_op jit(solution)/shard_map/pallas_call | solution.py:340
  69.7 11.6 %all_to_all.22 = f32[16,8,128]{2,1,0:T(8,128)S(1)} all-to-all(f32[16,8,128]{2,1,0:T(8,128)S(1)} %get-tuple-element.12), channel_id=1, replica_groups=mesh['yh'=4,'yl'=2,'xh'=2,'z'=8,'xl'=2,'c'=2] {'yh','yl','c'}, dimensions={0} | all-to-all | bytes 131072 | tf_op jit(solution)/shard_map/all_to_all | solution.py:348
  81.3 0.7 broadcast_in_dim.14
  82.0 3.9 %all-to-all-start.3 = ((f32[32,8,128]{2,1,0:T(8,128)}), f32[32,8,128]{2,1,0:T(8,128)S(1)}, u32[]{:S(2)}, u32[]{:S(2)}) async-start(f32[32,8,128]{2,1,0:T(8,128)} %broadcast_in_dim.14), calls=%async_computation.3 | async-start | bytes 262144 | tf_op jit(solution)/shard_map/all_to_all | solution.py:350
  85.8 2.0 %shard_map.113 = bf16[3,2,64,128]{3,2,1,0:T(8,128)(2,1)} custom-call(s32[1,64]{1,0:T(1,128)} %bitcast.13, s32[1,128]{1,0:T(1,128)} %bitcast.15, f32[3,2,64,128]{3,2,1,0:T(8,128)} %refs_2_.3, f32[2,64,128]{2,1,0:T(8,128)} %refs_3_.3, f32[4,128]{1,0:T(4,128)S(1)} %collective-permute-done.refs_4_, f32[4,128]{1,0:T(4,128)S(1)} %collective-permute-done.1.refs_5_, ...), custom_call_target="tpu_custom_call" | custom-call | flops 2000000 | bytes 1000000 | tf_op jit(solution)/shard_map/pallas_call | solution.py:329
  87.8 8.5 %all-to-all-done.3 = f32[32,8,128]{2,1,0:T(8,128)S(1)} async-done(((f32[32,8,128]{2,1,0:T(8,128)}), f32[32,8,128]{2,1,0:T(8,128)S(1)}, u32[]{:S(2)}, u32[]{:S(2)}) %all-to-all-start.3) | async-done | bytes 131104 | tf_op jit(solution)/shard_map/all_to_all | solution.py:350
  96.3 0.6 reduce_sum.19
  (1 shorter events, 0.0 us)
Async XLA Ops:
  1.4 11.9 %collective-permute-start = (f32[4,128]{1,0:T(4,128)S(1)}, f32[4,128]{1,0:T(4,128)S(1)}, u32[]{:S(2)}, u32[]{:S(2)}) collective-permute-start(f32[4,128]{1,0:T(4,128)S(1)} %bitcast.17), channel_id=1, source_target_pairs={{0,1},{1,2},{2,3},{3,4},{4,5},{5,6},{6,7},{7,8},{8,9},{9,10},{10,1... | collective-permute-start | bytes 6152 | tf_op jit(solution)/shard_map/ppermute | solution.py:296
  5.9 7.4 %collective-permute-start.1 = (f32[4,128]{1,0:T(4,128)S(1)}, f32[4,128]{1,0:T(4,128)S(1)}, u32[]{:S(2)}, u32[]{:S(2)}) collective-permute-start(f32[4,128]{1,0:T(4,128)S(1)} %bitcast.16), channel_id=1, source_target_pairs={{0,31},{1,0},{2,1},{3,2},{4,3},{5,4},{6,5},{7,6},{8,7},{9,8},{10,9... | collective-permute-start | bytes 6152 | tf_op jit(solution)/shard_map/ppermute | solution.py:296
  12.1 56.2 %copy-start = (bf16[512,512]{1,0:T(8,128)(2,1)S(1)}, bf16[512,512]{1,0:T(8,128)(2,1)}, u32[]{:S(2)}) copy-start(bf16[512,512]{1,0:T(8,128)(2,1)} %constant.29.clone.table_ref) | copy-start | bytes 1572868
  12.1 56.1 %copy-start.1 = (bf16[128,128]{1,0:T(8,128)(2,1)S(1)}, bf16[128,128]{1,0:T(8,128)(2,1)}, u32[]{:S(2)}) copy-start(bf16[128,128]{1,0:T(8,128)(2,1)} %constant.31.clone.order_ref) | copy-start | bytes 98308
  12.1 56.1 %copy-start.2 = (s32[2,2048]{1,0:T(2,128)S(1)}, s32[2,2048]{1,0:T(2,128)}, u32[]{:S(2)}) copy-start(s32[2,2048]{1,0:T(2,128)} %bins_ref.1) | copy-start | bytes 49156
  12.1 56.1 %copy-start.3 = (f32[2,16,128]{2,1,0:T(8,128)S(1)}, f32[2,16,128]{2,1,0:T(8,128)}, u32[]{:S(2)}) copy-start(f32[2,16,128]{2,1,0:T(8,128)} %constant.30.clone.turn_ref) | copy-start | bytes 49156
  82.0 14.4 %all-to-all-start.3 = ((f32[32,8,128]{2,1,0:T(8,128)}), f32[32,8,128]{2,1,0:T(8,128)S(1)}, u32[]{:S(2)}, u32[]{:S(2)}) async-start(f32[32,8,128]{2,1,0:T(8,128)} %broadcast_in_dim.14), calls=%async_computation.3 | async-start | bytes 262144 | tf_op jit(solution)/shard_map/all_to_all | solution.py:350

commit v5 on v3

v5 whole, which is shorter than its diff:
```python
import math

import jax
import jax.numpy as jnp
import numpy as np
from jax import lax
from jax.experimental import pallas as pl
from jax.experimental.pallas import tpu as pltpu
from jax.sharding import Mesh, PartitionSpec as P

NY = 2048
NZ = 2048
NB = 1024
KZ = 1024
BF = jnp.bfloat16
F32 = jnp.float32
GZ = ("yh", "yl", "xh")
GY = ("z", "xl", "c")
ACROSS = (((1,), (1,)), ((), ()))


def angle(a, b, length):
    return 2.0 * math.pi * ((a[:, None] * b[None, :]) % length) / length


def z_table():
    part, kappa, y, jh = np.meshgrid(*(np.arange(n) for n in (2, 16, 8, 4)), indexing="ij")
    modes = (16 * (8 * y + 4 * part + jh) + kappa).reshape(2, 1, 512, 1)
    turn = (modes * np.arange(128) % NZ + 128 * np.arange(8).reshape(1, 8, 1, 1)) % NZ
    return (np.cos(2.0 * math.pi * turn / NZ) / math.sqrt(NZ)).astype(jnp.bfloat16)


def y_tables():
    inner = angle((8 * np.arange(32)[None, :] + np.arange(8)[:, None]).reshape(-1), np.arange(256), 256)
    cos, sin = np.cos(inner), np.sin(inner)
    table = np.stack([np.stack([cos, -sin], axis=1), np.stack([sin, cos], axis=1)], axis=1)
    turn = angle(np.arange(8), np.arange(256), NY)
    order = np.zeros((128, 128), np.float32)
    for e in range(2):
        for cp in range(6):
            for y0 in range(8):
                order[16 * y0 + 8 * e + cp, 64 * e + 8 * cp + y0] = 1.0
    return (
        table.reshape(512, 512).astype(jnp.bfloat16),
        np.stack([np.cos(turn), np.sin(turn)]).astype(np.float32),
        order.astype(jnp.bfloat16),
    )


def metric(level):
    return 1.0 / (1.0 + 0.25 * level.astype(F32))


def roll(x, by, axis):
    return pltpu.roll(x, by % x.shape[axis], axis)


def hall(p, fb, den, my, mz, ylo_ref, yhi_ref, zlo, zhi):
    rows, lanes = fb.shape[2], fb.shape[3]
    row = lax.broadcasted_iota(jnp.int32, (rows, lanes), 0)
    lane = lax.broadcasted_iota(jnp.int32, (rows, lanes), 1)

    def d_y(f, at):
        up = jnp.where(row == rows - 1, yhi_ref[at : at + 1, :], roll(f, -1, 0))
        down = jnp.where(row == 0, ylo_ref[at : at + 1, :], roll(f, 1, 0))
        return (up - down) * my

    def d_z(f, at):
        up = jnp.where(lane == lanes - 1, zhi[at], roll(f, -1, 1))
        down = jnp.where(lane == 0, zlo[at], roll(f, 1, 1))
        return (up - down) * mz

    b_x, b_y, b_z = fb[0, p], fb[1, p], fb[2, p]
    half = 0.5 if p == 0 else -0.5
    cur_x = d_y(b_z, 2 + p) - d_z(b_y, 2 + p)
    cur_y = d_z(b_x, p) - half * fb[2, 1 - p]
    cur_z = half * fb[1, 1 - p] - d_y(b_x, p)
    dens = den[p]
    return (
        (cur_y * b_z - cur_z * b_y) / dens,
        (cur_z * b_x - cur_x * b_z) / dens,
        (cur_x * b_y - cur_y * b_x) / dens,
    )


def fetched(far, near, sems):
    copies = [pltpu.make_async_copy(a, b, sems.at[n]) for n, (a, b) in enumerate(zip(far, near))]
    for copy in copies:
        copy.start()
    for copy in copies:
        copy.wait()


def metrics(ly_ref, lz_ref, shape):
    half_y = jnp.broadcast_to(0.5 * metric(ly_ref[...]), (8, shape[0]))
    return jnp.broadcast_to(jnp.transpose(half_y)[:, 0:1], shape), 0.5 * metric(lz_ref[...])


def message_kernel(*refs):
    far, (ylo_ref, yhi_ref, msg_ref, held_ref, emf_ref), near, sems = refs[0:4], refs[4:9], refs[9:13], refs[13]
    fetched(far, near, sems)
    ly_ref, lz_ref, fb, den = near
    shape = fb.shape[2:]
    my, mz = metrics(ly_ref, lz_ref, shape)
    lane = lax.broadcasted_iota(jnp.int32, shape, 1)
    edge = (lane == 0) | (lane == 127)
    slot = lane >> 1
    signed = jnp.where(lane == 0, -mz, mz)
    none = [0.0] * 4
    inside, held = [], []
    own = jnp.zeros(shape, F32)
    for p in range(2):
        parts = hall(p, fb, den, my, mz, ylo_ref, yhi_ref, none, none)
        weight = signed / den[p]
        fields = [fb[comp, p] for comp in range(3)]
        inside.append([jnp.where(edge, 0.0, part) for part in parts])
        terms = list(parts) + [f * weight for f in fields] + fields[0:2]
        packed = jnp.zeros(shape, F32)
        for q, term in enumerate(terms):
            packed = jnp.where(slot == q, roll(term, 2 * q + 1, 1), packed)
        held.append(packed)
        for comp in range(2):
            k = 2 * p + comp
            own = jnp.where(slot == k, roll(fields[comp], 2 * k + 1, 1), own)
        for comp in range(3):
            emf_ref[comp, p] = inside[p][comp].astype(BF)
    held_ref[...] = held[0] + roll(held[1], 16, 1)
    first = own.astype(BF).astype(F32)
    own = own - first
    second = own.astype(BF).astype(F32)
    own = first + roll(second, 8, 1) + roll(own - second, 16, 1)
    folded = roll(own[0:16], 32, 1)
    for block in range(1, 4):
        folded = folded + roll(own[16 * block : 16 * block + 16], 32 + 24 * block, 1)
    for block in range(8):
        rows = slice(8 * block, 8 * block + 8)
        tile = jnp.concatenate([held[0][rows], held[1][rows]], axis=0)
        high = tile.astype(BF).astype(F32)
        low = (tile - high).astype(BF).astype(F32)
        values = [jnp.concatenate([inside[0][comp][rows], inside[1][comp][rows]], axis=0) for comp in range(3)]
        values.append(high + roll(low, 16, 1) + folded)
        for n, value in enumerate(values):
            for copy in range(2):
                msg_ref[2 * block + copy, 16 * n : 16 * n + 16, :] = value.astype(BF)


def finished(held, beside):
    slot = (lax.broadcasted_iota(jnp.int32, held.shape, 1) >> 1) & 7
    flat = roll(beside, -12, 1) * jnp.where(slot == 0, roll(held, -10, 1), roll(held, -8, 1))
    upright = roll(beside, -10, 1) * roll(held, -4, 1) + roll(beside, -8, 1) * roll(held, -2, 1)
    return held + jnp.where(slot == 2, -upright, flat)


def at_edges(values, spot):
    lane = lax.broadcasted_iota(jnp.int32, values.shape, 1)
    return jnp.where((lane == 0) | (lane == 127), roll(values, -spot, 1), 0.0).astype(BF)


def line_edges(x_ref):
    held = jnp.concatenate([x_ref[i, 48:64, :] for i in range(16)], axis=0).astype(F32)
    held = held + roll(held, -16, 1)
    lane = lax.broadcasted_iota(jnp.int32, held.shape, 1)
    beside = jnp.where((lane & 1) == 0, roll(roll(held, -16, 0), -1, 1), roll(roll(held, 16, 0), 1, 1))
    values = finished(held, beside)
    return [at_edges(values, 2 * comp + 1) for comp in range(3)]


def finish_emf(x_ref, held_ref, inside_ref, emf_ref):
    me = lax.axis_index("yh") * 4 + lax.axis_index("yl") * 2 + lax.axis_index("xh")

    def fields(block):
        folded = x_ref[block, 48:64, :].astype(F32)
        rows = []
        for n in range(4):
            own = roll(folded, -(32 + 24 * n), 1)
            rows.append(own + (roll(own, -8, 1) + roll(own, -16, 1)))
        return jnp.concatenate(rows, axis=0)

    low, high = fields(lax.rem(me + 15, 16)), fields(lax.rem(me + 1, 16))
    lane = lax.broadcasted_iota(jnp.int32, low.shape, 1)
    beside = jnp.where((lane & 1) == 0, roll(high, -1, 1), roll(low, 1, 1))
    beside = jnp.where(lane < 16, roll(beside, 12, 1), roll(beside, 24, 1))
    values = finished(held_ref[...], beside)
    for comp in range(3):
        for p in range(2):
            emf_ref[comp, p] = inside_ref[comp, p] + at_edges(values, 16 * p + 2 * comp + 1)


def z_kernel(x_ref, table_ref, held_ref, inside_ref, out_ref, emf_ref, mix_ref):
    edges = line_edges(x_ref)
    zero = jnp.zeros((80, 512), BF)
    total = None
    for n in range(4):
        lines = []
        for i in range(4 * n, 4 * n + 4):
            tiles = [x_ref[i, 16 * c : 16 * c + 16, :] + edges[c][16 * i : 16 * i + 16] for c in range(3)]
            lines.append(jnp.concatenate(tiles, axis=0))
        lines = jnp.concatenate([jnp.concatenate(lines, axis=1), zero], axis=0)
        blocks = []
        for e in range(2):
            for c in range(2):
                for jl in range(8):
                    kappa = 2 * jl + e
                    turns = [(kappa * i + 4 * c) % 16 for i in range(4 * n, 4 * n + 4)]
                    cells = [table_ref[m % 8, 32 * kappa : 32 * kappa + 32, :] for m in turns]
                    blocks.append(jnp.concatenate([-x if m >= 8 else x for m, x in zip(turns, cells)], axis=1))
        product = lax.dot_general(jnp.concatenate(blocks, axis=0), lines, ACROSS, preferred_element_type=F32)
        total = product if n == 0 else total + product
    total = total[0:512] + roll(total[512:1024], 64, 1)
    for c in range(2):
        for jl in range(8):
            at = 32 * (8 * c + jl)
            mix_ref[pl.ds(2 * jl + c, 32, stride=16), :] = total[at : at + 32]
    out_ref[...] = mix_ref[...].astype(BF)
    finish_emf(x_ref, held_ref, inside_ref, emf_ref)


def add(a, b):
    return (a[0] + b[0], a[1] + b[1])


def sub(a, b):
    return (a[0] - b[0], a[1] - b[1])


def turned(a, eighths):
    eighths %= 16
    if eighths == 0:
        return a
    if eighths == 4:
        return (a[1], -a[0])
    if eighths == 2:
        r = math.sqrt(0.5)
        return ((a[0] + a[1]) * r, (a[1] - a[0]) * r)
    if eighths == 6:
        r = math.sqrt(0.5)
        return ((a[1] - a[0]) * r, -(a[0] + a[1]) * r)
    cos, sin = math.cos(math.pi * eighths / 8), math.sin(math.pi * eighths / 8)
    return (a[0] * cos + a[1] * sin, a[1] * cos - a[0] * sin)


def fourier4(x):
    s, d = add(x[0], x[2]), sub(x[0], x[2])
    t, u = add(x[1], x[3]), turned(sub(x[1], x[3]), 4)
    return [add(s, t), add(d, u), sub(s, t), sub(d, u)]


def fourier8(x):
    even = fourier4([x[0], x[2], x[4], x[6]])
    odd = fourier4([x[1], x[3], x[5], x[7]])
    odd = [turned(value, 2 * k) for k, value in enumerate(odd)]
    return [add(a, b) for a, b in zip(even, odd)] + [sub(a, b) for a, b in zip(even, odd)]


def y_kernel(x_ref, table_ref, turn_ref, order_ref, bins_ref, power_ref, sums_ref):
    lhs = lax.dot_general(order_ref[...], x_ref[...], ACROSS, preferred_element_type=F32).astype(BF)
    product = jnp.dot(lhs, table_ref[...], preferred_element_type=F32)
    scale = 1.0 / (6.0 * NY)
    for e in range(2):
        held = []
        for y0 in range(8):
            at = 16 * y0 + 8 * e
            a, b = product[at : at + 8, 0:256], product[at : at + 8, 256:512]
            if y0 > 0:
                cos, sin = turn_ref[0, y0 : y0 + 1, :], turn_ref[1, y0 : y0 + 1, :]
                a, b = a * cos + b * sin, b * cos - a * sin
            held.append((a, b))
        for q1, (a, b) in enumerate(fourier8(held)):
            power_ref[e : e + 1, 256 * q1 : 256 * q1 + 256] = (
                jnp.sum(a * a + b * b, axis=0, keepdims=True) * scale
            )
    sums = jnp.zeros((8, 128), F32)
    for e in range(2):
        value = power_ref[e : e + 1, :]
        bins = bins_ref[e : e + 1, :]
        coarse = lax.broadcasted_iota(jnp.int32, (8, NY), 0) == (bins >> 7)
        fine = (lax.broadcasted_iota(jnp.int32, (128, NY), 0) == (bins & 127)).astype(F32).astype(BF)
        spread = jnp.where(coarse, value, 0.0)
        first = spread.astype(BF)
        spread = spread - first.astype(F32)
        second = spread.astype(BF)
        third = (spread - second.astype(F32)).astype(BF)
        for piece in (third, second, first):
            sums += lax.dot_general(piece, fine, ACROSS, preferred_element_type=F32)
    sums = sums * (NB / (KZ * NY))
    for copy in range(sums_ref.shape[0]):
        sums_ref[copy] = sums


def on_device(field_b, density, level_y, level_z, bins):
    y_local, z_local = field_b.shape[2], field_b.shape[3]

    def shift(cells, axis, step):
        count = lax.axis_size(axis)
        return lax.ppermute(cells, axis, [(i, (i + step) % count) for i in range(count)])

    ylo = shift(field_b[0::2, :, y_local - 1, :].reshape(4, z_local), GY, 1)
    yhi = shift(field_b[0::2, :, 0, :].reshape(4, z_local), GY, -1)
    half = lax.dynamic_index_in_dim(jnp.asarray(z_table()), lax.axis_index("xh"), keepdims=False)
    half, ylo, yhi = lax.optimization_barrier((half, ylo, yhi))
    small = pltpu.CompilerParams(vmem_limit_bytes=16 * 2**20)
    far = [
        pltpu.with_memory_space_constraint(x, pltpu.HBM)
        for x in (level_y[None, :], level_z[None, :], field_b, density)
    ]
    scratch = [
        pltpu.VMEM((1, y_local), jnp.int32),
        pltpu.VMEM((1, z_local), jnp.int32),
        pltpu.VMEM(field_b.shape, F32),
        pltpu.VMEM(density.shape, F32),
        pltpu.SemaphoreType.DMA((4,)),
    ]
    message, held, inside = pl.pallas_call(
        message_kernel,
        out_shape=(
            jax.ShapeDtypeStruct((16, 64, z_local), BF),
            jax.ShapeDtypeStruct((y_local, z_local), F32),
            jax.ShapeDtypeStruct(field_b.shape, BF),
        ),
        in_specs=[pl.BlockSpec(memory_space=pltpu.HBM)] * 4 + [pl.BlockSpec(memory_space=pltpu.VMEM)] * 2,
        scratch_shapes=scratch,
        compiler_params=small,
    )(*far, ylo, yhi)
    lines = lax.all_to_all(message, GZ, 0, 0, tiled=True)
    z_modes, emf = pl.pallas_call(
        z_kernel,
        out_shape=(jax.ShapeDtypeStruct((512, 128), BF), jax.ShapeDtypeStruct(field_b.shape, BF)),
        scratch_shapes=[pltpu.VMEM((512, 128), F32)],
        compiler_params=small,
    )(lines, half, held, inside)
    spread = lax.all_to_all(z_modes.reshape(256, 2, 128), ("yh", "yl") + GY, 0, 0, tiled=True).reshape(512, 128)
    first = ("yh", "yl", "c")
    second = ("xh", "z", "xl")
    mode_power, sums = pl.pallas_call(
        y_kernel,
        out_shape=(
            jax.ShapeDtypeStruct((2, NY), F32),
            jax.ShapeDtypeStruct((lax.axis_size(first), 8, 128), F32),
        ),
        compiler_params=small,
    )(spread, *y_tables(), bins)
    sums = jnp.sum(lax.all_to_all(sums, first, 0, 0, tiled=True), axis=0)
    copies = jnp.broadcast_to(sums[None], (lax.axis_size(second), 8, 128))
    spectrum = jnp.sum(lax.all_to_all(copies, second, 0, 0, tiled=True), axis=0).reshape(NB)
    return (emf, mode_power, spectrum)


def solution(mesh):
    fine = Mesh(mesh.devices.reshape(4, 2, 2, 8, 2, 2), GZ + GY)
    placed = (
        P(None, None, GY, GZ),
        P(None, GY, GZ),
        P(GY),
        P(GZ),
        P(GZ + GY, None),
    )
    return jax.shard_map(
        on_device,
        mesh=fine,
        in_specs=placed,
        out_specs=(P(None, None, GY, GZ), P(GZ + GY, None), P()),
        check_vma=False,
    )
```

time: 98.6 us -> 92.1 us (0.934)
  blocking collectives: 43.6 us -> 72.1 us
  waiting for transfers between devices: 21.6 us -> 0.01 us
  starting transfers between devices: 21.6 us -> 10.7 us
  Pallas kernels: 7.39 us -> 5.41 us
    all_to_all x1 -> x3, blocking collectives: 32 us -> 60.5 us  [the longest x1 29.9 us: on_device(): lax.all_to_all(z_modes.reshape(256, 2, 128), ('yh', 'yl') + GY, 0, 0, til...]
    all_to_all x2 -> x0, waiting for transfers between devices: 20.8 us -> none  [the longest x1 12.3 us: on_device(): lines = lax.all_to_all(message, GZ, 0, 0, tiled=True)]
    all_to_all x2 -> x0, starting transfers between devices: 10.9 us -> none  [the longest x1 7.01 us: on_device(): lines = lax.all_to_all(message, GZ, 0, 0, tiled=True)]
    pallas_call x3 -> x2, Pallas kernels: 5.99 us -> 3.93 us  [the longest x1 2.35 us: on_device(): pl.pallas_call(z_kernel, out_shape=(jax.ShapeDtypeStruct((512, 128), BF),...]
  transfers between devices with their start and end apart: 4 -> 2, of which waited for: 3 -> 0; matrix products, arithmetic and copies ran while one was open for 1% -> 1% of each run, Pallas kernels for 2% -> 0%
where the time goes in v5:
time: 92.1 us; the launch traced here: 91.7 us
  blocking collectives  72.1 us (78%)
  starting transfers between devices  10.7 us (12%)
  Pallas kernels  5.41 us (6%)
  local copies, waits for them, and re-layouts  2.14 us (2%)
    all_to_all x1, blocking collectives, on_device(): lax.all_to_all(z_modes.reshape(256, 2, 128), ('yh', 'yl') + GY, 0, 0, til...  29.9 us
    all_to_all x1, blocking collectives, on_device(): lines = lax.all_to_all(message, GZ, 0, 0, tiled=True)  17.3 us
    all_to_all x1, blocking collectives, on_device(): lax.all_to_all(copies, second, 0, 0, tiled=True)  13.4 us
    all_to_all x1, blocking collectives, on_device(): sums = jnp.sum(lax.all_to_all(sums, first, 0, 0, tiled=True), axis=0)  11.5 us
    ppermute x2, starting transfers between devices, shift(): lax.ppermute(cells, axis, [(i, (i + step) % count) for i in range(count)])  10.7 us
    pallas_call x1, Pallas kernels, on_device(): pl.pallas_call(z_kernel, out_shape=(jax.ShapeDtypeStruct((512, 128), BF),...  2.35 us
  transfers between devices with their start and end apart: 2, of which 0 were waited for; matrix products, arithmetic and copies ran while one was open for 1% of the time, Pallas kernels for 0%

profile of v5, /device:TPU:1, one launch (start us, length us, event | category | flops | bytes accessed | tf_op | source)
XLA Modules:
  0.0 91.7 jit_solution(15973191194492568636)
XLA Ops:
  0.6 0.7 fusion
  1.4 4.5 %collective-permute-start = (f32[4,128]{1,0:T(4,128)S(1)}, f32[4,128]{1,0:T(4,128)S(1)}, u32[]{:S(2)}, u32[]{:S(2)}) collective-permute-start(f32[4,128]{1,0:T(4,128)S(1)} %bitcast.13), channel_id=1, source_target_pairs={{0,1},{1,2},{2,3},{3,4},{4,5},{5,6},{6,7},{7,8},{8,9},{9,10},{10,1... | collective-permute-start | bytes 6152 | tf_op jit(solution)/shard_map/ppermute | solution.py:295
  5.9 6.2 %collective-permute-start.1 = (f32[4,128]{1,0:T(4,128)S(1)}, f32[4,128]{1,0:T(4,128)S(1)}, u32[]{:S(2)}, u32[]{:S(2)}) collective-permute-start(f32[4,128]{1,0:T(4,128)S(1)} %bitcast.12), channel_id=1, source_target_pairs={{0,31},{1,0},{2,1},{3,2},{4,3},{5,4},{6,5},{7,6},{8,7},{9,8},{10,9... | collective-permute-start | bytes 6152 | tf_op jit(solution)/shard_map/ppermute | solution.py:295
  12.1 0.0 copy-start
  12.1 0.0 copy-start.1
  12.1 0.0 copy-start.2
  12.1 0.0 copy-start.3
  12.1 1.4 %dynamic-slice_bitcast_fusion.table_ref = bf16[8,512,128]{2,1,0:T(8,128)(2,1)S(1)} fusion(bf16[2,8,512,128]{3,2,1,0:T(8,128)(2,1)} %constant.22.clone, s32[]{:T(128)S(6)} %select_n.4), kind=kLoop, calls=%fused_computation | loop fusion | bytes 2097156 | tf_op jit(solution)/shard_map/jit(dynamic_index_in_dim)/squeeze | solution.py:299
  13.5 0.0 collective-permute-done.refs_4_
  13.5 0.0 collective-permute-done.1.refs_5_
  13.5 1.6 %shard_map.112 = (bf16[16,64,128]{2,1,0:T(8,128)(2,1)S(1)}, f32[64,128]{1,0:T(8,128)S(1)}, bf16[3,2,64,128]{3,2,1,0:T(8,128)(2,1)S(1)}) custom-call(s32[1,64]{1,0:T(1,128)} %bitcast.14, s32[1,128]{1,0:T(1,128)} %bitcast.15, f32[3,2,64,128]{3,2,1,0:T(8,128)} %refs_2_.1, f32[2,64,128]{2,1,0:T(8,128)} %refs_3_.1, f32[4,128]{1,0:T(4,128)S(1)} %collective-permute-done.refs_4_, ...), custom_call_target="tpu_custom_call" | custom-call | tf_op jit(solution)/shard_map/pallas_call | solution.py:313
  15.1 17.3 %all_to_all.20.x_ref = bf16[16,64,128]{2,1,0:T(8,128)(2,1)S(1)} all-to-all(bf16[16,64,128]{2,1,0:T(8,128)(2,1)S(1)} %get-tuple-element.15), channel_id=1, replica_groups=mesh['yh'=4,'yl'=2,'xh'=2,'z'=8,'xl'=2,'c'=2] {'yh','yl','xh'}, dimensions={0} | all-to-all | bytes 524288 | tf_op jit(solution)/shard_map/all_to_all | solution.py:324
  32.4 2.3 %shard_map.113 = (bf16[512,128]{1,0:T(8,128)(2,1)S(1)}, bf16[3,2,64,128]{3,2,1,0:T(8,128)(2,1)}) custom-call(bf16[16,64,128]{2,1,0:T(8,128)(2,1)S(1)} %all_to_all.20.x_ref, bf16[8,512,128]{2,1,0:T(8,128)(2,1)S(1)} %dynamic-slice_bitcast_fusion.table_ref, f32[64,128]{1,0:T(8,128)S(1)} %get-tuple-element.17.held_ref, ...), custom_call_target="tpu_custom_call" | custom-call | tf_op jit(solution)/shard_map/pallas_call | solution.py:325
  34.7 29.9 %all_to_all.21 = bf16[256,2,128]{2,1,0:T(2,128)(2,1)S(1)} all-to-all(bf16[256,2,128]{2,1,0:T(2,128)(2,1)S(1)} %bitcast.10), channel_id=1, replica_groups=mesh['yh'=4,'yl'=2,'xh'=2,'z'=8,'xl'=2,'c'=2] {'yh','yl','z','xl','c'}, dimensions={0} | all-to-all | bytes 262144 | tf_op jit(solution)/shard_map/all_to_all | solution.py:331
  64.6 0.0 copy-done
  64.6 0.0 copy-done.1
  64.6 0.0 copy-done.2
  64.6 0.0 copy-done.3
  64.6 1.5 %shard_map.114 = (f32[2,2048]{1,0:T(2,128)}, f32[16,8,128]{2,1,0:T(8,128)S(1)}) custom-call(bf16[512,128]{1,0:T(8,128)(2,1)S(1)} %bitcast.9, bf16[512,512]{1,0:T(8,128)(2,1)S(1)} %copy-done, f32[2,8,256]{2,1,0:T(8,128)S(1)} %copy-done.3, bf16[128,128]{1,0:T(8,128)(2,1)S(1)} %copy-done.1, s32[2,2048]{1,0:T(2,128)S(1)} %copy-done.2), custom_call_target="tpu_custom_call" | custom-call | tf_op jit(solution)/shard_map/pallas_call | solution.py:334
  66.1 11.5 %all_to_all.22 = f32[16,8,128]{2,1,0:T(8,128)S(1)} all-to-all(f32[16,8,128]{2,1,0:T(8,128)S(1)} %get-tuple-element.22), channel_id=1, replica_groups=mesh['yh'=4,'yl'=2,'xh'=2,'z'=8,'xl'=2,'c'=2] {'yh','yl','c'}, dimensions={0} | all-to-all | bytes 131072 | tf_op jit(solution)/shard_map/all_to_all | solution.py:342
  77.7 13.4 %all_to_all.23 = f32[32,8,128]{2,1,0:T(8,128)S(1)} all-to-all(f32[32,8,128]{2,1,0:T(8,128)S(1)} %broadcast_in_dim.14), channel_id=1, replica_groups=mesh['yh'=4,'yl'=2,'xh'=2,'z'=8,'xl'=2,'c'=2] {'xh','z','xl'}, dimensions={0} | all-to-all | bytes 262144 | tf_op jit(solution)/shard_map/all_to_all | solution.py:344
  91.0 0.6 reduce_sum.19
  (2 shorter events, 0.0 us)
Async XLA Ops:
  1.4 12.1 %collective-permute-start = (f32[4,128]{1,0:T(4,128)S(1)}, f32[4,128]{1,0:T(4,128)S(1)}, u32[]{:S(2)}, u32[]{:S(2)}) collective-permute-start(f32[4,128]{1,0:T(4,128)S(1)} %bitcast.13), channel_id=1, source_target_pairs={{0,1},{1,2},{2,3},{3,4},{4,5},{5,6},{6,7},{7,8},{8,9},{9,10},{10,1... | collective-permute-start | bytes 6152 | tf_op jit(solution)/shard_map/ppermute | solution.py:295
  5.9 7.6 %collective-permute-start.1 = (f32[4,128]{1,0:T(4,128)S(1)}, f32[4,128]{1,0:T(4,128)S(1)}, u32[]{:S(2)}, u32[]{:S(2)}) collective-permute-start(f32[4,128]{1,0:T(4,128)S(1)} %bitcast.12), channel_id=1, source_target_pairs={{0,31},{1,0},{2,1},{3,2},{4,3},{5,4},{6,5},{7,6},{8,7},{9,8},{10,9... | collective-permute-start | bytes 6152 | tf_op jit(solution)/shard_map/ppermute | solution.py:295
  12.1 52.5 %copy-start = (bf16[512,512]{1,0:T(8,128)(2,1)S(1)}, bf16[512,512]{1,0:T(8,128)(2,1)}, u32[]{:S(2)}) copy-start(bf16[512,512]{1,0:T(8,128)(2,1)} %constant.23.clone.table_ref) | copy-start | bytes 1572868
  12.1 52.5 %copy-start.1 = (bf16[128,128]{1,0:T(8,128)(2,1)S(1)}, bf16[128,128]{1,0:T(8,128)(2,1)}, u32[]{:S(2)}) copy-start(bf16[128,128]{1,0:T(8,128)(2,1)} %constant.25.clone.order_ref) | copy-start | bytes 98308
  12.1 52.5 %copy-start.2 = (s32[2,2048]{1,0:T(2,128)S(1)}, s32[2,2048]{1,0:T(2,128)}, u32[]{:S(2)}) copy-start(s32[2,2048]{1,0:T(2,128)} %bins_ref.1) | copy-start | bytes 49156
  12.1 52.5 %copy-start.3 = (f32[2,8,256]{2,1,0:T(8,128)S(1)}, f32[2,8,256]{2,1,0:T(8,128)}, u32[]{:S(2)}) copy-start(f32[2,8,256]{2,1,0:T(8,128)} %constant.24.clone.turn_ref) | copy-start | bytes 49156

commit v6 on v5

--- a/solution.py
+++ b/solution.py
@@ -188,25 +188,36 @@
 
 def z_kernel(x_ref, table_ref, held_ref, inside_ref, out_ref, emf_ref, mix_ref):
     edges = line_edges(x_ref)
-    zero = jnp.zeros((80, 512), BF)
+    zero = jnp.zeros((16, 512), BF)
     total = None
-    for n in range(4):
-        lines = []
+    for n in range(2):
+        sums, gaps = [], []
         for i in range(4 * n, 4 * n + 4):
-            tiles = [x_ref[i, 16 * c : 16 * c + 16, :] + edges[c][16 * i : 16 * i + 16] for c in range(3)]
-            lines.append(jnp.concatenate(tiles, axis=0))
-        lines = jnp.concatenate([jnp.concatenate(lines, axis=1), zero], axis=0)
+            for side, pair in ((sums, 1), (gaps, -1)):
+                tiles = []
+                for c in range(3):
+                    near, far = (
+                        x_ref[m, 16 * c : 16 * c + 16, :] + edges[c][16 * m : 16 * m + 16] for m in (i, i + 8)
+                    )
+                    tiles.append(near + far if pair > 0 else near - far)
+                side.append(jnp.concatenate(tiles, axis=0))
+        sums, gaps = (jnp.concatenate([jnp.concatenate(x, axis=1), zero], axis=0) for x in (sums, gaps))
+        empty = jnp.zeros((64, 512), BF)
+        lines = jnp.concatenate(
+            [jnp.concatenate([sums, empty], axis=0), jnp.concatenate([empty, gaps], axis=0)], axis=1
+        )
         blocks = []
-        for e in range(2):
-            for c in range(2):
-                for jl in range(8):
-                    kappa = 2 * jl + e
-                    turns = [(kappa * i + 4 * c) % 16 for i in range(4 * n, 4 * n + 4)]
-                    cells = [table_ref[m % 8, 32 * kappa : 32 * kappa + 32, :] for m in turns]
-                    blocks.append(jnp.concatenate([-x if m >= 8 else x for m, x in zip(turns, cells)], axis=1))
+        for c in range(2):
+            for jl in range(8):
+                row = []
+                for kappa in (2 * jl, 2 * jl + 1):
+                    for i in range(4 * n, 4 * n + 4):
+                        m = (kappa * i + 4 * c) % 16
+                        cell = table_ref[m % 8, 32 * kappa : 32 * kappa + 32, :]
+                        row.append(-cell if m >= 8 else cell)
+                blocks.append(jnp.concatenate(row, axis=1))
         product = lax.dot_general(jnp.concatenate(blocks, axis=0), lines, ACROSS, preferred_element_type=F32)
         total = product if n == 0 else total + product
-    total = total[0:512] + roll(total[512:1024], 64, 1)
     for c in range(2):
         for jl in range(8):
             at = 32 * (8 * c + jl)
@@ -269,19 +280,25 @@
             power_ref[e : e + 1, 256 * q1 : 256 * q1 + 256] = (
                 jnp.sum(a * a + b * b, axis=0, keepdims=True) * scale
             )
-    sums = jnp.zeros((8, 128), F32)
+    sums = jnp.zeros((32, 128), F32)
+    steps = lax.broadcasted_iota(jnp.int32, (128, 128), 0).astype(F32).astype(BF)
+    one, none = jnp.ones((128, 128), BF), jnp.zeros((128, 128), BF)
     for e in range(2):
         value = power_ref[e : e + 1, :]
         bins = bins_ref[e : e + 1, :]
         coarse = lax.broadcasted_iota(jnp.int32, (8, NY), 0) == (bins >> 7)
-        fine = (lax.broadcasted_iota(jnp.int32, (128, NY), 0) == (bins & 127)).astype(F32).astype(BF)
+        within = jnp.broadcast_to((bins & 127).astype(F32), (16, NY)).astype(BF)
+        fine = []
+        for n in range(NY // 128):
+            tile = within[:, 128 * n : 128 * n + 128]
+            fine.append(jnp.where(steps == jnp.concatenate([tile] * 8, axis=0), one, none))
         spread = jnp.where(coarse, value, 0.0)
-        first = spread.astype(BF)
-        spread = spread - first.astype(F32)
-        second = spread.astype(BF)
-        third = (spread - second.astype(F32)).astype(BF)
-        for piece in (third, second, first):
-            sums += lax.dot_general(piece, fine, ACROSS, preferred_element_type=F32)
+        first = spread.astype(BF).astype(F32)
+        second = (spread - first).astype(BF).astype(F32)
+        third = spread - first - second
+        pieces = jnp.concatenate([third, second, first, jnp.zeros_like(first)], axis=0).astype(BF)
+        sums += lax.dot_general(pieces, jnp.concatenate(fine, axis=1), ACROSS, preferred_element_type=F32)
+    sums = sums[0:8] + sums[8:16] + sums[16:24]
     sums = sums * (NB / (KZ * NY))
     for copy in range(sums_ref.shape[0]):
         sums_ref[copy] = sums
@@ -340,8 +357,8 @@
         compiler_params=small,
     )(spread, *y_tables(), bins)
     sums = jnp.sum(lax.all_to_all(sums, first, 0, 0, tiled=True), axis=0)
-    copies = jnp.broadcast_to(sums[None], (lax.axis_size(second), 8, 128))
-    spectrum = jnp.sum(lax.all_to_all(copies, second, 0, 0, tiled=True), axis=0).reshape(NB)
+    copies = jnp.broadcast_to(sums.astype(BF)[None], (lax.axis_size(second), 8, 128))
+    spectrum = jnp.sum(lax.all_to_all(copies, second, 0, 0, tiled=True).astype(F32), axis=0).reshape(NB)
     return (emf, mode_power, spectrum)
 
 

time: 92.1 us -> 90.2 us (0.979)
  blocking collectives: 72.1 us -> 70.9 us
    all_to_all x1, blocking collectives: 13.4 us -> 12.2 us  [on_device(): lax.all_to_all(copies, second, 0, 0, tiled=True).astype(F32)]
  transfers between devices with their start and end apart: 2 -> 2, of which waited for: 0 -> 0; matrix products, arithmetic and copies ran while one was open for 1% -> 2% of each run, Pallas kernels for 0% -> 0%
where the time goes in v6:
time: 90.2 us; the launch traced here: 89.8 us
  blocking collectives  70.9 us (79%)
  starting transfers between devices  10.7 us (12%)
  Pallas kernels  4.7 us (5%)
  local copies, waits for them, and re-layouts  2.14 us (2%)
    all_to_all x1, blocking collectives, on_device(): lax.all_to_all(z_modes.reshape(256, 2, 128), ('yh', 'yl') + GY, 0, 0, til...  29.9 us
    all_to_all x1, blocking collectives, on_device(): lines = lax.all_to_all(message, GZ, 0, 0, tiled=True)  17.3 us
    all_to_all x1, blocking collectives, on_device(): lax.all_to_all(copies, second, 0, 0, tiled=True).astype(F32)  12.2 us
    all_to_all x1, blocking collectives, on_device(): sums = jnp.sum(lax.all_to_all(sums, first, 0, 0, tiled=True), axis=0)  11.5 us
    ppermute x2, starting transfers between devices, shift(): lax.ppermute(cells, axis, [(i, (i + step) % count) for i in range(count)])  10.7 us
    pallas_call x1, Pallas kernels, on_device(): pl.pallas_call(z_kernel, out_shape=(jax.ShapeDtypeStruct((512, 128), BF),...  1.81 us
  transfers between devices with their start and end apart: 2, of which 0 were waited for; matrix products, arithmetic and copies ran while one was open for 2% of the time, Pallas kernels for 0%

profile of v6, /device:TPU:1, one launch (start us, length us, event | category | flops | bytes accessed | tf_op | source)
XLA Modules:
  0.0 89.8 jit_solution(12137123908403048644)
XLA Ops:
  0.6 0.7 fusion
  1.4 4.5 %collective-permute-start = (f32[4,128]{1,0:T(4,128)S(1)}, f32[4,128]{1,0:T(4,128)S(1)}, u32[]{:S(2)}, u32[]{:S(2)}) collective-permute-start(f32[4,128]{1,0:T(4,128)S(1)} %bitcast.13), channel_id=1, source_target_pairs={{0,1},{1,2},{2,3},{3,4},{4,5},{5,6},{6,7},{7,8},{8,9},{9,10},{10,1... | collective-permute-start | bytes 6152 | tf_op jit(solution)/shard_map/ppermute | solution.py:312
  5.9 6.2 %collective-permute-start.1 = (f32[4,128]{1,0:T(4,128)S(1)}, f32[4,128]{1,0:T(4,128)S(1)}, u32[]{:S(2)}, u32[]{:S(2)}) collective-permute-start(f32[4,128]{1,0:T(4,128)S(1)} %bitcast.12), channel_id=1, source_target_pairs={{0,31},{1,0},{2,1},{3,2},{4,3},{5,4},{6,5},{7,6},{8,7},{9,8},{10,9... | collective-permute-start | bytes 6152 | tf_op jit(solution)/shard_map/ppermute | solution.py:312
  12.1 0.0 copy-start
  12.1 0.0 copy-start.1
  12.1 0.0 copy-start.2
  12.1 0.0 copy-start.3
  12.1 1.4 %dynamic-slice_bitcast_fusion.table_ref = bf16[8,512,128]{2,1,0:T(8,128)(2,1)S(1)} fusion(bf16[2,8,512,128]{3,2,1,0:T(8,128)(2,1)} %constant.22.clone, s32[]{:T(128)S(6)} %select_n.4), kind=kLoop, calls=%fused_computation | loop fusion | bytes 2097156 | tf_op jit(solution)/shard_map/jit(dynamic_index_in_dim)/squeeze | solution.py:316
  13.5 0.0 collective-permute-done.refs_4_
  13.5 0.0 collective-permute-done.1.refs_5_
  13.5 1.6 %shard_map.112 = (bf16[16,64,128]{2,1,0:T(8,128)(2,1)S(1)}, f32[64,128]{1,0:T(8,128)S(1)}, bf16[3,2,64,128]{3,2,1,0:T(8,128)(2,1)S(1)}) custom-call(s32[1,64]{1,0:T(1,128)} %bitcast.14, s32[1,128]{1,0:T(1,128)} %bitcast.15, f32[3,2,64,128]{3,2,1,0:T(8,128)} %refs_2_.1, f32[2,64,128]{2,1,0:T(8,128)} %refs_3_.1, f32[4,128]{1,0:T(4,128)S(1)} %collective-permute-done.refs_4_, ...), custom_call_target="tpu_custom_call" | custom-call | tf_op jit(solution)/shard_map/pallas_call | solution.py:330
  15.1 17.3 %all_to_all.20.x_ref = bf16[16,64,128]{2,1,0:T(8,128)(2,1)S(1)} all-to-all(bf16[16,64,128]{2,1,0:T(8,128)(2,1)S(1)} %get-tuple-element.15), channel_id=1, replica_groups=mesh['yh'=4,'yl'=2,'xh'=2,'z'=8,'xl'=2,'c'=2] {'yh','yl','xh'}, dimensions={0} | all-to-all | bytes 524288 | tf_op jit(solution)/shard_map/all_to_all | solution.py:341
  32.4 1.8 %shard_map.113 = (bf16[512,128]{1,0:T(8,128)(2,1)S(1)}, bf16[3,2,64,128]{3,2,1,0:T(8,128)(2,1)}) custom-call(bf16[16,64,128]{2,1,0:T(8,128)(2,1)S(1)} %all_to_all.20.x_ref, bf16[8,512,128]{2,1,0:T(8,128)(2,1)S(1)} %dynamic-slice_bitcast_fusion.table_ref, f32[64,128]{1,0:T(8,128)S(1)} %get-tuple-element.17.held_ref, ...), custom_call_target="tpu_custom_call" | custom-call | tf_op jit(solution)/shard_map/pallas_call | solution.py:342
  34.2 29.9 %all_to_all.21 = bf16[256,2,128]{2,1,0:T(2,128)(2,1)S(1)} all-to-all(bf16[256,2,128]{2,1,0:T(2,128)(2,1)S(1)} %bitcast.10), channel_id=1, replica_groups=mesh['yh'=4,'yl'=2,'xh'=2,'z'=8,'xl'=2,'c'=2] {'yh','yl','z','xl','c'}, dimensions={0} | all-to-all | bytes 262144 | tf_op jit(solution)/shard_map/all_to_all | solution.py:348
  64.1 0.0 copy-done
  64.1 0.0 copy-done.1
  64.1 0.0 copy-done.2
  64.1 0.0 copy-done.3
  64.1 1.3 %shard_map.114 = (f32[2,2048]{1,0:T(2,128)}, f32[16,8,128]{2,1,0:T(8,128)S(1)}) custom-call(bf16[512,128]{1,0:T(8,128)(2,1)S(1)} %bitcast.9, bf16[512,512]{1,0:T(8,128)(2,1)S(1)} %copy-done, f32[2,8,256]{2,1,0:T(8,128)S(1)} %copy-done.3, bf16[128,128]{1,0:T(8,128)(2,1)S(1)} %copy-done.1, s32[2,2048]{1,0:T(2,128)S(1)} %copy-done.2), custom_call_target="tpu_custom_call" | custom-call | tf_op jit(solution)/shard_map/pallas_call | solution.py:351
  65.4 11.5 %all_to_all.22 = f32[16,8,128]{2,1,0:T(8,128)S(1)} all-to-all(f32[16,8,128]{2,1,0:T(8,128)S(1)} %get-tuple-element.22), channel_id=1, replica_groups=mesh['yh'=4,'yl'=2,'xh'=2,'z'=8,'xl'=2,'c'=2] {'yh','yl','c'}, dimensions={0} | all-to-all | bytes 131072 | tf_op jit(solution)/shard_map/all_to_all | solution.py:359
  76.9 12.2 %all_to_all.23 = bf16[32,8,128]{2,1,0:T(8,128)(2,1)S(1)} all-to-all(bf16[32,8,128]{2,1,0:T(8,128)(2,1)S(1)} %broadcast_in_dim.14), channel_id=1, replica_groups=mesh['yh'=4,'yl'=2,'xh'=2,'z'=8,'xl'=2,'c'=2] {'xh','z','xl'}, dimensions={0} | all-to-all | bytes 131072 | tf_op jit(solution)/shard_map/all_to_all | solution.py:361
  89.2 0.6 convert_reduce_fusion
  (2 shorter events, 0.0 us)
Async XLA Ops:
  1.4 12.1 %collective-permute-start = (f32[4,128]{1,0:T(4,128)S(1)}, f32[4,128]{1,0:T(4,128)S(1)}, u32[]{:S(2)}, u32[]{:S(2)}) collective-permute-start(f32[4,128]{1,0:T(4,128)S(1)} %bitcast.13), channel_id=1, source_target_pairs={{0,1},{1,2},{2,3},{3,4},{4,5},{5,6},{6,7},{7,8},{8,9},{9,10},{10,1... | collective-permute-start | bytes 6152 | tf_op jit(solution)/shard_map/ppermute | solution.py:312
  5.9 7.6 %collective-permute-start.1 = (f32[4,128]{1,0:T(4,128)S(1)}, f32[4,128]{1,0:T(4,128)S(1)}, u32[]{:S(2)}, u32[]{:S(2)}) collective-permute-start(f32[4,128]{1,0:T(4,128)S(1)} %bitcast.12), channel_id=1, source_target_pairs={{0,31},{1,0},{2,1},{3,2},{4,3},{5,4},{6,5},{7,6},{8,7},{9,8},{10,9... | collective-permute-start | bytes 6152 | tf_op jit(solution)/shard_map/ppermute | solution.py:312
  12.1 52.0 %copy-start = (bf16[512,512]{1,0:T(8,128)(2,1)S(1)}, bf16[512,512]{1,0:T(8,128)(2,1)}, u32[]{:S(2)}) copy-start(bf16[512,512]{1,0:T(8,128)(2,1)} %constant.23.clone.table_ref) | copy-start | bytes 1572868
  12.1 52.0 %copy-start.1 = (bf16[128,128]{1,0:T(8,128)(2,1)S(1)}, bf16[128,128]{1,0:T(8,128)(2,1)}, u32[]{:S(2)}) copy-start(bf16[128,128]{1,0:T(8,128)(2,1)} %constant.25.clone.order_ref) | copy-start | bytes 98308
  12.1 52.0 %copy-start.2 = (s32[2,2048]{1,0:T(2,128)S(1)}, s32[2,2048]{1,0:T(2,128)}, u32[]{:S(2)}) copy-start(s32[2,2048]{1,0:T(2,128)} %bins_ref.1) | copy-start | bytes 49156
  12.1 52.0 %copy-start.3 = (f32[2,8,256]{2,1,0:T(8,128)S(1)}, f32[2,8,256]{2,1,0:T(8,128)}, u32[]{:S(2)}) copy-start(f32[2,8,256]{2,1,0:T(8,128)} %constant.24.clone.turn_ref) | copy-start | bytes 49156

commit v7 on v6

--- a/solution.py
+++ b/solution.py
@@ -55,26 +55,22 @@
     return pltpu.roll(x, by % x.shape[axis], axis)
 
 
-def hall(p, fb, den, my, mz, ylo_ref, yhi_ref, zlo, zhi):
+def hall(p, fb, den, my, mz):
     rows, lanes = fb.shape[2], fb.shape[3]
     row = lax.broadcasted_iota(jnp.int32, (rows, lanes), 0)
     lane = lax.broadcasted_iota(jnp.int32, (rows, lanes), 1)
 
-    def d_y(f, at):
-        up = jnp.where(row == rows - 1, yhi_ref[at : at + 1, :], roll(f, -1, 0))
-        down = jnp.where(row == 0, ylo_ref[at : at + 1, :], roll(f, 1, 0))
-        return (up - down) * my
-
-    def d_z(f, at):
-        up = jnp.where(lane == lanes - 1, zhi[at], roll(f, -1, 1))
-        down = jnp.where(lane == 0, zlo[at], roll(f, 1, 1))
-        return (up - down) * mz
+    def d_y(f):
+        return (jnp.where(row == rows - 1, 0.0, roll(f, -1, 0)) - jnp.where(row == 0, 0.0, roll(f, 1, 0))) * my
+
+    def d_z(f):
+        return (jnp.where(lane == lanes - 1, 0.0, roll(f, -1, 1)) - jnp.where(lane == 0, 0.0, roll(f, 1, 1))) * mz
 
     b_x, b_y, b_z = fb[0, p], fb[1, p], fb[2, p]
     half = 0.5 if p == 0 else -0.5
-    cur_x = d_y(b_z, 2 + p) - d_z(b_y, 2 + p)
-    cur_y = d_z(b_x, p) - half * fb[2, 1 - p]
-    cur_z = half * fb[1, 1 - p] - d_y(b_x, p)
+    cur_x = d_y(b_z) - d_z(b_y)
+    cur_y = d_z(b_x) - half * fb[2, 1 - p]
+    cur_z = half * fb[1, 1 - p] - d_y(b_x)
     dens = den[p]
     return (
         (cur_y * b_z - cur_z * b_y) / dens,
@@ -97,7 +93,7 @@
 
 
 def message_kernel(*refs):
-    far, (ylo_ref, yhi_ref, msg_ref, held_ref, emf_ref), near, sems = refs[0:4], refs[4:9], refs[9:13], refs[13]
+    far, (msg_ref, held_ref, emf_ref, tips_ref, weights_ref), near, sems = refs[0:4], refs[4:9], refs[9:13], refs[13]
     fetched(far, near, sems)
     ly_ref, lz_ref, fb, den = near
     shape = fb.shape[2:]
@@ -106,12 +102,18 @@
     edge = (lane == 0) | (lane == 127)
     slot = lane >> 1
     signed = jnp.where(lane == 0, -mz, mz)
-    none = [0.0] * 4
     inside, held = [], []
     own = jnp.zeros(shape, F32)
     for p in range(2):
-        parts = hall(p, fb, den, my, mz, ylo_ref, yhi_ref, none, none)
-        weight = signed / den[p]
+        parts = hall(p, fb, den, my, mz)
+        inverse = 1.0 / den[p]
+        weight = signed * inverse
+        for side, sign in ((0, -1.0), (1, 1.0)):
+            at = side * (shape[0] - 1)
+            upward = sign * my[at : at + 1] * inverse[at : at + 1]
+            for comp in range(3):
+                tips_ref[side, 2 * comp + p] = parts[comp][56 * side : 56 * side + 8]
+                weights_ref[side, 3 * p + comp : 3 * p + comp + 1, :] = upward * fb[comp, p, at : at + 1, :]
         fields = [fb[comp, p] for comp in range(3)]
         inside.append([jnp.where(edge, 0.0, part) for part in parts])
         terms = list(parts) + [f * weight for f in fields] + fields[0:2]
@@ -142,6 +144,47 @@
         for n, value in enumerate(values):
             for copy in range(2):
                 msg_ref[2 * block + copy, 16 * n : 16 * n + 16, :] = value.astype(BF)
+
+
+def rim_kernel(
+    ylo_ref, yhi_ref, msg_ref, held_ref, emf_ref, tips_ref, weights_ref, msg_out, held_out, emf_out
+):
+    msg_out[...] = msg_ref[...]
+    held_out[...] = held_ref[...]
+    emf_out[...] = emf_ref[...]
+    shape = (8, emf_ref.shape[3])
+    row = lax.broadcasted_iota(jnp.int32, shape, 0)
+    lane = lax.broadcasted_iota(jnp.int32, shape, 1)
+    inner = (lane > 0) & (lane < 127)
+    slot = lane >> 1
+    for side, rim_ref in ((0, ylo_ref), (1, yhi_ref)):
+        block = 7 * side
+        rows = slice(8 * block, 8 * block + 8)
+        held = held_ref[rows, :]
+        values = []
+        for p in range(2):
+            f_x, f_z = rim_ref[p : p + 1, :], rim_ref[2 + p : 3 + p, :]
+            w_x, w_y, w_z = (weights_ref[side, 3 * p + comp : 3 * p + comp + 1, :] for comp in range(3))
+            extra = (f_x * w_y, -(f_x * w_x + f_z * w_z), f_z * w_y)
+            for comp in range(3):
+                change = jnp.where(row == 7 * side, extra[comp], 0.0)
+                value = jnp.where(inner, tips_ref[side, 2 * comp + p] + change, 0.0)
+                emf_out[comp, p, rows, :] = value.astype(BF)
+                values.append(value)
+                moved = roll(change, 16 * p + 2 * comp + 1, 1)
+                held = held + jnp.where(slot == 8 * p + comp, moved, 0.0)
+        held_out[rows, :] = held
+        tile = jnp.concatenate([held, roll(held, -16, 1)], axis=0)
+        wide = lax.broadcasted_iota(jnp.int32, tile.shape, 1)
+        tile = jnp.where(wide < 16, tile, 0.0)
+        high = tile.astype(BF).astype(F32)
+        low = (tile - high).astype(BF).astype(F32)
+        old = msg_ref[2 * block, 48:64, :].astype(F32)
+        tiles = [jnp.concatenate([values[comp], values[3 + comp]], axis=0) for comp in range(3)]
+        tiles.append(jnp.where(wide < 32, high + roll(low, 16, 1), old))
+        for n, value in enumerate(tiles):
+            for copy in range(2):
+                msg_out[2 * block + copy, 16 * n : 16 * n + 16, :] = value.astype(BF)
 
 
 def finished(held, beside):
@@ -327,17 +370,21 @@
         pltpu.VMEM(density.shape, F32),
         pltpu.SemaphoreType.DMA((4,)),
     ]
-    message, held, inside = pl.pallas_call(
+    made = (
+        jax.ShapeDtypeStruct((16, 64, z_local), BF),
+        jax.ShapeDtypeStruct((y_local, z_local), F32),
+        jax.ShapeDtypeStruct(field_b.shape, BF),
+    )
+    rims = (jax.ShapeDtypeStruct((2, 6, 8, z_local), F32), jax.ShapeDtypeStruct((2, 8, z_local), F32))
+    local = pl.pallas_call(
         message_kernel,
-        out_shape=(
-            jax.ShapeDtypeStruct((16, 64, z_local), BF),
-            jax.ShapeDtypeStruct((y_local, z_local), F32),
-            jax.ShapeDtypeStruct(field_b.shape, BF),
-        ),
-        in_specs=[pl.BlockSpec(memory_space=pltpu.HBM)] * 4 + [pl.BlockSpec(memory_space=pltpu.VMEM)] * 2,
+        out_shape=made + rims,
+        in_specs=[pl.BlockSpec(memory_space=pltpu.HBM)] * 4,
         scratch_shapes=scratch,
         compiler_params=small,
-    )(*far, ylo, yhi)
+        cost_estimate=pl.CostEstimate(flops=2_000_000, bytes_accessed=1_000_000, transcendentals=0),
+    )(*far)
+    message, held, inside = pl.pallas_call(rim_kernel, out_shape=made, compiler_params=small)(ylo, yhi, *local)
     lines = lax.all_to_all(message, GZ, 0, 0, tiled=True)
     z_modes, emf = pl.pallas_call(
         z_kernel,

time: 90.2 us -> 90.3 us (level)
    all_to_all x1, blocking collectives: 17.3 us -> 15.7 us  [on_device(): lines = lax.all_to_all(message, GZ, 0, 0, tiled=True)]
    all_to_all x1, blocking collectives: 29.9 us -> 31.2 us  [on_device(): lax.all_to_all(z_modes.reshape(256, 2, 128), ('yh', 'yl') + GY, 0, 0, til...]
    pallas_call x1 -> x2, Pallas kernels: 1.58 us -> 1.83 us  [the longest x1 1.59 us: on_device(): pl.pallas_call(message_kernel, out_shape=made + rims, in_specs=[pl.BlockS...]
  transfers between devices with their start and end apart: 2 -> 2, of which waited for: 0 -> 0; matrix products, arithmetic and copies ran while one was open for 2% -> 2% of each run, Pallas kernels for 0% -> 2%
where the time goes in v7:
time: 90.3 us; the launch traced here: 89.8 us
  blocking collectives  70.7 us (78%)
  starting transfers between devices  10.7 us (12%)
  Pallas kernels  4.95 us (5%)
  local copies, waits for them, and re-layouts  2.14 us (2%)
    all_to_all x1, blocking collectives, on_device(): lax.all_to_all(z_modes.reshape(256, 2, 128), ('yh', 'yl') + GY, 0, 0, til...  31.2 us
    all_to_all x1, blocking collectives, on_device(): lines = lax.all_to_all(message, GZ, 0, 0, tiled=True)  15.7 us
    all_to_all x1, blocking collectives, on_device(): lax.all_to_all(copies, second, 0, 0, tiled=True).astype(F32)  12.2 us
    all_to_all x1, blocking collectives, on_device(): sums = jnp.sum(lax.all_to_all(sums, first, 0, 0, tiled=True), axis=0)  11.5 us
    ppermute x2, starting transfers between devices, shift(): lax.ppermute(cells, axis, [(i, (i + step) % count) for i in range(count)])  10.7 us
    pallas_call x1, Pallas kernels, on_device(): pl.pallas_call(z_kernel, out_shape=(jax.ShapeDtypeStruct((512, 128), BF),...  1.82 us
  transfers between devices with their start and end apart: 2, of which 0 were waited for; matrix products, arithmetic and copies ran while one was open for 2% of the time, Pallas kernels for 2%

profile of v7, /device:TPU:1, one launch (start us, length us, event | category | flops | bytes accessed | tf_op | source)
XLA Modules:
  0.0 89.8 jit_solution(12205919811232734629)
XLA Ops:
  0.6 0.7 fusion
  1.4 4.5 %collective-permute-start = (f32[4,128]{1,0:T(4,128)S(1)}, f32[4,128]{1,0:T(4,128)S(1)}, u32[]{:S(2)}, u32[]{:S(2)}) collective-permute-start(f32[4,128]{1,0:T(4,128)S(1)} %bitcast.13), channel_id=1, source_target_pairs={{0,1},{1,2},{2,3},{3,4},{4,5},{5,6},{6,7},{7,8},{8,9},{9,10},{10,1... | collective-permute-start | bytes 6152 | tf_op jit(solution)/shard_map/ppermute | solution.py:355
  5.9 6.2 %collective-permute-start.1 = (f32[4,128]{1,0:T(4,128)S(1)}, f32[4,128]{1,0:T(4,128)S(1)}, u32[]{:S(2)}, u32[]{:S(2)}) collective-permute-start(f32[4,128]{1,0:T(4,128)S(1)} %bitcast.12), channel_id=1, source_target_pairs={{0,31},{1,0},{2,1},{3,2},{4,3},{5,4},{6,5},{7,6},{8,7},{9,8},{10,9... | collective-permute-start | bytes 6152 | tf_op jit(solution)/shard_map/ppermute | solution.py:355
  12.1 0.0 copy-start
  12.1 0.0 copy-start.1
  12.1 0.0 copy-start.2
  12.1 0.0 copy-start.3
  12.1 1.4 %dynamic-slice_bitcast_fusion.table_ref = bf16[8,512,128]{2,1,0:T(8,128)(2,1)S(1)} fusion(bf16[2,8,512,128]{3,2,1,0:T(8,128)(2,1)} %constant.22.clone, s32[]{:T(128)S(6)} %select_n.4), kind=kLoop, calls=%fused_computation | loop fusion | bytes 2097156 | tf_op jit(solution)/shard_map/jit(dynamic_index_in_dim)/squeeze | solution.py:359
  13.5 1.6 %shard_map.112 = (bf16[16,64,128]{2,1,0:T(8,128)(2,1)S(1)}, f32[64,128]{1,0:T(8,128)S(1)}, bf16[3,2,64,128]{3,2,1,0:T(8,128)(2,1)S(1)}, f32[2,6,8,128]{3,2,1,0:T(8,128)S(1)}, f32[2,8,128]{2,1,0:T(8,128)S(1)}) custom-call(s32[1,64]{1,0:T(1,128)} %bitcast.14, s32[1,128]{1,0:T(1,128)} %bitcast.15, f32[3,2,64,128]{3,2,1,0:T(8,128)} %refs_2_.1, f32[2,64,128]{2,1,0:T(8,128)} %refs_3_.1), custom_call_target="tpu_custom_call" | custom-call | flops 2000000 | bytes 1000000 | tf_op jit(solution)/shard_map/pallas_call | solution.py:379
  15.1 0.0 collective-permute-done.ylo_ref
  15.1 0.0 collective-permute-done.1.yhi_ref
  15.1 0.2 shard_map.113
  15.4 15.7 %all_to_all.20.x_ref = bf16[16,64,128]{2,1,0:T(8,128)(2,1)S(1)} all-to-all(bf16[16,64,128]{2,1,0:T(8,128)(2,1)S(1)} %get-tuple-element.25), channel_id=1, replica_groups=mesh['yh'=4,'yl'=2,'xh'=2,'z'=8,'xl'=2,'c'=2] {'yh','yl','xh'}, dimensions={0} | all-to-all | bytes 524288 | tf_op jit(solution)/shard_map/all_to_all | solution.py:388
  31.1 1.8 %shard_map.114 = (bf16[512,128]{1,0:T(8,128)(2,1)S(1)}, bf16[3,2,64,128]{3,2,1,0:T(8,128)(2,1)}) custom-call(bf16[16,64,128]{2,1,0:T(8,128)(2,1)S(1)} %all_to_all.20.x_ref, bf16[8,512,128]{2,1,0:T(8,128)(2,1)S(1)} %dynamic-slice_bitcast_fusion.table_ref, f32[64,128]{1,0:T(8,128)S(1)} %get-tuple-element.27.held_ref, ...), custom_call_target="tpu_custom_call" | custom-call | tf_op jit(solution)/shard_map/pallas_call | solution.py:389
  32.9 31.2 %all_to_all.21 = bf16[256,2,128]{2,1,0:T(2,128)(2,1)S(1)} all-to-all(bf16[256,2,128]{2,1,0:T(2,128)(2,1)S(1)} %bitcast.10), channel_id=1, replica_groups=mesh['yh'=4,'yl'=2,'xh'=2,'z'=8,'xl'=2,'c'=2] {'yh','yl','z','xl','c'}, dimensions={0} | all-to-all | bytes 262144 | tf_op jit(solution)/shard_map/all_to_all | solution.py:395
  64.1 0.0 copy-done
  64.1 0.0 copy-done.1
  64.1 0.0 copy-done.2
  64.2 0.0 copy-done.3
  64.2 1.3 %shard_map.115 = (f32[2,2048]{1,0:T(2,128)}, f32[16,8,128]{2,1,0:T(8,128)S(1)}) custom-call(bf16[512,128]{1,0:T(8,128)(2,1)S(1)} %bitcast.9, bf16[512,512]{1,0:T(8,128)(2,1)S(1)} %copy-done, f32[2,8,256]{2,1,0:T(8,128)S(1)} %copy-done.3, bf16[128,128]{1,0:T(8,128)(2,1)S(1)} %copy-done.1, s32[2,2048]{1,0:T(2,128)S(1)} %copy-done.2), custom_call_target="tpu_custom_call" | custom-call | tf_op jit(solution)/shard_map/pallas_call | solution.py:398
  65.5 11.5 %all_to_all.22 = f32[16,8,128]{2,1,0:T(8,128)S(1)} all-to-all(f32[16,8,128]{2,1,0:T(8,128)S(1)} %get-tuple-element.32), channel_id=1, replica_groups=mesh['yh'=4,'yl'=2,'xh'=2,'z'=8,'xl'=2,'c'=2] {'yh','yl','c'}, dimensions={0} | all-to-all | bytes 131072 | tf_op jit(solution)/shard_map/all_to_all | solution.py:406
  77.0 12.2 %all_to_all.23 = bf16[32,8,128]{2,1,0:T(8,128)(2,1)S(1)} all-to-all(bf16[32,8,128]{2,1,0:T(8,128)(2,1)S(1)} %broadcast_in_dim.14), channel_id=1, replica_groups=mesh['yh'=4,'yl'=2,'xh'=2,'z'=8,'xl'=2,'c'=2] {'xh','z','xl'}, dimensions={0} | all-to-all | bytes 131072 | tf_op jit(solution)/shard_map/all_to_all | solution.py:408
  89.2 0.6 convert_reduce_fusion
  (2 shorter events, 0.0 us)
Async XLA Ops:
  1.4 13.7 %collective-permute-start = (f32[4,128]{1,0:T(4,128)S(1)}, f32[4,128]{1,0:T(4,128)S(1)}, u32[]{:S(2)}, u32[]{:S(2)}) collective-permute-start(f32[4,128]{1,0:T(4,128)S(1)} %bitcast.13), channel_id=1, source_target_pairs={{0,1},{1,2},{2,3},{3,4},{4,5},{5,6},{6,7},{7,8},{8,9},{9,10},{10,1... | collective-permute-start | bytes 6152 | tf_op jit(solution)/shard_map/ppermute | solution.py:355
  5.9 9.2 %collective-permute-start.1 = (f32[4,128]{1,0:T(4,128)S(1)}, f32[4,128]{1,0:T(4,128)S(1)}, u32[]{:S(2)}, u32[]{:S(2)}) collective-permute-start(f32[4,128]{1,0:T(4,128)S(1)} %bitcast.12), channel_id=1, source_target_pairs={{0,31},{1,0},{2,1},{3,2},{4,3},{5,4},{6,5},{7,6},{8,7},{9,8},{10,9... | collective-permute-start | bytes 6152 | tf_op jit(solution)/shard_map/ppermute | solution.py:355
  12.1 52.1 %copy-start = (bf16[512,512]{1,0:T(8,128)(2,1)S(1)}, bf16[512,512]{1,0:T(8,128)(2,1)}, u32[]{:S(2)}) copy-start(bf16[512,512]{1,0:T(8,128)(2,1)} %constant.23.clone.table_ref) | copy-start | bytes 1572868
  12.1 52.0 %copy-start.1 = (bf16[128,128]{1,0:T(8,128)(2,1)S(1)}, bf16[128,128]{1,0:T(8,128)(2,1)}, u32[]{:S(2)}) copy-start(bf16[128,128]{1,0:T(8,128)(2,1)} %constant.25.clone.order_ref) | copy-start | bytes 98308
  12.1 52.0 %copy-start.2 = (s32[2,2048]{1,0:T(2,128)S(1)}, s32[2,2048]{1,0:T(2,128)}, u32[]{:S(2)}) copy-start(s32[2,2048]{1,0:T(2,128)} %bins_ref.1) | copy-start | bytes 49156
  12.1 52.0 %copy-start.3 = (f32[2,8,256]{2,1,0:T(8,128)S(1)}, f32[2,8,256]{2,1,0:T(8,128)}, u32[]{:S(2)}) copy-start(f32[2,8,256]{2,1,0:T(8,128)} %constant.24.clone.turn_ref) | copy-start | bytes 49156

commit v8 on v7

--- a/solution.py
+++ b/solution.py
@@ -92,8 +92,26 @@
     return jnp.broadcast_to(jnp.transpose(half_y)[:, 0:1], shape), 0.5 * metric(lz_ref[...])
 
 
+def border_kernel(ly_far, fb_far, den_far, upper_ref, lower_ref, levels, top, bottom, dens, sems):
+    last = fb_far.shape[2] - 8
+    far = (ly_far, fb_far.at[:, :, 0:8, :], fb_far.at[:, :, last : last + 8, :], den_far.at[:, 0:8, :])
+    fetched(far, (levels, top, bottom, dens), sems)
+    for p in range(2):
+        for comp in range(3):
+            upper_ref[2 * comp + p : 2 * comp + p + 1, :] = top[comp, p, 0:1, :]
+        for n, comp in enumerate((0, 2)):
+            upper_ref[6 + 2 * n + p : 7 + 2 * n + p, :] = top[comp, p, 1:2, :]
+            lower_ref[2 * n + p : 2 * n + p + 1, :] = bottom[comp, p, 7:8, :]
+        upper_ref[10 + p : 11 + p, :] = dens[p, 0:1, :]
+    scale = 0.5 * metric(levels[...])[:, 0:1]
+    upper_ref[12:16, :] = jnp.broadcast_to(scale, (4, upper_ref.shape[1]))
+
+
 def message_kernel(*refs):
-    far, (msg_ref, held_ref, emf_ref, tips_ref, weights_ref), near, sems = refs[0:4], refs[4:9], refs[9:13], refs[13]
+    far, table_ref, outs, near, sems = refs[0:4], refs[4], refs[5:12], refs[12:16], refs[16]
+    msg_ref, held_ref, emf_ref, tips_ref, low_ref, last_ref, half_ref = outs
+    table_copy = pltpu.make_async_copy(table_ref.at[lax.axis_index("xh")], half_ref, sems.at[4])
+    table_copy.start()
     fetched(far, near, sems)
     ly_ref, lz_ref, fb, den = near
     shape = fb.shape[2:]
@@ -108,12 +126,13 @@
         parts = hall(p, fb, den, my, mz)
         inverse = 1.0 / den[p]
         weight = signed * inverse
-        for side, sign in ((0, -1.0), (1, 1.0)):
-            at = side * (shape[0] - 1)
-            upward = sign * my[at : at + 1] * inverse[at : at + 1]
-            for comp in range(3):
-                tips_ref[side, 2 * comp + p] = parts[comp][56 * side : 56 * side + 8]
-                weights_ref[side, 3 * p + comp : 3 * p + comp + 1, :] = upward * fb[comp, p, at : at + 1, :]
+        downward, upward = -my[0:1] * inverse[0:1], my[63:64] * inverse[63:64]
+        for comp in range(3):
+            tips_ref[2 * comp + p] = parts[comp][56:64]
+            low_ref[2 * comp + p : 2 * comp + p + 1, :] = parts[comp][0:1]
+            low_ref[6 + 3 * p + comp : 7 + 3 * p + comp, :] = downward * fb[comp, p, 0:1, :]
+            last_ref[3 * p + comp : 3 * p + comp + 1, :] = upward * fb[comp, p, 63:64, :]
+            last_ref[6 + 2 * comp + p : 7 + 2 * comp + p, :] = fb[comp, p, 63:64, :]
         fields = [fb[comp, p] for comp in range(3)]
         inside.append([jnp.where(edge, 0.0, part) for part in parts])
         terms = list(parts) + [f * weight for f in fields] + fields[0:2]
@@ -126,6 +145,9 @@
             own = jnp.where(slot == k, roll(fields[comp], 2 * k + 1, 1), own)
         for comp in range(3):
             emf_ref[comp, p] = inside[p][comp].astype(BF)
+    last_ref[12:13, :] = mz
+    last_ref[13:16, :] = jnp.zeros((3, shape[1]), F32)
+    low_ref[12:16, :] = jnp.zeros((4, shape[1]), F32)
     held_ref[...] = held[0] + roll(held[1], 16, 1)
     first = own.astype(BF).astype(F32)
     own = own - first
@@ -134,6 +156,8 @@
     folded = roll(own[0:16], 32, 1)
     for block in range(1, 4):
         folded = folded + roll(own[16 * block : 16 * block + 16], 32 + 24 * block, 1)
+    held = [roll(x, -1, 0) for x in held]
+    inside = [[roll(x, -1, 0) for x in plane] for plane in inside]
     for block in range(8):
         rows = slice(8 * block, 8 * block + 8)
         tile = jnp.concatenate([held[0][rows], held[1][rows]], axis=0)
@@ -144,11 +168,15 @@
         for n, value in enumerate(values):
             for copy in range(2):
                 msg_ref[2 * block + copy, 16 * n : 16 * n + 16, :] = value.astype(BF)
-
-
-def rim_kernel(
-    ylo_ref, yhi_ref, msg_ref, held_ref, emf_ref, tips_ref, weights_ref, msg_out, held_out, emf_out
-):
+    table_copy.wait()
+
+
+def changes(f_x, f_z, weights_ref, at):
+    w_x, w_y, w_z = (weights_ref[at + comp : at + comp + 1, :] for comp in range(3))
+    return (f_x * w_y, -(f_x * w_x + f_z * w_z), f_z * w_y)
+
+
+def rim_kernel(next_ref, msg_ref, held_ref, emf_ref, tips_ref, last_ref, msg_out, held_out, emf_out):
     msg_out[...] = msg_ref[...]
     held_out[...] = held_ref[...]
     emf_out[...] = emf_ref[...]
@@ -157,34 +185,56 @@
     lane = lax.broadcasted_iota(jnp.int32, shape, 1)
     inner = (lane > 0) & (lane < 127)
     slot = lane >> 1
-    for side, rim_ref in ((0, ylo_ref), (1, yhi_ref)):
-        block = 7 * side
-        rows = slice(8 * block, 8 * block + 8)
-        held = held_ref[rows, :]
-        values = []
-        for p in range(2):
-            f_x, f_z = rim_ref[p : p + 1, :], rim_ref[2 + p : 3 + p, :]
-            w_x, w_y, w_z = (weights_ref[side, 3 * p + comp : 3 * p + comp + 1, :] for comp in range(3))
-            extra = (f_x * w_y, -(f_x * w_x + f_z * w_z), f_z * w_y)
-            for comp in range(3):
-                change = jnp.where(row == 7 * side, extra[comp], 0.0)
-                value = jnp.where(inner, tips_ref[side, 2 * comp + p] + change, 0.0)
-                emf_out[comp, p, rows, :] = value.astype(BF)
-                values.append(value)
-                moved = roll(change, 16 * p + 2 * comp + 1, 1)
-                held = held + jnp.where(slot == 8 * p + comp, moved, 0.0)
-        held_out[rows, :] = held
-        tile = jnp.concatenate([held, roll(held, -16, 1)], axis=0)
-        wide = lax.broadcasted_iota(jnp.int32, tile.shape, 1)
-        tile = jnp.where(wide < 16, tile, 0.0)
-        high = tile.astype(BF).astype(F32)
-        low = (tile - high).astype(BF).astype(F32)
-        old = msg_ref[2 * block, 48:64, :].astype(F32)
-        tiles = [jnp.concatenate([values[comp], values[3 + comp]], axis=0) for comp in range(3)]
-        tiles.append(jnp.where(wide < 32, high + roll(low, 16, 1), old))
-        for n, value in enumerate(tiles):
-            for copy in range(2):
-                msg_out[2 * block + copy, 16 * n : 16 * n + 16, :] = value.astype(BF)
+    mz = last_ref[12:13, :]
+    line = lax.broadcasted_iota(jnp.int32, (1, shape[1]), 1)
+    signed = jnp.where(line == 0, -mz, mz)
+    beyond = next_ref[...]
+    wide = lax.broadcasted_iota(jnp.int32, beyond.shape, 1)
+    slope = (jnp.where(wide == 127, 0.0, roll(beyond, -1, 1)) - jnp.where(wide == 0, 0.0, roll(beyond, 1, 1))) * mz
+    my = beyond[12:13]
+    rows = slice(56, 64)
+    held = held_ref[rows, :]
+    values, tiles = [], []
+    for p in range(2):
+        f = [beyond[2 * comp + p : 2 * comp + p + 1] for comp in range(3)]
+        g = [beyond[2 * comp + 1 - p : 2 * comp + 2 - p] for comp in range(3)]
+        d_z = [slope[2 * comp + p : 2 * comp + p + 1] for comp in range(2)]
+        dy_x = (beyond[6 + p : 7 + p] - last_ref[6 + p : 7 + p, :]) * my
+        dy_z = (beyond[8 + p : 9 + p] - last_ref[10 + p : 11 + p, :]) * my
+        half = 0.5 if p == 0 else -0.5
+        cur_x, cur_y, cur_z = dy_z - d_z[1], d_z[0] - half * g[2], half * g[1] - dy_x
+        dens = beyond[10 + p : 11 + p]
+        made = [
+            (cur_y * f[2] - cur_z * f[1]) / dens,
+            (cur_z * f[0] - cur_x * f[2]) / dens,
+            (cur_x * f[1] - cur_y * f[0]) / dens,
+        ]
+        weight = signed / dens
+        terms = made + [x * weight for x in f] + f[0:2]
+        packed = jnp.zeros(shape, F32)
+        for q, term in enumerate(terms):
+            packed = jnp.where(slot == q, roll(jnp.broadcast_to(term, shape), 2 * q + 1, 1), packed)
+        extra = changes(f[0], f[2], last_ref, 3 * p)
+        for comp in range(3):
+            change = jnp.where(row == 7, extra[comp], 0.0)
+            value = jnp.where(inner, tips_ref[2 * comp + p] + change, 0.0)
+            emf_out[comp, p, rows, :] = value.astype(BF)
+            values.append(jnp.where(row == 7, jnp.where(inner, made[comp], 0.0), roll(value, -1, 0)))
+            held = held + jnp.where(slot == 8 * p + comp, roll(change, 16 * p + 2 * comp + 1, 1), 0.0)
+        tiles.append(packed)
+    held_out[rows, :] = held
+    for p in range(2):
+        moved = roll(held if p == 0 else roll(held, -16, 1), -1, 0)
+        tiles[p] = jnp.where(lane < 16, jnp.where(row == 7, tiles[p], moved), 0.0)
+    tile = jnp.concatenate(tiles, axis=0)
+    high = tile.astype(BF).astype(F32)
+    low = (tile - high).astype(BF).astype(F32)
+    old = msg_ref[14, 48:64, :].astype(F32)
+    tiles = [jnp.concatenate([values[comp], values[3 + comp]], axis=0) for comp in range(3)]
+    tiles.append(jnp.where(wide < 32, high + roll(low, 16, 1), old))
+    for n, value in enumerate(tiles):
+        for copy in range(2):
+            msg_out[14 + copy, 16 * n : 16 * n + 16, :] = value.astype(BF)
 
 
 def finished(held, beside):
@@ -208,7 +258,7 @@
     return [at_edges(values, 2 * comp + 1) for comp in range(3)]
 
 
-def finish_emf(x_ref, held_ref, inside_ref, emf_ref):
+def finish_emf(x_ref, held_ref, inside_ref, low_ref, before_ref, emf_ref):
     me = lax.axis_index("yh") * 4 + lax.axis_index("yl") * 2 + lax.axis_index("xh")
 
     def fields(block):
@@ -223,13 +273,30 @@
     lane = lax.broadcasted_iota(jnp.int32, low.shape, 1)
     beside = jnp.where((lane & 1) == 0, roll(high, -1, 1), roll(low, 1, 1))
     beside = jnp.where(lane < 16, roll(beside, 12, 1), roll(beside, 24, 1))
-    values = finished(held_ref[...], beside)
+    shape = (8, low.shape[1])
+    row = lax.broadcasted_iota(jnp.int32, shape, 0)
+    lane = lax.broadcasted_iota(jnp.int32, shape, 1)
+    inner = (lane > 0) & (lane < 127)
+    tips = {}
+    held = held_ref[0:8, :]
+    for p in range(2):
+        extra = changes(before_ref[p : p + 1, :], before_ref[2 + p : 3 + p, :], low_ref, 6 + 3 * p)
+        for comp in range(3):
+            change = jnp.where(row == 0, extra[comp], 0.0)
+            value = low_ref[2 * comp + p : 2 * comp + p + 1, :] + extra[comp]
+            plain = inside_ref[comp, p, 0:8, :].astype(F32)
+            tips[comp, p] = jnp.where(row == 0, jnp.where(inner, value, 0.0), plain)
+            moved = roll(change, 16 * p + 2 * comp + 1, 1)
+            held = held + jnp.where((lane >> 1) == 8 * p + comp, moved, 0.0)
+    values = finished(jnp.concatenate([held, held_ref[8:64, :]], axis=0), beside)
     for comp in range(3):
         for p in range(2):
-            emf_ref[comp, p] = inside_ref[comp, p] + at_edges(values, 16 * p + 2 * comp + 1)
-
-
-def z_kernel(x_ref, table_ref, held_ref, inside_ref, out_ref, emf_ref, mix_ref):
+            edges = at_edges(values, 16 * p + 2 * comp + 1)
+            emf_ref[comp, p] = inside_ref[comp, p] + edges
+            emf_ref[comp, p, 0:8, :] = (tips[comp, p] + edges[0:8].astype(F32)).astype(BF)
+
+
+def z_kernel(x_ref, table_ref, held_ref, inside_ref, low_ref, before_ref, out_ref, emf_ref, mix_ref):
     edges = line_edges(x_ref)
     zero = jnp.zeros((16, 512), BF)
     total = None
@@ -266,7 +333,7 @@
             at = 32 * (8 * c + jl)
             mix_ref[pl.ds(2 * jl + c, 32, stride=16), :] = total[at : at + 32]
     out_ref[...] = mix_ref[...].astype(BF)
-    finish_emf(x_ref, held_ref, inside_ref, emf_ref)
+    finish_emf(x_ref, held_ref, inside_ref, low_ref, before_ref, emf_ref)
 
 
 def add(a, b):
@@ -354,44 +421,58 @@
         count = lax.axis_size(axis)
         return lax.ppermute(cells, axis, [(i, (i + step) % count) for i in range(count)])
 
-    ylo = shift(field_b[0::2, :, y_local - 1, :].reshape(4, z_local), GY, 1)
-    yhi = shift(field_b[0::2, :, 0, :].reshape(4, z_local), GY, -1)
-    half = lax.dynamic_index_in_dim(jnp.asarray(z_table()), lax.axis_index("xh"), keepdims=False)
-    half, ylo, yhi = lax.optimization_barrier((half, ylo, yhi))
     small = pltpu.CompilerParams(vmem_limit_bytes=16 * 2**20)
     far = [
         pltpu.with_memory_space_constraint(x, pltpu.HBM)
         for x in (level_y[None, :], level_z[None, :], field_b, density)
     ]
+    upper, lower = pl.pallas_call(
+        border_kernel,
+        out_shape=(jax.ShapeDtypeStruct((16, z_local), F32), jax.ShapeDtypeStruct((4, z_local), F32)),
+        in_specs=[pl.BlockSpec(memory_space=pltpu.HBM)] * 3,
+        scratch_shapes=[
+            pltpu.VMEM((1, y_local), jnp.int32),
+            pltpu.VMEM((3, 2, 8, z_local), F32),
+            pltpu.VMEM((3, 2, 8, z_local), F32),
+            pltpu.VMEM((2, 8, z_local), F32),
+            pltpu.SemaphoreType.DMA((4,)),
+        ],
+        compiler_params=small,
+    )(far[0], far[2], far[3])
+    after = shift(upper, GY, -1)
+    before = shift(lower, GY, 1)
     scratch = [
         pltpu.VMEM((1, y_local), jnp.int32),
         pltpu.VMEM((1, z_local), jnp.int32),
         pltpu.VMEM(field_b.shape, F32),
         pltpu.VMEM(density.shape, F32),
-        pltpu.SemaphoreType.DMA((4,)),
+        pltpu.SemaphoreType.DMA((5,)),
     ]
     made = (
         jax.ShapeDtypeStruct((16, 64, z_local), BF),
         jax.ShapeDtypeStruct((y_local, z_local), F32),
         jax.ShapeDtypeStruct(field_b.shape, BF),
     )
-    rims = (jax.ShapeDtypeStruct((2, 6, 8, z_local), F32), jax.ShapeDtypeStruct((2, 8, z_local), F32))
-    local = pl.pallas_call(
+    rows = [jax.ShapeDtypeStruct(shape, F32) for shape in ((6, 8, z_local), (16, z_local), (16, z_local))]
+    table = pltpu.with_memory_space_constraint(jnp.asarray(z_table()), pltpu.HBM)
+    message, held, inside, tips, low, last, half = pl.pallas_call(
         message_kernel,
-        out_shape=made + rims,
-        in_specs=[pl.BlockSpec(memory_space=pltpu.HBM)] * 4,
+        out_shape=made + tuple(rows) + (jax.ShapeDtypeStruct(table.shape[1:], BF),),
+        in_specs=[pl.BlockSpec(memory_space=pltpu.HBM)] * 5,
         scratch_shapes=scratch,
         compiler_params=small,
-        cost_estimate=pl.CostEstimate(flops=2_000_000, bytes_accessed=1_000_000, transcendentals=0),
-    )(*far)
-    message, held, inside = pl.pallas_call(rim_kernel, out_shape=made, compiler_params=small)(ylo, yhi, *local)
+        cost_estimate=pl.CostEstimate(flops=2_000_000, bytes_accessed=2_000_000, transcendentals=0),
+    )(*far, table)
+    message, held, inside = pl.pallas_call(rim_kernel, out_shape=made, compiler_params=small)(
+        after, message, held, inside, tips, last
+    )
     lines = lax.all_to_all(message, GZ, 0, 0, tiled=True)
     z_modes, emf = pl.pallas_call(
         z_kernel,
         out_shape=(jax.ShapeDtypeStruct((512, 128), BF), jax.ShapeDtypeStruct(field_b.shape, BF)),
         scratch_shapes=[pltpu.VMEM((512, 128), F32)],
         compiler_params=small,
-    )(lines, half, held, inside)
+    )(lines, half, held, inside, low, before)
     spread = lax.all_to_all(z_modes.reshape(256, 2, 128), ("yh", "yl") + GY, 0, 0, tiled=True).reshape(512, 128)
     first = ("yh", "yl", "c")
     second = ("xh", "z", "xl")

time: 90.3 us -> 87.2 us (0.966)
  blocking collectives: 70.7 us -> 53.7 us
  waiting for transfers between devices: 0.01 us -> 9.29 us
  starting transfers between devices: 10.7 us -> 15.5 us
  local copies, waits for them, and re-layouts: 2.14 us -> 0.04 us
  Pallas kernels: 4.95 us -> 6.92 us
    all_to_all x1 -> x0, blocking collectives: 15.7 us -> none  [on_device(): lines = lax.all_to_all(message, GZ, 0, 0, tiled=True)]
    ppermute x2, waiting for transfers between devices: 0.01 us -> 9.29 us  [shift(): lax.ppermute(cells, axis, [(i, (i + step) % count) for i in range(count)])]
    all_to_all x0 -> x1, starting transfers between devices: none -> 4.35 us  [on_device(): lines = lax.all_to_all(message, GZ, 0, 0, tiled=True)]
    squeeze x1 -> x0, local copies, waits for them, and re-layouts: 1.35 us -> none  [on_device(): lax.dynamic_index_in_dim(jnp.asarray(z_table()), lax.axis_index('xh'), ke...]
    all_to_all x1, blocking collectives: 31.2 us -> 29.9 us  [on_device(): lax.all_to_all(z_modes.reshape(256, 2, 128), ('yh', 'yl') + GY, 0, 0, til...]
    pallas_call x1 -> x2, Pallas kernels: 1.59 us -> 2.87 us  [the longest x1 1.97 us: on_device(): pl.pallas_call(message_kernel, out_shape=made + tuple(rows) + (jax.ShapeD...]
  transfers between devices with their start and end apart: 2 -> 3, of which waited for: 0 -> 1; matrix products, arithmetic and copies ran while one was open for 2% -> 0% of each run, Pallas kernels for 2% -> 2%
where the time goes in v8:
time: 87.2 us; the launch traced here: 86.7 us
  blocking collectives  53.7 us (62%)
  starting transfers between devices  15.5 us (18%)
  waiting for transfers between devices  9.29 us (11%)
  Pallas kernels  6.92 us (8%)
    all_to_all x1, blocking collectives, on_device(): lax.all_to_all(z_modes.reshape(256, 2, 128), ('yh', 'yl') + GY, 0, 0, til...  29.9 us
    all_to_all x1, blocking collectives, on_device(): lax.all_to_all(copies, second, 0, 0, tiled=True).astype(F32)  12.2 us
    all_to_all x1, blocking collectives, on_device(): sums = jnp.sum(lax.all_to_all(sums, first, 0, 0, tiled=True), axis=0)  11.5 us
    ppermute x2, starting transfers between devices, shift(): lax.ppermute(cells, axis, [(i, (i + step) % count) for i in range(count)])  11.1 us
    ppermute x2, waiting for transfers between devices, shift(): lax.ppermute(cells, axis, [(i, (i + step) % count) for i in range(count)])  9.29 us
    all_to_all x1, starting transfers between devices, on_device(): lines = lax.all_to_all(message, GZ, 0, 0, tiled=True)  4.35 us
    pallas_call x1, Pallas kernels, on_device(): pl.pallas_call(message_kernel, out_shape=made + tuple(rows) + (jax.ShapeD...  1.97 us
    pallas_call x1, Pallas kernels, on_device(): pl.pallas_call(z_kernel, out_shape=(jax.ShapeDtypeStruct((512, 128), BF),...  1.82 us
  transfers between devices with their start and end apart: 3, of which 1 were waited for; matrix products, arithmetic and copies ran while one was open for 0% of the time, Pallas kernels for 2%

profile of v8, /device:TPU:1, one launch (start us, length us, event | category | flops | bytes accessed | tf_op | source)
XLA Modules:
  0.0 86.7 jit_solution(8243190274388098719)
XLA Ops:
  0.6 0.9 %shard_map.112 = (f32[16,128]{1,0:T(8,128)S(1)}, f32[4,128]{1,0:T(4,128)S(1)}) custom-call(s32[1,64]{1,0:T(1,128)} %bitcast.8, f32[3,2,64,128]{3,2,1,0:T(8,128)} %refs_2_.1, f32[2,64,128]{2,1,0:T(8,128)} %refs_3_.1), custom_call_target="tpu_custom_call" | custom-call | tf_op jit(solution)/shard_map/pallas_call | solution.py:429
  1.5 8.8 %collective-permute-start = (f32[16,128]{1,0:T(8,128)S(1)}, f32[16,128]{1,0:T(8,128)S(1)}, u32[]{:S(2)}, u32[]{:S(2)}) collective-permute-start(f32[16,128]{1,0:T(8,128)S(1)} %get-tuple-element.19), channel_id=1, source_target_pairs={{0,31},{1,0},{2,1},{3,2},{4,3},{5,4},{6,5},{7,6},{8,7},{9,8},{10,9... | collective-permute-start | bytes 24584 | tf_op jit(solution)/shard_map/ppermute | solution.py:422
  10.3 0.0 copy-start
  10.3 0.0 copy-start.1
  10.4 0.0 copy-start.2
  10.4 0.0 copy-start.3
  10.4 2.0 %shard_map.113 = (bf16[16,64,128]{2,1,0:T(8,128)(2,1)S(1)}, f32[64,128]{1,0:T(8,128)S(1)}, bf16[3,2,64,128]{3,2,1,0:T(8,128)(2,1)S(1)}, f32[6,8,128]{2,1,0:T(8,1...) custom-call(s32[1,64]{1,0:T(1,128)} %bitcast.9, s32[1,128]{1,0:T(1,128)} %bitcast.10, ...), custom_call_target="tpu_custom_call" | custom-call | flops 2000000 | bytes 2000000 | tf_op jit(solution)/shard_map/pallas_call | solution.py:458
  12.4 0.0 collective-permute-done.next_ref
  12.4 0.9 %shard_map.114 = (bf16[16,64,128]{2,1,0:T(8,128)(2,1)}, f32[64,128]{1,0:T(8,128)S(1)}, bf16[3,2,64,128]{3,2,1,0:T(8,128)(2,1)S(1)}) custom-call(f32[16,128]{1,0:T(8,128)S(1)} %collective-permute-done.next_ref, bf16[16,64,128]{2,1,0:T(8,128)(2,1)S(1)} %get-tuple-element.20.msg_ref, f32[64,128]{1,0:T(8,128)S(1)} %get-tuple-element.21.held_ref, ...), custom_call_target="tpu_custom_call" | custom-call | tf_op jit(solution)/shard_map/pallas_call | solution.py:466
  13.3 4.3 %all-to-all-start = ((bf16[16,64,128]{2,1,0:T(8,128)(2,1)}), bf16[16,64,128]{2,1,0:T(8,128)(2,1)S(1)}, u32[]{:S(2)}, u32[]{:S(2)}) async-start(bf16[16,64,128]{2,1,0:T(8,128)(2,1)} %get-tuple-element.25), calls=%async_computation | async-start | bytes 524288 | tf_op jit(solution)/shard_map/all_to_all | solution.py:469
  17.7 2.3 %collective-permute-start.1 = (f32[4,128]{1,0:T(4,128)S(1)}, f32[4,128]{1,0:T(4,128)S(1)}, u32[]{:S(2)}, u32[]{:S(2)}) collective-permute-start(f32[4,128]{1,0:T(4,128)S(1)} %get-tuple-element.30), channel_id=1, source_target_pairs={{0,1},{1,2},{2,3},{3,4},{4,5},{5,6},{6,7},{7,8},{8,9},{9,10},{10,1... | collective-permute-start | bytes 6152 | tf_op jit(solution)/shard_map/ppermute | solution.py:422
  20.0 9.3 %collective-permute-done.1.before_ref = f32[4,128]{1,0:T(4,128)S(1)} collective-permute-done((f32[4,128]{1,0:T(4,128)S(1)}, f32[4,128]{1,0:T(4,128)S(1)}, u32[]{:S(2)}, u32[]{:S(2)}) %collective-permute-start.1) | collective-permute-done | bytes 2080 | tf_op jit(solution)/shard_map/ppermute | solution.py:422
  29.3 0.0 all-to-all-done.x_ref
  29.3 1.8 %shard_map.115 = (bf16[512,128]{1,0:T(8,128)(2,1)S(1)}, bf16[3,2,64,128]{3,2,1,0:T(8,128)(2,1)}) custom-call(bf16[16,64,128]{2,1,0:T(8,128)(2,1)S(1)} %all-to-all-done.x_ref, bf16[8,512,128]{2,1,0:T(8,128)(2,1)S(1)} %get-tuple-element.26.table_ref, f32[64,128]{1,0:T(8,128)S(1)} %get-tuple-element.27.held_ref, ...), custom_call_target="tpu_custom_call" | custom-call | tf_op jit(solution)/shard_map/pallas_call | solution.py:470
  31.1 29.9 %all_to_all.20 = bf16[256,2,128]{2,1,0:T(2,128)(2,1)S(1)} all-to-all(bf16[256,2,128]{2,1,0:T(2,128)(2,1)S(1)} %bitcast.6), channel_id=1, replica_groups=mesh['yh'=4,'yl'=2,'xh'=2,'z'=8,'xl'=2,'c'=2] {'yh','yl','z','xl','c'}, dimensions={0} | all-to-all | bytes 262144 | tf_op jit(solution)/shard_map/all_to_all | solution.py:476
  61.0 0.0 copy-done
  61.0 0.0 copy-done.1
  61.0 0.0 copy-done.2
  61.0 0.0 copy-done.3
  61.0 1.3 %shard_map.116 = (f32[2,2048]{1,0:T(2,128)}, f32[16,8,128]{2,1,0:T(8,128)S(1)}) custom-call(bf16[512,128]{1,0:T(8,128)(2,1)S(1)} %bitcast.5, bf16[512,512]{1,0:T(8,128)(2,1)S(1)} %copy-done, f32[2,8,256]{2,1,0:T(8,128)S(1)} %copy-done.3, bf16[128,128]{1,0:T(8,128)(2,1)S(1)} %copy-done.1, s32[2,2048]{1,0:T(2,128)S(1)} %copy-done.2), custom_call_target="tpu_custom_call" | custom-call | tf_op jit(solution)/shard_map/pallas_call | solution.py:479
  62.3 11.5 %all_to_all.21 = f32[16,8,128]{2,1,0:T(8,128)S(1)} all-to-all(f32[16,8,128]{2,1,0:T(8,128)S(1)} %get-tuple-element.34), channel_id=1, replica_groups=mesh['yh'=4,'yl'=2,'xh'=2,'z'=8,'xl'=2,'c'=2] {'yh','yl','c'}, dimensions={0} | all-to-all | bytes 131072 | tf_op jit(solution)/shard_map/all_to_all | solution.py:487
  73.8 12.2 %all_to_all.22 = bf16[32,8,128]{2,1,0:T(8,128)(2,1)S(1)} all-to-all(bf16[32,8,128]{2,1,0:T(8,128)(2,1)S(1)} %broadcast_in_dim.14), channel_id=1, replica_groups=mesh['yh'=4,'yl'=2,'xh'=2,'z'=8,'xl'=2,'c'=2] {'xh','z','xl'}, dimensions={0} | all-to-all | bytes 131072 | tf_op jit(solution)/shard_map/all_to_all | solution.py:489
  86.1 0.6 convert_reduce_fusion
  (2 shorter events, 0.0 us)
Async XLA Ops:
  1.5 10.8 %collective-permute-start = (f32[16,128]{1,0:T(8,128)S(1)}, f32[16,128]{1,0:T(8,128)S(1)}, u32[]{:S(2)}, u32[]{:S(2)}) collective-permute-start(f32[16,128]{1,0:T(8,128)S(1)} %get-tuple-element.19), channel_id=1, source_target_pairs={{0,31},{1,0},{2,1},{3,2},{4,3},{5,4},{6,5},{7,6},{8,7},{9,8},{10,9... | collective-permute-start | bytes 24584 | tf_op jit(solution)/shard_map/ppermute | solution.py:422
  10.3 50.7 %copy-start = (bf16[512,512]{1,0:T(8,128)(2,1)S(1)}, bf16[512,512]{1,0:T(8,128)(2,1)}, u32[]{:S(2)}) copy-start(bf16[512,512]{1,0:T(8,128)(2,1)} %constant.11.clone.table_ref) | copy-start | bytes 1572868
  10.3 50.7 %copy-start.1 = (bf16[128,128]{1,0:T(8,128)(2,1)S(1)}, bf16[128,128]{1,0:T(8,128)(2,1)}, u32[]{:S(2)}) copy-start(bf16[128,128]{1,0:T(8,128)(2,1)} %constant.13.clone.order_ref) | copy-start | bytes 98308
  10.4 50.7 %copy-start.2 = (s32[2,2048]{1,0:T(2,128)S(1)}, s32[2,2048]{1,0:T(2,128)}, u32[]{:S(2)}) copy-start(s32[2,2048]{1,0:T(2,128)} %bins_ref.1) | copy-start | bytes 49156
  10.4 50.7 %copy-start.3 = (f32[2,8,256]{2,1,0:T(8,128)S(1)}, f32[2,8,256]{2,1,0:T(8,128)}, u32[]{:S(2)}) copy-start(f32[2,8,256]{2,1,0:T(8,128)} %constant.12.clone.turn_ref) | copy-start | bytes 49156
  13.3 16.0 %all-to-all-start = ((bf16[16,64,128]{2,1,0:T(8,128)(2,1)}), bf16[16,64,128]{2,1,0:T(8,128)(2,1)S(1)}, u32[]{:S(2)}, u32[]{:S(2)}) async-start(bf16[16,64,128]{2,1,0:T(8,128)(2,1)} %get-tuple-element.25), calls=%async_computation | async-start | bytes 524288 | tf_op jit(solution)/shard_map/all_to_all | solution.py:469
  17.7 11.6 %collective-permute-start.1 = (f32[4,128]{1,0:T(4,128)S(1)}, f32[4,128]{1,0:T(4,128)S(1)}, u32[]{:S(2)}, u32[]{:S(2)}) collective-permute-start(f32[4,128]{1,0:T(4,128)S(1)} %get-tuple-element.30), channel_id=1, source_target_pairs={{0,1},{1,2},{2,3},{3,4},{4,5},{5,6},{6,7},{7,8},{8,9},{9,10},{10,1... | collective-permute-start | bytes 6152 | tf_op jit(solution)/shard_map/ppermute | solution.py:422

commit v9 on v8

--- a/solution.py
+++ b/solution.py
@@ -15,7 +15,7 @@
 BF = jnp.bfloat16
 F32 = jnp.float32
 GZ = ("yh", "yl", "xh")
-GY = ("z", "xl", "c")
+GY = ('z', 'xl', 'c')
 ACROSS = (((1,), (1,)), ((), ()))
 
 
@@ -474,8 +474,8 @@
         compiler_params=small,
     )(lines, half, held, inside, low, before)
     spread = lax.all_to_all(z_modes.reshape(256, 2, 128), ("yh", "yl") + GY, 0, 0, tiled=True).reshape(512, 128)
-    first = ("yh", "yl", "c")
-    second = ("xh", "z", "xl")
+    first = ('xh', 'xl', 'c')
+    second = ('yh', 'yl', 'z')
     mode_power, sums = pl.pallas_call(
         y_kernel,
         out_shape=(

time: 87.2 us -> 86.8 us (level)
    all_to_all x1, blocking collectives: 11.5 us -> 7.86 us  [on_device(): sums = jnp.sum(lax.all_to_all(sums, first, 0, 0, tiled=True), axis=0)]
    all_to_all x1, blocking collectives: 12.2 us -> 15.4 us  [on_device(): lax.all_to_all(copies, second, 0, 0, tiled=True).astype(F32)]
where the time goes in v9:
time: 86.8 us; the launch traced here: 86.3 us
  blocking collectives  53.2 us (61%)
  starting transfers between devices  15.5 us (18%)
  waiting for transfers between devices  9.29 us (11%)
  Pallas kernels  6.92 us (8%)
    all_to_all x1, blocking collectives, on_device(): lax.all_to_all(z_modes.reshape(256, 2, 128), ('yh', 'yl') + GY, 0, 0, til...  29.9 us
    all_to_all x1, blocking collectives, on_device(): lax.all_to_all(copies, second, 0, 0, tiled=True).astype(F32)  15.4 us
    ppermute x2, starting transfers between devices, shift(): lax.ppermute(cells, axis, [(i, (i + step) % count) for i in range(count)])  11.1 us
    ppermute x2, waiting for transfers between devices, shift(): lax.ppermute(cells, axis, [(i, (i + step) % count) for i in range(count)])  9.29 us
    all_to_all x1, blocking collectives, on_device(): sums = jnp.sum(lax.all_to_all(sums, first, 0, 0, tiled=True), axis=0)  7.86 us
    all_to_all x1, starting transfers between devices, on_device(): lines = lax.all_to_all(message, GZ, 0, 0, tiled=True)  4.35 us
    pallas_call x1, Pallas kernels, on_device(): pl.pallas_call(message_kernel, out_shape=made + tuple(rows) + (jax.ShapeD...  1.97 us
    pallas_call x1, Pallas kernels, on_device(): pl.pallas_call(z_kernel, out_shape=(jax.ShapeDtypeStruct((512, 128), BF),...  1.82 us
  transfers between devices with their start and end apart: 3, of which 1 were waited for; matrix products, arithmetic and copies ran while one was open for 0% of the time, Pallas kernels for 2%

profile of v9, /device:TPU:1, one launch (start us, length us, event | category | flops | bytes accessed | tf_op | source)
XLA Modules:
  0.0 86.3 jit_solution(7221213033771350350)
XLA Ops:
  0.6 0.9 %shard_map.112 = (f32[16,128]{1,0:T(8,128)S(1)}, f32[4,128]{1,0:T(4,128)S(1)}) custom-call(s32[1,64]{1,0:T(1,128)} %bitcast.8, f32[3,2,64,128]{3,2,1,0:T(8,128)} %refs_2_.1, f32[2,64,128]{2,1,0:T(8,128)} %refs_3_.1), custom_call_target="tpu_custom_call" | custom-call | tf_op jit(solution)/shard_map/pallas_call | solution.py:429
  1.5 8.8 %collective-permute-start = (f32[16,128]{1,0:T(8,128)S(1)}, f32[16,128]{1,0:T(8,128)S(1)}, u32[]{:S(2)}, u32[]{:S(2)}) collective-permute-start(f32[16,128]{1,0:T(8,128)S(1)} %get-tuple-element.19), channel_id=1, source_target_pairs={{0,31},{1,0},{2,1},{3,2},{4,3},{5,4},{6,5},{7,6},{8,7},{9,8},{10,9... | collective-permute-start | bytes 24584 | tf_op jit(solution)/shard_map/ppermute | solution.py:422
  10.3 0.0 copy-start
  10.3 0.0 copy-start.1
  10.4 0.0 copy-start.2
  10.4 0.0 copy-start.3
  10.4 2.0 %shard_map.113 = (bf16[16,64,128]{2,1,0:T(8,128)(2,1)S(1)}, f32[64,128]{1,0:T(8,128)S(1)}, bf16[3,2,64,128]{3,2,1,0:T(8,128)(2,1)S(1)}, f32[6,8,128]{2,1,0:T(8,1...) custom-call(s32[1,64]{1,0:T(1,128)} %bitcast.9, s32[1,128]{1,0:T(1,128)} %bitcast.10, ...), custom_call_target="tpu_custom_call" | custom-call | flops 2000000 | bytes 2000000 | tf_op jit(solution)/shard_map/pallas_call | solution.py:458
  12.4 0.0 collective-permute-done.next_ref
  12.4 0.9 %shard_map.114 = (bf16[16,64,128]{2,1,0:T(8,128)(2,1)}, f32[64,128]{1,0:T(8,128)S(1)}, bf16[3,2,64,128]{3,2,1,0:T(8,128)(2,1)S(1)}) custom-call(f32[16,128]{1,0:T(8,128)S(1)} %collective-permute-done.next_ref, bf16[16,64,128]{2,1,0:T(8,128)(2,1)S(1)} %get-tuple-element.20.msg_ref, f32[64,128]{1,0:T(8,128)S(1)} %get-tuple-element.21.held_ref, ...), custom_call_target="tpu_custom_call" | custom-call | tf_op jit(solution)/shard_map/pallas_call | solution.py:466
  13.3 4.3 %all-to-all-start = ((bf16[16,64,128]{2,1,0:T(8,128)(2,1)}), bf16[16,64,128]{2,1,0:T(8,128)(2,1)S(1)}, u32[]{:S(2)}, u32[]{:S(2)}) async-start(bf16[16,64,128]{2,1,0:T(8,128)(2,1)} %get-tuple-element.25), calls=%async_computation | async-start | bytes 524288 | tf_op jit(solution)/shard_map/all_to_all | solution.py:469
  17.7 2.3 %collective-permute-start.1 = (f32[4,128]{1,0:T(4,128)S(1)}, f32[4,128]{1,0:T(4,128)S(1)}, u32[]{:S(2)}, u32[]{:S(2)}) collective-permute-start(f32[4,128]{1,0:T(4,128)S(1)} %get-tuple-element.30), channel_id=1, source_target_pairs={{0,1},{1,2},{2,3},{3,4},{4,5},{5,6},{6,7},{7,8},{8,9},{9,10},{10,1... | collective-permute-start | bytes 6152 | tf_op jit(solution)/shard_map/ppermute | solution.py:422
  20.0 9.3 %collective-permute-done.1.before_ref = f32[4,128]{1,0:T(4,128)S(1)} collective-permute-done((f32[4,128]{1,0:T(4,128)S(1)}, f32[4,128]{1,0:T(4,128)S(1)}, u32[]{:S(2)}, u32[]{:S(2)}) %collective-permute-start.1) | collective-permute-done | bytes 2080 | tf_op jit(solution)/shard_map/ppermute | solution.py:422
  29.3 0.0 all-to-all-done.x_ref
  29.3 1.8 %shard_map.115 = (bf16[512,128]{1,0:T(8,128)(2,1)S(1)}, bf16[3,2,64,128]{3,2,1,0:T(8,128)(2,1)}) custom-call(bf16[16,64,128]{2,1,0:T(8,128)(2,1)S(1)} %all-to-all-done.x_ref, bf16[8,512,128]{2,1,0:T(8,128)(2,1)S(1)} %get-tuple-element.26.table_ref, f32[64,128]{1,0:T(8,128)S(1)} %get-tuple-element.27.held_ref, ...), custom_call_target="tpu_custom_call" | custom-call | tf_op jit(solution)/shard_map/pallas_call | solution.py:470
  31.1 29.9 %all_to_all.20 = bf16[256,2,128]{2,1,0:T(2,128)(2,1)S(1)} all-to-all(bf16[256,2,128]{2,1,0:T(2,128)(2,1)S(1)} %bitcast.6), channel_id=1, replica_groups=mesh['yh'=4,'yl'=2,'xh'=2,'z'=8,'xl'=2,'c'=2] {'yh','yl','z','xl','c'}, dimensions={0} | all-to-all | bytes 262144 | tf_op jit(solution)/shard_map/all_to_all | solution.py:476
  61.0 0.0 copy-done
  61.0 0.0 copy-done.1
  61.0 0.0 copy-done.2
  61.0 0.0 copy-done.3
  61.0 1.3 %shard_map.116 = (f32[2,2048]{1,0:T(2,128)}, f32[8,8,128]{2,1,0:T(8,128)S(1)}) custom-call(bf16[512,128]{1,0:T(8,128)(2,1)S(1)} %bitcast.5, bf16[512,512]{1,0:T(8,128)(2,1)S(1)} %copy-done, f32[2,8,256]{2,1,0:T(8,128)S(1)} %copy-done.3, bf16[128,128]{1,0:T(8,128)(2,1)S(1)} %copy-done.1, s32[2,2048]{1,0:T(2,128)S(1)} %copy-done.2), custom_call_target="tpu_custom_call" | custom-call | tf_op jit(solution)/shard_map/pallas_call | solution.py:479
  62.3 7.9 %all_to_all.21 = f32[8,8,128]{2,1,0:T(8,128)S(1)} all-to-all(f32[8,8,128]{2,1,0:T(8,128)S(1)} %get-tuple-element.34), channel_id=1, replica_groups=mesh['yh'=4,'yl'=2,'xh'=2,'z'=8,'xl'=2,'c'=2] {'xh','xl','c'}, dimensions={0} | all-to-all | bytes 65536 | tf_op jit(solution)/shard_map/all_to_all | solution.py:487
  70.2 15.4 %all_to_all.22 = bf16[64,8,128]{2,1,0:T(8,128)(2,1)S(1)} all-to-all(bf16[64,8,128]{2,1,0:T(8,128)(2,1)S(1)} %broadcast_in_dim.14), channel_id=1, replica_groups=mesh['yh'=4,'yl'=2,'xh'=2,'z'=8,'xl'=2,'c'=2] {'yh','yl','z'}, dimensions={0} | all-to-all | bytes 262144 | tf_op jit(solution)/shard_map/all_to_all | solution.py:489
  85.7 0.7 convert_reduce_fusion
  (2 shorter events, 0.0 us)
Async XLA Ops:
  1.5 10.8 %collective-permute-start = (f32[16,128]{1,0:T(8,128)S(1)}, f32[16,128]{1,0:T(8,128)S(1)}, u32[]{:S(2)}, u32[]{:S(2)}) collective-permute-start(f32[16,128]{1,0:T(8,128)S(1)} %get-tuple-element.19), channel_id=1, source_target_pairs={{0,31},{1,0},{2,1},{3,2},{4,3},{5,4},{6,5},{7,6},{8,7},{9,8},{10,9... | collective-permute-start | bytes 24584 | tf_op jit(solution)/shard_map/ppermute | solution.py:422
  10.3 50.7 %copy-start = (bf16[512,512]{1,0:T(8,128)(2,1)S(1)}, bf16[512,512]{1,0:T(8,128)(2,1)}, u32[]{:S(2)}) copy-start(bf16[512,512]{1,0:T(8,128)(2,1)} %constant.11.clone.table_ref) | copy-start | bytes 1572868
  10.3 50.7 %copy-start.1 = (bf16[128,128]{1,0:T(8,128)(2,1)S(1)}, bf16[128,128]{1,0:T(8,128)(2,1)}, u32[]{:S(2)}) copy-start(bf16[128,128]{1,0:T(8,128)(2,1)} %constant.13.clone.order_ref) | copy-start | bytes 98308
  10.4 50.7 %copy-start.2 = (s32[2,2048]{1,0:T(2,128)S(1)}, s32[2,2048]{1,0:T(2,128)}, u32[]{:S(2)}) copy-start(s32[2,2048]{1,0:T(2,128)} %bins_ref.1) | copy-start | bytes 49156
  10.4 50.7 %copy-start.3 = (f32[2,8,256]{2,1,0:T(8,128)S(1)}, f32[2,8,256]{2,1,0:T(8,128)}, u32[]{:S(2)}) copy-start(f32[2,8,256]{2,1,0:T(8,128)} %constant.12.clone.turn_ref) | copy-start | bytes 49156
  13.3 16.0 %all-to-all-start = ((bf16[16,64,128]{2,1,0:T(8,128)(2,1)}), bf16[16,64,128]{2,1,0:T(8,128)(2,1)S(1)}, u32[]{:S(2)}, u32[]{:S(2)}) async-start(bf16[16,64,128]{2,1,0:T(8,128)(2,1)} %get-tuple-element.25), calls=%async_computation | async-start | bytes 524288 | tf_op jit(solution)/shard_map/all_to_all | solution.py:469
  17.7 11.6 %collective-permute-start.1 = (f32[4,128]{1,0:T(4,128)S(1)}, f32[4,128]{1,0:T(4,128)S(1)}, u32[]{:S(2)}, u32[]{:S(2)}) collective-permute-start(f32[4,128]{1,0:T(4,128)S(1)} %get-tuple-element.30), channel_id=1, source_target_pairs={{0,1},{1,2},{2,3},{3,4},{4,5},{5,6},{6,7},{7,8},{8,9},{9,10},{10,1... | collective-permute-start | bytes 6152 | tf_op jit(solution)/shard_map/ppermute | solution.py:422

commit v10 on v9

--- a/solution.py
+++ b/solution.py
@@ -167,7 +167,7 @@
         values.append(high + roll(low, 16, 1) + folded)
         for n, value in enumerate(values):
             for copy in range(2):
-                msg_ref[2 * block + copy, 16 * n : 16 * n + 16, :] = value.astype(BF)
+                msg_ref[8 * copy + block, 16 * n : 16 * n + 16, :] = value.astype(BF)
     table_copy.wait()
 
 
@@ -229,12 +229,12 @@
     tile = jnp.concatenate(tiles, axis=0)
     high = tile.astype(BF).astype(F32)
     low = (tile - high).astype(BF).astype(F32)
-    old = msg_ref[14, 48:64, :].astype(F32)
+    old = msg_ref[7, 48:64, :].astype(F32)
     tiles = [jnp.concatenate([values[comp], values[3 + comp]], axis=0) for comp in range(3)]
     tiles.append(jnp.where(wide < 32, high + roll(low, 16, 1), old))
     for n, value in enumerate(tiles):
         for copy in range(2):
-            msg_out[14 + copy, 16 * n : 16 * n + 16, :] = value.astype(BF)
+            msg_out[8 * copy + 7, 16 * n : 16 * n + 16, :] = value.astype(BF)
 
 
 def finished(held, beside):
@@ -249,8 +249,12 @@
     return jnp.where((lane == 0) | (lane == 127), roll(values, -spot, 1), 0.0).astype(BF)
 
 
+def spot(block):
+    return (block & 1) * 8 + (block >> 1)
+
+
 def line_edges(x_ref):
-    held = jnp.concatenate([x_ref[i, 48:64, :] for i in range(16)], axis=0).astype(F32)
+    held = jnp.concatenate([x_ref[spot(i), 48:64, :] for i in range(16)], axis=0).astype(F32)
     held = held + roll(held, -16, 1)
     lane = lax.broadcasted_iota(jnp.int32, held.shape, 1)
     beside = jnp.where((lane & 1) == 0, roll(roll(held, -16, 0), -1, 1), roll(roll(held, 16, 0), 1, 1))
@@ -262,7 +266,7 @@
     me = lax.axis_index("yh") * 4 + lax.axis_index("yl") * 2 + lax.axis_index("xh")
 
     def fields(block):
-        folded = x_ref[block, 48:64, :].astype(F32)
+        folded = x_ref[spot(block), 48:64, :].astype(F32)
         rows = []
         for n in range(4):
             own = roll(folded, -(32 + 24 * n), 1)
@@ -307,7 +311,7 @@
                 tiles = []
                 for c in range(3):
                     near, far = (
-                        x_ref[m, 16 * c : 16 * c + 16, :] + edges[c][16 * m : 16 * m + 16] for m in (i, i + 8)
+                        x_ref[spot(m), 16 * c : 16 * c + 16, :] + edges[c][16 * m : 16 * m + 16] for m in (i, i + 8)
                     )
                     tiles.append(near + far if pair > 0 else near - far)
                 side.append(jnp.concatenate(tiles, axis=0))
@@ -466,7 +470,7 @@
     message, held, inside = pl.pallas_call(rim_kernel, out_shape=made, compiler_params=small)(
         after, message, held, inside, tips, last
     )
-    lines = lax.all_to_all(message, GZ, 0, 0, tiled=True)
+    lines = lax.all_to_all(message, ("xh", "yh", "yl"), 0, 0, tiled=True)
     z_modes, emf = pl.pallas_call(
         z_kernel,
         out_shape=(jax.ShapeDtypeStruct((512, 128), BF), jax.ShapeDtypeStruct(field_b.shape, BF)),
@@ -474,7 +478,7 @@
         compiler_params=small,
     )(lines, half, held, inside, low, before)
     spread = lax.all_to_all(z_modes.reshape(256, 2, 128), ("yh", "yl") + GY, 0, 0, tiled=True).reshape(512, 128)
-    first = ('xh', 'xl', 'c')
+    first = ('c', 'xl', 'xh')
     second = ('yh', 'yl', 'z')
     mode_power, sums = pl.pallas_call(
         y_kernel,

time: 86.8 us -> 86.7 us (level)
  no operation moved by 1% of the time
where the time goes in v10:
time: 86.7 us; the launch traced here: 86.3 us
  blocking collectives  53.2 us (61%)
  starting transfers between devices  15.5 us (18%)
  waiting for transfers between devices  9.29 us (11%)
  Pallas kernels  6.92 us (8%)
    all_to_all x1, blocking collectives, on_device(): lax.all_to_all(z_modes.reshape(256, 2, 128), ('yh', 'yl') + GY, 0, 0, til...  29.5 us
    all_to_all x1, blocking collectives, on_device(): lax.all_to_all(copies, second, 0, 0, tiled=True).astype(F32)  15.3 us
    ppermute x2, starting transfers between devices, shift(): lax.ppermute(cells, axis, [(i, (i + step) % count) for i in range(count)])  11.1 us
    ppermute x2, waiting for transfers between devices, shift(): lax.ppermute(cells, axis, [(i, (i + step) % count) for i in range(count)])  9.29 us
    all_to_all x1, blocking collectives, on_device(): sums = jnp.sum(lax.all_to_all(sums, first, 0, 0, tiled=True), axis=0)  8.36 us
    all_to_all x1, starting transfers between devices, on_device(): lines = lax.all_to_all(message, ('xh', 'yh', 'yl'), 0, 0, tiled=True)  4.35 us
    pallas_call x1, Pallas kernels, on_device(): pl.pallas_call(message_kernel, out_shape=made + tuple(rows) + (jax.ShapeD...  1.97 us
    pallas_call x1, Pallas kernels, on_device(): pl.pallas_call(z_kernel, out_shape=(jax.ShapeDtypeStruct((512, 128), BF),...  1.81 us
  transfers between devices with their start and end apart: 3, of which 1 were waited for; matrix products, arithmetic and copies ran while one was open for 0% of the time, Pallas kernels for 2%

profile of v10, /device:TPU:1, one launch (start us, length us, event | category | flops | bytes accessed | tf_op | source)
XLA Modules:
  0.0 86.3 jit_solution(14175199579362898418)
XLA Ops:
  0.6 0.9 %shard_map.112 = (f32[16,128]{1,0:T(8,128)S(1)}, f32[4,128]{1,0:T(4,128)S(1)}) custom-call(s32[1,64]{1,0:T(1,128)} %bitcast.8, f32[3,2,64,128]{3,2,1,0:T(8,128)} %refs_2_.1, f32[2,64,128]{2,1,0:T(8,128)} %refs_3_.1), custom_call_target="tpu_custom_call" | custom-call | tf_op jit(solution)/shard_map/pallas_call | solution.py:433
  1.5 8.8 %collective-permute-start = (f32[16,128]{1,0:T(8,128)S(1)}, f32[16,128]{1,0:T(8,128)S(1)}, u32[]{:S(2)}, u32[]{:S(2)}) collective-permute-start(f32[16,128]{1,0:T(8,128)S(1)} %get-tuple-element.19), channel_id=1, source_target_pairs={{0,31},{1,0},{2,1},{3,2},{4,3},{5,4},{6,5},{7,6},{8,7},{9,8},{10,9... | collective-permute-start | bytes 24584 | tf_op jit(solution)/shard_map/ppermute | solution.py:426
  10.3 0.0 copy-start
  10.3 0.0 copy-start.1
  10.4 0.0 copy-start.2
  10.4 0.0 copy-start.3
  10.4 2.0 %shard_map.113 = (bf16[16,64,128]{2,1,0:T(8,128)(2,1)S(1)}, f32[64,128]{1,0:T(8,128)S(1)}, bf16[3,2,64,128]{3,2,1,0:T(8,128)(2,1)S(1)}, f32[6,8,128]{2,1,0:T(8,1...) custom-call(s32[1,64]{1,0:T(1,128)} %bitcast.9, s32[1,128]{1,0:T(1,128)} %bitcast.10, ...), custom_call_target="tpu_custom_call" | custom-call | flops 2000000 | bytes 2000000 | tf_op jit(solution)/shard_map/pallas_call | solution.py:462
  12.4 0.0 collective-permute-done.next_ref
  12.4 0.9 %shard_map.114 = (bf16[16,64,128]{2,1,0:T(8,128)(2,1)}, f32[64,128]{1,0:T(8,128)S(1)}, bf16[3,2,64,128]{3,2,1,0:T(8,128)(2,1)S(1)}) custom-call(f32[16,128]{1,0:T(8,128)S(1)} %collective-permute-done.next_ref, bf16[16,64,128]{2,1,0:T(8,128)(2,1)S(1)} %get-tuple-element.20.msg_ref, f32[64,128]{1,0:T(8,128)S(1)} %get-tuple-element.21.held_ref, ...), custom_call_target="tpu_custom_call" | custom-call | tf_op jit(solution)/shard_map/pallas_call | solution.py:470
  13.3 4.3 %all-to-all-start = ((bf16[16,64,128]{2,1,0:T(8,128)(2,1)}), bf16[16,64,128]{2,1,0:T(8,128)(2,1)S(1)}, u32[]{:S(2)}, u32[]{:S(2)}) async-start(bf16[16,64,128]{2,1,0:T(8,128)(2,1)} %get-tuple-element.25), calls=%async_computation | async-start | bytes 524288 | tf_op jit(solution)/shard_map/all_to_all | solution.py:473
  17.7 2.3 %collective-permute-start.1 = (f32[4,128]{1,0:T(4,128)S(1)}, f32[4,128]{1,0:T(4,128)S(1)}, u32[]{:S(2)}, u32[]{:S(2)}) collective-permute-start(f32[4,128]{1,0:T(4,128)S(1)} %get-tuple-element.30), channel_id=1, source_target_pairs={{0,1},{1,2},{2,3},{3,4},{4,5},{5,6},{6,7},{7,8},{8,9},{9,10},{10,1... | collective-permute-start | bytes 6152 | tf_op jit(solution)/shard_map/ppermute | solution.py:426
  20.0 9.3 %collective-permute-done.1.before_ref = f32[4,128]{1,0:T(4,128)S(1)} collective-permute-done((f32[4,128]{1,0:T(4,128)S(1)}, f32[4,128]{1,0:T(4,128)S(1)}, u32[]{:S(2)}, u32[]{:S(2)}) %collective-permute-start.1) | collective-permute-done | bytes 2080 | tf_op jit(solution)/shard_map/ppermute | solution.py:426
  29.3 0.0 all-to-all-done.x_ref
  29.3 1.8 %shard_map.115 = (bf16[512,128]{1,0:T(8,128)(2,1)S(1)}, bf16[3,2,64,128]{3,2,1,0:T(8,128)(2,1)}) custom-call(bf16[16,64,128]{2,1,0:T(8,128)(2,1)S(1)} %all-to-all-done.x_ref, bf16[8,512,128]{2,1,0:T(8,128)(2,1)S(1)} %get-tuple-element.26.table_ref, f32[64,128]{1,0:T(8,128)S(1)} %get-tuple-element.27.held_ref, ...), custom_call_target="tpu_custom_call" | custom-call | tf_op jit(solution)/shard_map/pallas_call | solution.py:474
  31.1 29.5 %all_to_all.20 = bf16[256,2,128]{2,1,0:T(2,128)(2,1)S(1)} all-to-all(bf16[256,2,128]{2,1,0:T(2,128)(2,1)S(1)} %bitcast.6), channel_id=1, replica_groups=mesh['yh'=4,'yl'=2,'xh'=2,'z'=8,'xl'=2,'c'=2] {'yh','yl','z','xl','c'}, dimensions={0} | all-to-all | bytes 262144 | tf_op jit(solution)/shard_map/all_to_all | solution.py:480
  60.5 0.0 copy-done
  60.6 0.0 copy-done.1
  60.6 0.0 copy-done.2
  60.6 0.0 copy-done.3
  60.6 1.3 %shard_map.116 = (f32[2,2048]{1,0:T(2,128)}, f32[8,8,128]{2,1,0:T(8,128)S(1)}) custom-call(bf16[512,128]{1,0:T(8,128)(2,1)S(1)} %bitcast.5, bf16[512,512]{1,0:T(8,128)(2,1)S(1)} %copy-done, f32[2,8,256]{2,1,0:T(8,128)S(1)} %copy-done.3, bf16[128,128]{1,0:T(8,128)(2,1)S(1)} %copy-done.1, s32[2,2048]{1,0:T(2,128)S(1)} %copy-done.2), custom_call_target="tpu_custom_call" | custom-call | tf_op jit(solution)/shard_map/pallas_call | solution.py:483
  61.9 8.4 %all_to_all.21 = f32[8,8,128]{2,1,0:T(8,128)S(1)} all-to-all(f32[8,8,128]{2,1,0:T(8,128)S(1)} %get-tuple-element.34), channel_id=1, replica_groups=mesh['yh'=4,'yl'=2,'xh'=2,'z'=8,'xl'=2,'c'=2] {'c','xl','xh'}, dimensions={0} | all-to-all | bytes 65536 | tf_op jit(solution)/shard_map/all_to_all | solution.py:491
  70.3 15.3 %all_to_all.22 = bf16[64,8,128]{2,1,0:T(8,128)(2,1)S(1)} all-to-all(bf16[64,8,128]{2,1,0:T(8,128)(2,1)S(1)} %broadcast_in_dim.14), channel_id=1, replica_groups=mesh['yh'=4,'yl'=2,'xh'=2,'z'=8,'xl'=2,'c'=2] {'yh','yl','z'}, dimensions={0} | all-to-all | bytes 262144 | tf_op jit(solution)/shard_map/all_to_all | solution.py:493
  85.6 0.7 convert_reduce_fusion
  (2 shorter events, 0.0 us)
Async XLA Ops:
  1.5 10.8 %collective-permute-start = (f32[16,128]{1,0:T(8,128)S(1)}, f32[16,128]{1,0:T(8,128)S(1)}, u32[]{:S(2)}, u32[]{:S(2)}) collective-permute-start(f32[16,128]{1,0:T(8,128)S(1)} %get-tuple-element.19), channel_id=1, source_target_pairs={{0,31},{1,0},{2,1},{3,2},{4,3},{5,4},{6,5},{7,6},{8,7},{9,8},{10,9... | collective-permute-start | bytes 24584 | tf_op jit(solution)/shard_map/ppermute | solution.py:426
  10.3 50.2 %copy-start = (bf16[512,512]{1,0:T(8,128)(2,1)S(1)}, bf16[512,512]{1,0:T(8,128)(2,1)}, u32[]{:S(2)}) copy-start(bf16[512,512]{1,0:T(8,128)(2,1)} %constant.11.clone.table_ref) | copy-start | bytes 1572868
  10.3 50.2 %copy-start.1 = (bf16[128,128]{1,0:T(8,128)(2,1)S(1)}, bf16[128,128]{1,0:T(8,128)(2,1)}, u32[]{:S(2)}) copy-start(bf16[128,128]{1,0:T(8,128)(2,1)} %constant.13.clone.order_ref) | copy-start | bytes 98308
  10.4 50.2 %copy-start.2 = (s32[2,2048]{1,0:T(2,128)S(1)}, s32[2,2048]{1,0:T(2,128)}, u32[]{:S(2)}) copy-start(s32[2,2048]{1,0:T(2,128)} %bins_ref.1) | copy-start | bytes 49156
  10.4 50.2 %copy-start.3 = (f32[2,8,256]{2,1,0:T(8,128)S(1)}, f32[2,8,256]{2,1,0:T(8,128)}, u32[]{:S(2)}) copy-start(f32[2,8,256]{2,1,0:T(8,128)} %constant.12.clone.turn_ref) | copy-start | bytes 49156
  13.3 16.0 %all-to-all-start = ((bf16[16,64,128]{2,1,0:T(8,128)(2,1)}), bf16[16,64,128]{2,1,0:T(8,128)(2,1)S(1)}, u32[]{:S(2)}, u32[]{:S(2)}) async-start(bf16[16,64,128]{2,1,0:T(8,128)(2,1)} %get-tuple-element.25), calls=%async_computation | async-start | bytes 524288 | tf_op jit(solution)/shard_map/all_to_all | solution.py:473
  17.7 11.6 %collective-permute-start.1 = (f32[4,128]{1,0:T(4,128)S(1)}, f32[4,128]{1,0:T(4,128)S(1)}, u32[]{:S(2)}, u32[]{:S(2)}) collective-permute-start(f32[4,128]{1,0:T(4,128)S(1)} %get-tuple-element.30), channel_id=1, source_target_pairs={{0,1},{1,2},{2,3},{3,4},{4,5},{5,6},{6,7},{7,8},{8,9},{9,10},{10,1... | collective-permute-start | bytes 6152 | tf_op jit(solution)/shard_map/ppermute | solution.py:426

commit v11 on v9

--- a/solution.py
+++ b/solution.py
@@ -474,7 +474,7 @@
         compiler_params=small,
     )(lines, half, held, inside, low, before)
     spread = lax.all_to_all(z_modes.reshape(256, 2, 128), ("yh", "yl") + GY, 0, 0, tiled=True).reshape(512, 128)
-    first = ('xh', 'xl', 'c')
+    first = ('c', 'xl', 'xh')
     second = ('yh', 'yl', 'z')
     mode_power, sums = pl.pallas_call(
         y_kernel,

time: 86.8 us -> 87 us (level)
  no operation moved by 1% of the time
where the time goes in v11:
time: 87 us; the launch traced here: 86.5 us
  blocking collectives  53.4 us (61%)
  starting transfers between devices  15.5 us (18%)
  waiting for transfers between devices  9.29 us (11%)
  Pallas kernels  6.92 us (8%)
    all_to_all x1, blocking collectives, on_device(): lax.all_to_all(z_modes.reshape(256, 2, 128), ('yh', 'yl') + GY, 0, 0, til...  29.9 us
    all_to_all x1, blocking collectives, on_device(): lax.all_to_all(copies, second, 0, 0, tiled=True).astype(F32)  15.4 us
    ppermute x2, starting transfers between devices, shift(): lax.ppermute(cells, axis, [(i, (i + step) % count) for i in range(count)])  11.1 us
    ppermute x2, waiting for transfers between devices, shift(): lax.ppermute(cells, axis, [(i, (i + step) % count) for i in range(count)])  9.29 us
    all_to_all x1, blocking collectives, on_device(): sums = jnp.sum(lax.all_to_all(sums, first, 0, 0, tiled=True), axis=0)  8.07 us
    all_to_all x1, starting transfers between devices, on_device(): lines = lax.all_to_all(message, GZ, 0, 0, tiled=True)  4.35 us
    pallas_call x1, Pallas kernels, on_device(): pl.pallas_call(message_kernel, out_shape=made + tuple(rows) + (jax.ShapeD...  1.97 us
    pallas_call x1, Pallas kernels, on_device(): pl.pallas_call(z_kernel, out_shape=(jax.ShapeDtypeStruct((512, 128), BF),...  1.82 us
  transfers between devices with their start and end apart: 3, of which 1 were waited for; matrix products, arithmetic and copies ran while one was open for 0% of the time, Pallas kernels for 2%

profile of v11, /device:TPU:1, one launch (start us, length us, event | category | flops | bytes accessed | tf_op | source)
XLA Modules:
  0.0 86.5 jit_solution(8028698463868677790)
XLA Ops:
  0.6 0.9 %shard_map.112 = (f32[16,128]{1,0:T(8,128)S(1)}, f32[4,128]{1,0:T(4,128)S(1)}) custom-call(s32[1,64]{1,0:T(1,128)} %bitcast.8, f32[3,2,64,128]{3,2,1,0:T(8,128)} %refs_2_.1, f32[2,64,128]{2,1,0:T(8,128)} %refs_3_.1), custom_call_target="tpu_custom_call" | custom-call | tf_op jit(solution)/shard_map/pallas_call | solution.py:429
  1.5 8.8 %collective-permute-start = (f32[16,128]{1,0:T(8,128)S(1)}, f32[16,128]{1,0:T(8,128)S(1)}, u32[]{:S(2)}, u32[]{:S(2)}) collective-permute-start(f32[16,128]{1,0:T(8,128)S(1)} %get-tuple-element.19), channel_id=1, source_target_pairs={{0,31},{1,0},{2,1},{3,2},{4,3},{5,4},{6,5},{7,6},{8,7},{9,8},{10,9... | collective-permute-start | bytes 24584 | tf_op jit(solution)/shard_map/ppermute | solution.py:422
  10.3 0.0 copy-start
  10.3 0.0 copy-start.1
  10.4 0.0 copy-start.2
  10.4 0.0 copy-start.3
  10.4 2.0 %shard_map.113 = (bf16[16,64,128]{2,1,0:T(8,128)(2,1)S(1)}, f32[64,128]{1,0:T(8,128)S(1)}, bf16[3,2,64,128]{3,2,1,0:T(8,128)(2,1)S(1)}, f32[6,8,128]{2,1,0:T(8,1...) custom-call(s32[1,64]{1,0:T(1,128)} %bitcast.9, s32[1,128]{1,0:T(1,128)} %bitcast.10, ...), custom_call_target="tpu_custom_call" | custom-call | flops 2000000 | bytes 2000000 | tf_op jit(solution)/shard_map/pallas_call | solution.py:458
  12.4 0.0 collective-permute-done.next_ref
  12.4 0.9 %shard_map.114 = (bf16[16,64,128]{2,1,0:T(8,128)(2,1)}, f32[64,128]{1,0:T(8,128)S(1)}, bf16[3,2,64,128]{3,2,1,0:T(8,128)(2,1)S(1)}) custom-call(f32[16,128]{1,0:T(8,128)S(1)} %collective-permute-done.next_ref, bf16[16,64,128]{2,1,0:T(8,128)(2,1)S(1)} %get-tuple-element.20.msg_ref, f32[64,128]{1,0:T(8,128)S(1)} %get-tuple-element.21.held_ref, ...), custom_call_target="tpu_custom_call" | custom-call | tf_op jit(solution)/shard_map/pallas_call | solution.py:466
  13.3 4.3 %all-to-all-start = ((bf16[16,64,128]{2,1,0:T(8,128)(2,1)}), bf16[16,64,128]{2,1,0:T(8,128)(2,1)S(1)}, u32[]{:S(2)}, u32[]{:S(2)}) async-start(bf16[16,64,128]{2,1,0:T(8,128)(2,1)} %get-tuple-element.25), calls=%async_computation | async-start | bytes 524288 | tf_op jit(solution)/shard_map/all_to_all | solution.py:469
  17.7 2.3 %collective-permute-start.1 = (f32[4,128]{1,0:T(4,128)S(1)}, f32[4,128]{1,0:T(4,128)S(1)}, u32[]{:S(2)}, u32[]{:S(2)}) collective-permute-start(f32[4,128]{1,0:T(4,128)S(1)} %get-tuple-element.30), channel_id=1, source_target_pairs={{0,1},{1,2},{2,3},{3,4},{4,5},{5,6},{6,7},{7,8},{8,9},{9,10},{10,1... | collective-permute-start | bytes 6152 | tf_op jit(solution)/shard_map/ppermute | solution.py:422
  20.0 9.3 %collective-permute-done.1.before_ref = f32[4,128]{1,0:T(4,128)S(1)} collective-permute-done((f32[4,128]{1,0:T(4,128)S(1)}, f32[4,128]{1,0:T(4,128)S(1)}, u32[]{:S(2)}, u32[]{:S(2)}) %collective-permute-start.1) | collective-permute-done | bytes 2080 | tf_op jit(solution)/shard_map/ppermute | solution.py:422
  29.3 0.0 all-to-all-done.x_ref
  29.3 1.8 %shard_map.115 = (bf16[512,128]{1,0:T(8,128)(2,1)S(1)}, bf16[3,2,64,128]{3,2,1,0:T(8,128)(2,1)}) custom-call(bf16[16,64,128]{2,1,0:T(8,128)(2,1)S(1)} %all-to-all-done.x_ref, bf16[8,512,128]{2,1,0:T(8,128)(2,1)S(1)} %get-tuple-element.26.table_ref, f32[64,128]{1,0:T(8,128)S(1)} %get-tuple-element.27.held_ref, ...), custom_call_target="tpu_custom_call" | custom-call | tf_op jit(solution)/shard_map/pallas_call | solution.py:470
  31.1 29.9 %all_to_all.20 = bf16[256,2,128]{2,1,0:T(2,128)(2,1)S(1)} all-to-all(bf16[256,2,128]{2,1,0:T(2,128)(2,1)S(1)} %bitcast.6), channel_id=1, replica_groups=mesh['yh'=4,'yl'=2,'xh'=2,'z'=8,'xl'=2,'c'=2] {'yh','yl','z','xl','c'}, dimensions={0} | all-to-all | bytes 262144 | tf_op jit(solution)/shard_map/all_to_all | solution.py:476
  61.0 0.0 copy-done
  61.0 0.0 copy-done.1
  61.0 0.0 copy-done.2
  61.0 0.0 copy-done.3
  61.0 1.3 %shard_map.116 = (f32[2,2048]{1,0:T(2,128)}, f32[8,8,128]{2,1,0:T(8,128)S(1)}) custom-call(bf16[512,128]{1,0:T(8,128)(2,1)S(1)} %bitcast.5, bf16[512,512]{1,0:T(8,128)(2,1)S(1)} %copy-done, f32[2,8,256]{2,1,0:T(8,128)S(1)} %copy-done.3, bf16[128,128]{1,0:T(8,128)(2,1)S(1)} %copy-done.1, s32[2,2048]{1,0:T(2,128)S(1)} %copy-done.2), custom_call_target="tpu_custom_call" | custom-call | tf_op jit(solution)/shard_map/pallas_call | solution.py:479
  62.3 8.1 %all_to_all.21 = f32[8,8,128]{2,1,0:T(8,128)S(1)} all-to-all(f32[8,8,128]{2,1,0:T(8,128)S(1)} %get-tuple-element.34), channel_id=1, replica_groups=mesh['yh'=4,'yl'=2,'xh'=2,'z'=8,'xl'=2,'c'=2] {'c','xl','xh'}, dimensions={0} | all-to-all | bytes 65536 | tf_op jit(solution)/shard_map/all_to_all | solution.py:487
  70.4 15.4 %all_to_all.22 = bf16[64,8,128]{2,1,0:T(8,128)(2,1)S(1)} all-to-all(bf16[64,8,128]{2,1,0:T(8,128)(2,1)S(1)} %broadcast_in_dim.14), channel_id=1, replica_groups=mesh['yh'=4,'yl'=2,'xh'=2,'z'=8,'xl'=2,'c'=2] {'yh','yl','z'}, dimensions={0} | all-to-all | bytes 262144 | tf_op jit(solution)/shard_map/all_to_all | solution.py:489
  85.9 0.7 convert_reduce_fusion
  (2 shorter events, 0.0 us)
Async XLA Ops:
  1.5 10.8 %collective-permute-start = (f32[16,128]{1,0:T(8,128)S(1)}, f32[16,128]{1,0:T(8,128)S(1)}, u32[]{:S(2)}, u32[]{:S(2)}) collective-permute-start(f32[16,128]{1,0:T(8,128)S(1)} %get-tuple-element.19), channel_id=1, source_target_pairs={{0,31},{1,0},{2,1},{3,2},{4,3},{5,4},{6,5},{7,6},{8,7},{9,8},{10,9... | collective-permute-start | bytes 24584 | tf_op jit(solution)/shard_map/ppermute | solution.py:422
  10.3 50.7 %copy-start = (bf16[512,512]{1,0:T(8,128)(2,1)S(1)}, bf16[512,512]{1,0:T(8,128)(2,1)}, u32[]{:S(2)}) copy-start(bf16[512,512]{1,0:T(8,128)(2,1)} %constant.11.clone.table_ref) | copy-start | bytes 1572868
  10.3 50.7 %copy-start.1 = (bf16[128,128]{1,0:T(8,128)(2,1)S(1)}, bf16[128,128]{1,0:T(8,128)(2,1)}, u32[]{:S(2)}) copy-start(bf16[128,128]{1,0:T(8,128)(2,1)} %constant.13.clone.order_ref) | copy-start | bytes 98308
  10.4 50.7 %copy-start.2 = (s32[2,2048]{1,0:T(2,128)S(1)}, s32[2,2048]{1,0:T(2,128)}, u32[]{:S(2)}) copy-start(s32[2,2048]{1,0:T(2,128)} %bins_ref.1) | copy-start | bytes 49156
  10.4 50.7 %copy-start.3 = (f32[2,8,256]{2,1,0:T(8,128)S(1)}, f32[2,8,256]{2,1,0:T(8,128)}, u32[]{:S(2)}) copy-start(f32[2,8,256]{2,1,0:T(8,128)} %constant.12.clone.turn_ref) | copy-start | bytes 49156
  13.3 16.0 %all-to-all-start = ((bf16[16,64,128]{2,1,0:T(8,128)(2,1)}), bf16[16,64,128]{2,1,0:T(8,128)(2,1)S(1)}, u32[]{:S(2)}, u32[]{:S(2)}) async-start(bf16[16,64,128]{2,1,0:T(8,128)(2,1)} %get-tuple-element.25), calls=%async_computation | async-start | bytes 524288 | tf_op jit(solution)/shard_map/all_to_all | solution.py:469
  17.7 11.6 %collective-permute-start.1 = (f32[4,128]{1,0:T(4,128)S(1)}, f32[4,128]{1,0:T(4,128)S(1)}, u32[]{:S(2)}, u32[]{:S(2)}) collective-permute-start(f32[4,128]{1,0:T(4,128)S(1)} %get-tuple-element.30), channel_id=1, source_target_pairs={{0,1},{1,2},{2,3},{3,4},{4,5},{5,6},{6,7},{7,8},{8,9},{9,10},{10,1... | collective-permute-start | bytes 6152 | tf_op jit(solution)/shard_map/ppermute | solution.py:422
